TPU v7x, 512 devices: a whole 4x8x8 slice. The times are simulated.
512 devices in a mesh: col: 8 (over y_lo, core), row: 8 (over z), tok: 8 (over y_hi, x).
Axes of the slice: x: 4, y: 8 (y_hi: 2, y_lo: 4; y = y_hi * 4 + y_lo), z: 8, core: 2. Of those that a mesh axis runs over, the one named last changes fastest.
Arguments:
- queries: bfloat16 [1024, 16384], P('tok', ('col', 'row')), may hold values from -512 to 512
- key_rows: bfloat16 [1024, 16384], P('tok', ('col', 'row')), may hold values from -12 to 12
- values: bfloat16 [1024, 16384], P('tok', ('col', 'row')), may hold values from -6 to 6
- code_first: int32 [16384, 2048], P(('row', 'tok'), 'col'), may hold values from 0 to 255
- code_second: int32 [16384, 2048], P(('row', 'tok'), 'col'), may hold values from 0 to 255
- book_first: bfloat16 [256, 8], replicated, may hold values from -0.59765625 to 0.59765625
- book_second: bfloat16 [256, 8], replicated, may hold values from -0.59765625 to 0.59765625
- scales: float32 [16384], P(('row', 'tok')), may hold values from 0.015 to 0.15
- target: bfloat16 [1024, 16384], P(None, ('row', 'tok')), may hold values from -2 to 2
Outputs:
- misfit: bfloat16 [1024, 16384], P(None, ('row', 'tok'))
- grad_scales: float32 [16384], P(('row', 'tok'))
- grad_books: float32 [2, 256, 8], replicated
All inputs are finite; a program needn't handle non-finite values.
Results may differ from a plain program's by a relative error of at most 0.0053.
Values may be sent and summed in bfloat16 or wider, within the bound.
No kernel may reach another device: no remote copies, remote signals or barrier semaphores. Data moves between devices by JAX's collectives and lax.ppermute only.
A program may use at most 64 MiB of HBM per device.

v0:
```python
import math

import jax
import jax.numpy as jnp
from jax import lax
from jax.sharding import Mesh
from jax.sharding import PartitionSpec as P

HEAD_DIM = 128
ENTRIES = 256
GROUP = 8
TOK = ("tok_0", "tok_1")
ROW_TOK = ("row", "tok_0", "tok_1")
COL = ("col_0", "col_1")
COL_ROW_TOK = ("col_0", "col_1", "row", "tok_0", "tok_1")
COL_ROW = ("col_0", "col_1", "row")


def in_one_piece(arrays, axis, dim, along):
    both = jnp.concatenate(arrays, axis=along)
    filled, at, done = (lax.all_gather(both, axis, axis=dim, tiled=True), 0, [])
    for a in arrays:
        done.append(lax.slice_in_dim(filled, at, at + a.shape[along], axis=along))
        at += a.shape[along]
    return tuple(done)


def laid_out(pieces, dim):
    dims = list(pieces.shape[1:])
    dims[dim] *= pieces.shape[0]
    return jnp.moveaxis(pieces, 0, dim).reshape(dims)


def all_blocks(array, axes, sequence):
    pieces = array
    for k in sequence:
        pieces = lax.all_gather(pieces, axes[k])
    done = sequence[::-1]
    back = [done.index(k) for k in range(len(axes))]
    pieces = pieces.transpose(*back, *range(len(axes), pieces.ndim))
    return pieces.reshape(-1, *array.shape)


def whole_of(array, axes, sequence, dim):
    return laid_out(all_blocks(array, axes, sequence), dim)


def in_blocks(array, dim, peers):
    before, after = (array.shape[:dim], array.shape[dim + 1 :])
    return jnp.moveaxis(array.reshape(*before, peers, -1, *after), dim, 0)


def summed_on_arrival(array, axis, dim):
    peers = lax.axis_size(axis)
    pieces = lax.all_to_all(in_blocks(array, dim, peers), axis, 0, 0, tiled=True)
    return jnp.sum(pieces, axis=0)


def copy_for_each(array, axis):
    peers = lax.axis_size(axis)
    return lax.all_to_all(
        jnp.broadcast_to(array[None], (peers, *array.shape)), axis, 0, 0, tiled=True
    )


def gather_directly(array, axis, dim):
    return laid_out(copy_for_each(array, axis), dim)


def over_copies(array, axis):
    return copy_for_each(array, axis).sum(axis=0)


def by_axis(array, axes):
    for axis in axes:
        array = lax.psum(array, axis)
    return array


def one_hot_codes(codes):
    return (codes[..., None] == lax.iota(jnp.int32, ENTRIES)).astype(jnp.bfloat16)


def dequantize(first_codes, second_codes, book_first, book_second):
    rows, groups = first_codes.shape
    first_part = jnp.einsum(
        "rgk,kj->rgj", one_hot_codes(first_codes), book_first, preferred_element_type=jnp.float32
    )
    second_part = jnp.einsum(
        "rgk,kj->rgj", one_hot_codes(second_codes), book_second, preferred_element_type=jnp.float32
    )
    return (first_part + second_part).reshape(rows, groups * GROUP)


def split_terms(scaled):
    upper = scaled.astype(jnp.bfloat16)
    lower = (scaled - upper.astype(jnp.float32)).astype(jnp.bfloat16)
    return jnp.concatenate([upper, lower], axis=-1)


def bin_terms(codes, split):
    parts = jnp.einsum(
        "rgk,rgj->kj", one_hot_codes(codes), split, preferred_element_type=jnp.float32
    )
    return parts[:, :GROUP] + parts[:, GROUP:]


def block_size(rows, groups):
    return math.gcd(rows, max(1, 32768 // groups))


def tile_unscaled(code_first, code_second, book_first, book_second):
    rows, groups = code_first.shape
    block = block_size(rows, groups)
    count = rows // block

    def one_block(operands):
        first_codes, second_codes = operands
        return dequantize(first_codes, second_codes, book_first, book_second)

    blocks = lax.map(
        one_block,
        (code_first.reshape(count, block, groups), code_second.reshape(count, block, groups)),
    )
    return blocks.reshape(rows, groups * GROUP)


def tile_grads(code_first, code_second, scales, unscaled_rows, grad_rows):
    rows, groups = code_first.shape
    block = block_size(rows, groups)
    count = rows // block

    def step(total, index):
        start = index * block
        first_codes = lax.dynamic_slice_in_dim(code_first, start, block, 0)
        second_codes = lax.dynamic_slice_in_dim(code_second, start, block, 0)
        row_scales = lax.dynamic_slice_in_dim(scales, start, block, 0)
        unscaled = unscaled_rows(first_codes, second_codes, start, block)
        weight_grad = grad_rows(start, block)
        scale_part = jnp.sum(weight_grad * unscaled, axis=1)
        split = split_terms((row_scales[:, None] * weight_grad).reshape(block, groups, GROUP))
        total = total + jnp.stack([bin_terms(first_codes, split), bin_terms(second_codes, split)])
        return (total, scale_part)

    total, parts = lax.scan(
        step, jnp.zeros((2, ENTRIES, GROUP), jnp.float32), lax.iota(jnp.int32, count)
    )
    return (total, parts.reshape(rows))


def local(
    queries, key_rows, values, code_first, code_second, book_first, book_second, scales, target
):
    tok_rows, width = queries.shape
    heads_here = width // HEAD_DIM
    query_heads = queries.reshape(tok_rows, heads_here, HEAD_DIM)
    query_place = lax.axis_index(TOK) * tok_rows + lax.iota(jnp.int32, tok_rows)
    running_max = jnp.full((heads_here, tok_rows), -1e30, jnp.float32)
    key_piece, value_piece = in_one_piece((key_rows, values), TOK, 0, 1)
    length = key_piece.shape[0]
    key_heads = key_piece.reshape(length, heads_here, HEAD_DIM)
    value_heads = value_piece.reshape(length, heads_here, HEAD_DIM)
    scores = jnp.einsum(
        "qhd,khd->hqk", query_heads, key_heads, preferred_element_type=jnp.float32
    ) / math.sqrt(HEAD_DIM)
    key_place = lax.iota(jnp.int32, length)
    allowed = (key_place[None, :] <= query_place[:, None])[None]
    masked = jnp.where(allowed, scores, -1e30)
    fresh_max = jnp.maximum(running_max, jnp.max(masked, axis=-1))
    exponent = jnp.where(allowed, jnp.exp(scores - fresh_max[..., None]), 0.0)
    probs = exponent.astype(jnp.bfloat16)
    running_sum = jnp.sum(exponent, axis=-1)
    weighted = jnp.einsum("hqk,khd->hqd", probs, value_heads, preferred_element_type=jnp.float32)
    running_max, running_sum, weighted = (fresh_max, running_sum, weighted)
    attended = (
        (weighted / running_sum[..., None])
        .transpose(1, 0, 2)
        .reshape(tok_rows, width)
        .astype(jnp.bfloat16)
    )
    out_rows, groups = code_first.shape
    unscaled = tile_unscaled(code_first, code_second, book_first, book_second)
    weight = (scales[:, None] * unscaled).astype(jnp.bfloat16)
    count_row = lax.axis_size("row")
    count_tok = lax.axis_size(TOK)
    collected = whole_of(attended[None], ROW_TOK, (1, 0, 2), 0)
    blocks = collected.reshape(count_row, count_tok, tok_rows, width)
    split_weight = weight.reshape(out_rows, count_row, width)
    partial_value = jnp.einsum(
        "rtkc,orc->tko", blocks, split_weight, preferred_element_type=jnp.float32
    ).reshape(count_tok * tok_rows, out_rows)
    shares_sum = summed_on_arrival(partial_value, COL, 0)
    share_rows = shares_sum.shape[0]
    own_target = lax.dynamic_slice_in_dim(target, lax.axis_index(COL) * share_rows, share_rows, 0)
    misfit_share = (shares_sum - own_target.astype(jnp.float32)).astype(jnp.bfloat16)
    misfit = gather_directly(misfit_share, COL, 0)
    token_count = misfit.shape[0]

    def grad_rows(start, size):
        misfit_cols = lax.dynamic_slice_in_dim(misfit, start, size, 1)
        return (
            jnp.einsum(
                "tko,rtkc->orc",
                misfit_cols.reshape(count_tok, tok_rows, size),
                blocks,
                preferred_element_type=jnp.float32,
            ).reshape(size, groups * GROUP)
            / token_count
        )

    def stored_rows(first_codes, second_codes, start, size):
        return lax.dynamic_slice_in_dim(unscaled, start, size, 0)

    book_part, scale_part = tile_grads(code_first, code_second, scales, stored_rows, grad_rows)
    grad_scales = over_copies(scale_part, COL)
    grad_books = by_axis(book_part, COL_ROW_TOK)
    return (misfit, grad_scales, grad_books)


def solution(mesh):
    split = Mesh(
        mesh.devices.reshape(4, 2, mesh.shape["row"], 2, 4),
        ("col_0", "col_1", "row", "tok_0", "tok_1"),
    )
    return jax.shard_map(
        local,
        mesh=split,
        in_specs=(
            P(TOK, COL_ROW),
            P(TOK, COL_ROW),
            P(TOK, COL_ROW),
            P(ROW_TOK, COL),
            P(ROW_TOK, COL),
            P(),
            P(),
            P(ROW_TOK),
            P(None, ROW_TOK),
        ),
        out_specs=(P(None, ROW_TOK), P(ROW_TOK), P()),
        check_vma=False,
    )
```

profile of v0, /device:TPU:8, one launch (start us, length us, event | category | flops | bytes accessed | tf_op | source)
XLA Modules:
  0.0 372.9 jit_solution(685231861578435844)
XLA Ops:
  10.1 72.1 %all-gather.6.cloned.1.call-done = bf16[1024,512]{0,1:T(8,128)(2,1)} async-done(((bf16[128,512]{0,1:T(8,128)(2,1)}), bf16[1024,512]{0,1:T(8,128)(2,1)}) %all-gather.6.cloned.1.call-update) | async-done | bytes 1048592 | tf_op jit(solution)/shard_map/all_gather | solution.py:21
  84.6 8.9 %all_gather.19 = bf16[2,1,128,256]{3,2,1,0:T(8,128)(2,1)} all-gather(bf16[1,1,128,256]{3,2,1,0:T(8,128)(2,1)S(1)} %copy.92), channel_id=1, replica_groups=mesh['col_0'=4,'col_1'=2,'row'=8,'tok_0'=2,'tok_1'=4] {'tok_0'}, dimensions={0}, use_global_device_ids=true | all-gather | bytes 196608 | tf_op jit(solution)/shard_map/all_gather | solution.py:37
  93.6 38.8 %all-gather.8.cloned.1.call-done = bf16[16,1,128,256]{3,2,1,0:T(8,128)(2,1)} async-done(((bf16[2,1,128,256]{3,2,1,0:T(8,128)(2,1)}), bf16[16,1,128,256]{3,2,1,0:T(8,128)(2,1)}) %all-gather.8.cloned.1.call-update) | async-done | bytes 1048592 | tf_op jit(solution)/shard_map/all_gather | solution.py:37
  132.4 48.4 %while.23 = (s32[]{:T(128)}, f32[2,128,2048]{2,1,0:T(8,128)}, s32[2,128,256]{2,1,0:T(8,128)S(1)}, bf16[256,8]{0,1:T(8,128)(2,1)S(1)}, s32[2,128,256]{2,1,0:T(8,128)S(1)}, /*index=5*/bf16[256,8]{0,1:T(8,128)(2,1)S(1)}, s32[]{:T(128)}) while((s32[]{:T(128)}, f32[2,128,2048]{2,1,0:T(8,128)}, s32[2,128,256]{2,1,0:T(8,128)S(1)}, ...), condition=%wide.region_3.4_spmd, body=%wide.region_2.3_spmd.sunk | while | flops 285474816 | bytes 10232401 | solution.py:121
  132.5 11.1 %fusion.53 = f32[128,256,8]{1,2,0:T(8,128)S(1)} fusion(s32[128,256]{1,0:T(8,128)S(1)} %get-tuple-element.320, bf16[256,8]{0,1:T(8,128)(2,1)S(1)} %get-tuple-element.353), kind=kOutput, calls=%fused_computation.2.clone.1 | convolution fusion | flops 142606336 | bytes 1183744 | tf_op jit(solution)/shard_map/while/body/eval_jaxpr/rgk,kj->rgj/dot_general | solution.py:86
  143.5 11.1 %fusion.54 = f32[128,256,8]{1,2,0:T(8,128)S(1)} fusion(f32[128,256,8]{1,2,0:T(8,128)S(1)} %fusion.53, s32[128,256]{1,0:T(8,128)S(1)} %get-tuple-element.321, bf16[256,8]{0,1:T(8,128)(2,1)S(1)} %get-tuple-element.355), kind=kOutput, calls=%fused_computation.6.clone.1 | convolution fusion | flops 142868480 | bytes 2232320 | tf_op jit(solution)/shard_map/while/body/eval_jaxpr/rgk,kj->rgj/dot_general | solution.py:89
  156.7 11.1 %fusion.53 = f32[128,256,8]{1,2,0:T(8,128)S(1)} fusion(s32[128,256]{1,0:T(8,128)S(1)} %get-tuple-element.320, bf16[256,8]{0,1:T(8,128)(2,1)S(1)} %get-tuple-element.353), kind=kOutput, calls=%fused_computation.2.clone.1 | convolution fusion | flops 142606336 | bytes 1183744 | tf_op jit(solution)/shard_map/while/body/eval_jaxpr/rgk,kj->rgj/dot_general | solution.py:86
  167.7 11.1 %fusion.54 = f32[128,256,8]{1,2,0:T(8,128)S(1)} fusion(f32[128,256,8]{1,2,0:T(8,128)S(1)} %fusion.53, s32[128,256]{1,0:T(8,128)S(1)} %get-tuple-element.321, bf16[256,8]{0,1:T(8,128)(2,1)S(1)} %get-tuple-element.355), kind=kOutput, calls=%fused_computation.6.clone.1 | convolution fusion | flops 142868480 | bytes 2232320 | tf_op jit(solution)/shard_map/while/body/eval_jaxpr/rgk,kj->rgj/dot_general | solution.py:89
  192.8 5.1 %all-to-all-start = ((f32[8,128,256]{2,1,0:T(8,128)}), f32[8,128,256]{2,1,0:T(8,128)S(1)}, u32[]{:S(2)}, u32[]{:S(2)}) async-start(f32[8,128,256]{2,1,0:T(8,128)} %convolution_bitcast_fusion.1), calls=%async_computation | async-start | bytes 2097152 | tf_op jit(solution)/shard_map/all_to_all | solution.py:55
  198.0 23.1 %all-to-all-done = f32[8,128,256]{2,1,0:T(8,128)S(1)} async-done(((f32[8,128,256]{2,1,0:T(8,128)}), f32[8,128,256]{2,1,0:T(8,128)S(1)}, u32[]{:S(2)}, u32[]{:S(2)}) %all-to-all-start) | async-done | bytes 1048608 | tf_op jit(solution)/shard_map/all_to_all | solution.py:55
  222.8 6.8 %all-to-all-start.1 = ((bf16[8,128,256]{2,1,0:T(8,128)(2,1)}), bf16[8,128,256]{2,1,0:T(8,128)(2,1)S(1)}, u32[]{:S(2)}, u32[]{:S(2)}) async-start(bf16[8,128,256]{2,1,0:T(8,128)(2,1)} %broadcast_in_dim.71), calls=%async_computation.1 | async-start | bytes 1048576 | tf_op jit(solution)/shard_map/all_to_all | solution.py:61
  229.7 6.5 %copy.99 = bf16[8,8,128,256]{2,3,0,1:T(8,128)(2,1)} copy(bf16[8,8,128,256]{3,2,0,1:T(8,128)(2,1)} %bitcast.122) | data formatting | bytes 8388608
  236.2 5.7 %all-to-all-done.1 = bf16[8,128,256]{2,1,0:T(8,128)(2,1)S(1)} async-done(((bf16[8,128,256]{2,1,0:T(8,128)(2,1)}), bf16[8,128,256]{2,1,0:T(8,128)(2,1)S(1)}, u32[]{:S(2)}, u32[]{:S(2)}) %all-to-all-start.1) | async-done | bytes 524320 | tf_op jit(solution)/shard_map/all_to_all | solution.py:61
  241.8 34.5 %while.24 = (s32[]{:T(128)}, f32[2,256,8]{1,2,0:T(8,128)S(1)}, f32[2,128]{1,0:T(2,128)S(1)}, s32[2]{0:T(128)S(1)}, s32[256,256]{1,0:T(8,128)S(1)}, /*index=5*/bf...) while((s32[]{:T(128)}, f32[2,256,8]{1,2,0:T(8,128)S(1)}, ...), condition=%wide.region_7.8_spmd.clone, body=%wide.region_5.7_spmd.clone.sunk | while | flops 1097089024 | bytes 15863005 | solution.py:145
  243.2 4.1 %multiply_reduce_fusion.2 = (f32[128]{0:T(128)S(1)}, f32[128,2048]{1,0:T(8,128)S(1)}) fusion(f32[256,2048]{1,0:T(8,128)} %get-tuple-element.394, s32[]{:T(128)S(6)} %select_n.29, f32[128]{0:T(128)S(1)} %dynamic-slice_multiply_fusion.2, bf16[8,128,128]{2,1,0:T(8,128)(2,1)S(1)} %bitcast.118, bf16[2048,128,8]{1,0,2:T(8,128)(2,1)} %bitcast.116), kind=kOutput, calls=%fused_computation.25.clone.1 | convolution fusion | flops 537919360 | bytes 6554628 | tf_op jit(solution)/shard_map/while/body/eval_jaxpr/tko,rtkc->orc/dot_general | solution.py:202
  247.9 5.5 %fusion.60 = f32[256,16]{0,1:T(8,128)S(1)} fusion(s32[128,256]{0,1:T(8,128)S(1)} %copy.135, bf16[128,256,8]{0,2,1:T(8,128)(2,1)S(1)} %fusion.57, bf16[128,256,8]{0,2,1:T(8,128)(2,1)S(1)} %bitcast_convert_fusion.2), kind=kOutput, calls=%fused_computation.20.clone.1 | convolution fusion | flops 278921216 | bytes 1196032 | tf_op jit(solution)/shard_map/while/body/eval_jaxpr/rgk,rgj->kj/dot_general | solution.py:102
  253.5 5.5 %fusion.58 = f32[256,16]{0,1:T(8,128)S(1)} fusion(s32[128,256]{0,1:T(8,128)S(1)} %copy.133, bf16[128,256,8]{0,2,1:T(8,128)(2,1)S(1)} %fusion.57, bf16[128,256,8]{0,2,1:T(8,128)(2,1)S(1)} %bitcast_convert_fusion.2), kind=kOutput, calls=%fused_computation.19.clone.1 | convolution fusion | flops 278921216 | bytes 1196032 | tf_op jit(solution)/shard_map/while/body/eval_jaxpr/rgk,rgj->kj/dot_general | solution.py:102
  265.2 5.5 %fusion.60 = f32[256,16]{0,1:T(8,128)S(1)} fusion(s32[128,256]{0,1:T(8,128)S(1)} %copy.135, bf16[128,256,8]{0,2,1:T(8,128)(2,1)S(1)} %fusion.57, bf16[128,256,8]{0,2,1:T(8,128)(2,1)S(1)} %bitcast_convert_fusion.2), kind=kOutput, calls=%fused_computation.20.clone.1 | convolution fusion | flops 278921216 | bytes 1196032 | tf_op jit(solution)/shard_map/while/body/eval_jaxpr/rgk,rgj->kj/dot_general | solution.py:102
  270.8 5.5 %fusion.58 = f32[256,16]{0,1:T(8,128)S(1)} fusion(s32[128,256]{0,1:T(8,128)S(1)} %copy.133, bf16[128,256,8]{0,2,1:T(8,128)(2,1)S(1)} %fusion.57, bf16[128,256,8]{0,2,1:T(8,128)(2,1)S(1)} %bitcast_convert_fusion.2), kind=kOutput, calls=%fused_computation.19.clone.1 | convolution fusion | flops 278921216 | bytes 1196032 | tf_op jit(solution)/shard_map/while/body/eval_jaxpr/rgk,rgj->kj/dot_general | solution.py:102
  276.4 16.8 %psum.35 = f32[2,256,8]{1,2,0:T(8,128)S(1)} all-reduce(f32[2,256,8]{1,2,0:T(8,128)S(1)} %get-tuple-element.90), channel_id=1, replica_groups=mesh['col_0'=4,'col_1'=2,'row'=8,'tok_0'=2,'tok_1'=4] {'col_0'}, use_global_device_ids=true, to_apply=%region_9.10 | all-reduce | flops 4096 | bytes 32768 | tf_op jit(solution)/shard_map/psum | solution.py:76
  296.5 30.8 %psum.37 = f32[2,256,8]{1,2,0:T(8,128)S(1)} all-reduce(f32[2,256,8]{1,2,0:T(8,128)S(1)} %psum.36), channel_id=1, replica_groups=mesh['col_0'=4,'col_1'=2,'row'=8,'tok_0'=2,'tok_1'=4] {'row'}, use_global_device_ids=true, to_apply=%region_11.12 | all-reduce | flops 4096 | bytes 32768 | tf_op jit(solution)/shard_map/psum | solution.py:76
  327.3 14.9 %psum.38 = f32[2,256,8]{1,2,0:T(8,128)S(1)} all-reduce(f32[2,256,8]{1,2,0:T(8,128)S(1)} %psum.37), channel_id=1, replica_groups=mesh['col_0'=4,'col_1'=2,'row'=8,'tok_0'=2,'tok_1'=4] {'tok_0'}, use_global_device_ids=true, to_apply=%region_12.13 | all-reduce | flops 4096 | bytes 32768 | tf_op jit(solution)/shard_map/psum | solution.py:76
  342.8 6.3 %all-to-all-start.2 = ((f32[8,1,256]{2,1,0:T(1,128)}), f32[8,1,256]{2,1,0:T(1,128)S(1)}, u32[]{:S(2)}, u32[]{:S(2)}) async-start(f32[8,1,256]{2,1,0:T(1,128)} %broadcast_in_dim.75), calls=%async_computation.2 | async-start | bytes 16384 | tf_op jit(solution)/shard_map/all_to_all | solution.py:61
  349.2 15.9 %psum.39 = f32[2,256,8]{1,2,0:T(8,128)} all-reduce(f32[2,256,8]{1,2,0:T(8,128)S(1)} %psum.38), channel_id=1, replica_groups=mesh['col_0'=4,'col_1'=2,'row'=8,'tok_0'=2,'tok_1'=4] {'tok_1'}, use_global_device_ids=true, to_apply=%region_13.14 | all-reduce | flops 4096 | bytes 32768 | tf_op jit(solution)/shard_map/psum | solution.py:76
  (83 shorter events, 35.3 us)
Async XLA Ops:
  7.2 76.3 %copy-start = (bf16[128,256]{1,0:T(8,128)(2,1)S(1)}, bf16[128,256]{1,0:T(8,128)(2,1)}, u32[]{:S(2)}) copy-start(bf16[128,256]{1,0:T(8,128)(2,1)} %param.13) | copy-start | bytes 196612
  7.2 75.0 %all-gather.6.cloned.1.call-start = ((), (), s32[]{:S(2)}) async-start(), calls=%async_computation.3 | async-start | bytes 1179648 | tf_op jit(solution)/shard_map/all_gather | solution.py:21
  9.8 122.5 %all-gather.8.cloned.1.call-start = ((), (), s32[]{:S(2)}) async-start(), calls=%async_computation.4 | async-start | bytes 1179648 | tf_op jit(solution)/shard_map/all_gather | solution.py:37
  10.0 122.4 %copy-start.2 = (s32[256,256]{1,0:T(8,128)S(1)}, s32[256,256]{1,0:T(8,128)}, u32[]{:S(2)}) copy-start(s32[256,256]{1,0:T(8,128)} %param.16) | copy-start | bytes 786436
  10.0 122.4 %copy-start.3 = (s32[256,256]{1,0:T(8,128)S(1)}, s32[256,256]{1,0:T(8,128)}, u32[]{:S(2)}) copy-start(s32[256,256]{1,0:T(8,128)} %param.17) | copy-start | bytes 786436
  10.0 122.4 %copy-start.5 = (bf16[256,8]{0,1:T(8,128)(2,1)S(1)}, bf16[256,8]{0,1:T(8,128)(2,1)}, u32[]{:S(2)}) copy-start(bf16[256,8]{0,1:T(8,128)(2,1)} %param.18) | copy-start | bytes 12292
  10.0 122.4 %copy-start.6 = (bf16[256,8]{0,1:T(8,128)(2,1)S(1)}, bf16[256,8]{0,1:T(8,128)(2,1)}, u32[]{:S(2)}) copy-start(bf16[256,8]{0,1:T(8,128)(2,1)} %param.19) | copy-start | bytes 12292
  93.6 92.6 %all-gather.10.cloned.1.call-start = ((), (), s32[]{:S(2)}) async-start(), calls=%async_computation.5 | async-start | bytes 5242880 | tf_op jit(solution)/shard_map/all_gather | solution.py:37
  180.8 2.5 copy-start.4
  188.6 1.9 copy-start.1
  192.8 28.3 %all-to-all-start = ((f32[8,128,256]{2,1,0:T(8,128)}), f32[8,128,256]{2,1,0:T(8,128)S(1)}, u32[]{:S(2)}, u32[]{:S(2)}) async-start(f32[8,128,256]{2,1,0:T(8,128)} %convolution_bitcast_fusion.1), calls=%async_computation | async-start | bytes 2097152 | tf_op jit(solution)/shard_map/all_to_all | solution.py:55
  222.8 19.0 %all-to-all-start.1 = ((bf16[8,128,256]{2,1,0:T(8,128)(2,1)}), bf16[8,128,256]{2,1,0:T(8,128)(2,1)S(1)}, u32[]{:S(2)}, u32[]{:S(2)}) async-start(bf16[8,128,256]{2,1,0:T(8,128)(2,1)} %broadcast_in_dim.71), calls=%async_computation.1 | async-start | bytes 1048576 | tf_op jit(solution)/shard_map/all_to_all | solution.py:61
  342.8 22.2 %all-to-all-start.2 = ((f32[8,1,256]{2,1,0:T(1,128)}), f32[8,1,256]{2,1,0:T(1,128)S(1)}, u32[]{:S(2)}, u32[]{:S(2)}) async-start(f32[8,1,256]{2,1,0:T(1,128)} %broadcast_in_dim.75), calls=%async_computation.2 | async-start | bytes 16384 | tf_op jit(solution)/shard_map/all_to_all | solution.py:61
Sparse Core Ops, SparseCore 0:
  11.6 70.5 all-gather.5
  93.7 38.6 all-gather.7
  134.5 51.6 all-gather.9
where the time goes:
time: 374 us; the launch traced here: 373 us
  waiting for transfers between devices  142 us (38%)
  blocking collectives  90.7 us (24%)
  matrix products  77.5 us (21%)
  local copies, waits for them, and re-layouts  25.3 us (7%)
  starting transfers between devices  18.5 us (5%)
  between operations  13.9 us (4%)
    psum x5, blocking collectives, by_axis(): array = lax.psum(array, axis)  81.7 us
    all_gather x1, waiting for transfers between devices, in_one_piece(): filled, at, done = (lax.all_gather(both, axis, axis=dim, tiled=True), 0, [])  72.1 us
    all_gather x2, waiting for transfers between devices, all_blocks(): pieces = lax.all_gather(pieces, axes[k])  41.3 us
    all_to_all x1, waiting for transfers between devices, summed_on_arrival(): lax.all_to_all(in_blocks(array, dim, peers), axis, 0, 0, tiled=True)  23.1 us
    dot_general x2, matrix products, dequantize(): jnp.einsum('rgk,kj->rgj', one_hot_codes(second_codes), book_second, prefe...  22.1 us
    dot_general x2, matrix products, dequantize(): jnp.einsum('rgk,kj->rgj', one_hot_codes(first_codes), book_first, preferr...  22.1 us
    dot_general x4, matrix products, bin_terms(): jnp.einsum('rgk,rgj->kj', one_hot_codes(codes), split, preferred_element_...  22 us
    unnamed x19, local copies, waits for them, and re-layouts  13.6 us
  transfers between devices with their start and end apart: 6, of which 5 were waited for; matrix products, arithmetic and copies ran while one was open for 15% of the time, Pallas kernels for 0%

commit v1 on v0

v1 whole, which is shorter than its diff:
```python
import math

import jax
import jax.numpy as jnp
from jax import lax
from jax.experimental import pallas as pl
from jax.experimental.pallas import tpu as pltpu
from jax.sharding import Mesh
from jax.sharding import PartitionSpec as P

HEAD_DIM = 128
ENTRIES = 256
GROUP = 8
LOW = 8
HIGH = ENTRIES // LOW
TOK = ("tok_0", "tok_1")
ROW_TOK = ("row", "tok_0", "tok_1")
COL = ("col_0", "col_1")
COL_ROW = ("col_0", "col_1", "row")
f32, bf16 = jnp.float32, jnp.bfloat16


def exchange(pieces, axis):
    return lax.all_to_all(pieces, axis, 0, 0, tiled=True)


def copies(array, axis):
    return exchange(jnp.broadcast_to(array[None], (lax.axis_size(axis), *array.shape)), axis)


def swap(array, axis):
    return lax.ppermute(array, axis, [(0, 1), (1, 0)])


def in_order(mine, theirs, place):
    first = place == 0
    return jnp.where(first, mine, theirs), jnp.where(first, theirs, mine)


def dequant_kernel(codes_ref, table_ref, scale_ref, out_ref):
    groups, rows = codes_ref.shape
    tables = [table_ref[i] for i in range(4)]
    scale = jnp.broadcast_to(scale_ref[...], (GROUP, rows))

    def group_rows(g):
        both = jnp.broadcast_to(codes_ref[pl.ds(g, 1), :], (GROUP, rows))
        parts = []
        for at in range(0, rows, 128):
            packed = both[:, at : at + 128]
            total = None
            for book in range(2):
                code = (packed & 255) if book == 0 else (packed >> 8)
                place = code & 127
                near = jnp.take_along_axis(tables[2 * book], place, axis=1)
                far = jnp.take_along_axis(tables[2 * book + 1], place, axis=1)
                entry = jnp.where(code >= 128, far, near)
                total = entry if total is None else total + entry
            parts.append(total * scale[:, at : at + 128])
        return jnp.concatenate(parts, axis=1)

    def step(i, carry):
        for k in range(4):
            pair = [group_rows(i * 8 + 2 * k + n) for n in range(2)]
            start = pl.multiple_of(i * 64 + 16 * k, 16)
            out_ref[pl.ds(start, 16), :] = jnp.concatenate(pair, axis=0).astype(bf16)
        return carry

    lax.fori_loop(0, groups // 8, step, 0)


def dequantize(codes, table, scales):
    blocks, groups, rows = codes.shape
    return pl.pallas_call(
        dequant_kernel,
        grid=(blocks,),
        in_specs=[
            pl.BlockSpec((None, groups, rows), lambda i: (i, 0, 0)),
            pl.BlockSpec((4, GROUP, 128), lambda i: (0, 0, 0)),
            pl.BlockSpec((None, 1, rows), lambda i: (i, 0, 0)),
        ],
        out_specs=pl.BlockSpec((None, groups * GROUP, rows), lambda i: (i, 0, 0)),
        out_shape=jax.ShapeDtypeStruct((blocks, groups * GROUP, rows), bf16),
        name="dequant",
    )(codes, table, scales)


def project_kernel(core_ref, att_ref, weight_ref, keep_ref, send_ref):
    steps, tokens, width = att_ref.shape
    half = tokens // 2
    for out_ref, who in ((send_ref, 1 - core_ref[0]), (keep_ref, core_ref[0])):
        start = pl.multiple_of(who * half, half)
        total = None
        for z in range(steps):
            part = jnp.dot(
                att_ref[z, pl.ds(start, half), :],
                weight_ref[z * width : (z + 1) * width, :],
                preferred_element_type=f32,
            )
            total = part if total is None else total + part
        out_ref[...] = total


def project(core, attended, weight):
    steps, tokens, width = attended.shape
    blocks, depth, rows = weight.shape
    out = jax.ShapeDtypeStruct((tokens // 2, blocks * rows), f32)
    out_spec = pl.BlockSpec((tokens // 2, rows), lambda i, core: (0, i))
    return pl.pallas_call(
        project_kernel,
        grid_spec=pltpu.PrefetchScalarGridSpec(
            num_scalar_prefetch=1,
            grid=(blocks,),
            in_specs=[
                pl.BlockSpec((steps, tokens, width), lambda i, core: (0, 0, 0)),
                pl.BlockSpec((None, depth, rows), lambda i, core: (i, 0, 0)),
            ],
            out_specs=[out_spec, out_spec],
        ),
        out_shape=[out, out],
        name="project",
    )(core, attended, weight)


def grads_kernel(scaling, att_ref, misfit_ref, weight_ref, codes_ref, scale_ref, gs_ref, bins_ref):
    block, step = pl.program_id(0), pl.program_id(1)
    width, rows = weight_ref.shape
    groups = width // GROUP
    weight_grad = (
        lax.dot_general(
            att_ref[...], misfit_ref[...], (((0,), (0,)), ((), ())), preferred_element_type=f32
        )
        * scaling
    )

    @pl.when(step == 0)
    def _():
        gs_ref[...] = jnp.zeros_like(gs_ref)

    @pl.when((block == 0) & (step == 0))
    def _():
        bins_ref[...] = jnp.zeros_like(bins_ref)

    weighted = weight_grad * weight_ref[...].astype(f32)
    gs_ref[...] += jnp.sum(weighted.reshape(groups, GROUP, rows), axis=0)
    scaled = weight_grad * scale_ref[...]
    at = lax.broadcasted_iota(jnp.int32, (16, rows), 0)
    low_rows = [(2 * d + (at >= 8).astype(jnp.int32)).astype(f32).astype(bf16) for d in range(LOW // 2)]
    high_rows = [(16 * d + at).astype(f32).astype(bf16) for d in range(HIGH // 16)]
    zero, one = jnp.zeros((16, rows), bf16), jnp.ones((16, rows), bf16)
    for book in range(2):
        total = None
        for start in range(0, groups, 8):
            highs, lows = [], []
            for g in range(start, start + 8):
                entry = scaled[GROUP * g : GROUP * (g + 1), :]
                twice = jnp.concatenate([entry, entry], axis=0).astype(bf16)
                packed = codes_ref[g : g + 1, :]
                code = (packed & 255) if book == 0 else (packed >> 8)
                low = jnp.broadcast_to((code & (LOW - 1)).astype(f32), (16, rows)).astype(bf16)
                high = jnp.broadcast_to((code >> 3).astype(f32), (16, rows)).astype(bf16)
                lows.append(jnp.concatenate([jnp.where(low == r, twice, zero) for r in low_rows], axis=0))
                highs.append(jnp.concatenate([jnp.where(high == r, one, zero) for r in high_rows], axis=0))
            part = lax.dot_general(
                jnp.concatenate(highs, axis=1),
                jnp.concatenate(lows, axis=1),
                (((1,), (1,)), ((), ())),
                preferred_element_type=f32,
            )
            total = part if total is None else total + part
        bins_ref[book] += total


def gradients(attended, misfit, weight, codes, scales, scaling):
    steps, tokens, width = attended.shape
    blocks, depth, rows = weight.shape
    return pl.pallas_call(
        lambda *refs: grads_kernel(scaling, *refs),
        grid=(blocks, steps),
        in_specs=[
            pl.BlockSpec((None, tokens, width), lambda i, z: (z, 0, 0)),
            pl.BlockSpec((tokens, rows), lambda i, z: (0, i)),
            pl.BlockSpec((None, width, rows), lambda i, z: (i, z, 0)),
            pl.BlockSpec((None, width // GROUP, rows), lambda i, z: (i, z, 0)),
            pl.BlockSpec((None, 1, rows), lambda i, z: (i, 0, 0)),
        ],
        out_specs=[
            pl.BlockSpec((None, GROUP, rows), lambda i, z: (i, 0, 0)),
            pl.BlockSpec((2, HIGH, LOW * GROUP), lambda i, z: (0, 0, 0)),
        ],
        out_shape=[
            jax.ShapeDtypeStruct((blocks, GROUP, rows), f32),
            jax.ShapeDtypeStruct((2, HIGH, LOW * GROUP), f32),
        ],
        name="grads",
    )(attended, misfit, weight, codes, scales)


def attend(queries, keys, values, places):
    scores = jnp.einsum("qd,kd->qk", queries, keys, preferred_element_type=f32) / math.sqrt(HEAD_DIM)
    allowed = lax.iota(jnp.int32, keys.shape[0])[None, :] <= places[:, None]
    row_max = jnp.max(jnp.where(allowed, scores, -1e30), axis=-1, keepdims=True)
    exponent = jnp.where(allowed, jnp.exp(scores - row_max), 0.0)
    row_sum = jnp.sum(exponent, axis=-1, keepdims=True)
    weighted = jnp.einsum("qk,kd->qd", exponent.astype(bf16), values, preferred_element_type=f32)
    return (weighted / row_sum).astype(bf16)


def local(
    queries, key_rows, values, code_first, code_second, book_first, book_second, scales, target
):
    tok_rows, width = queries.shape
    high, across = lax.axis_index("tok_0"), lax.axis_index("tok_1")
    count_across = lax.axis_size("tok_1")
    lane, core = lax.axis_index("col_0"), lax.axis_index("col_1")
    count_lane = lax.axis_size("col_0")
    rows = code_first.shape[0]
    tokens = lax.axis_size(TOK) * tok_rows

    def of_head(array, head):
        return lax.dynamic_slice_in_dim(array, head * HEAD_DIM, HEAD_DIM, 1)

    their_queries = swap(of_head(queries, 1 - high), "tok_0")
    pairs = jnp.stack(
        [jnp.concatenate([of_head(key_rows, h), of_head(values, h)], axis=1) for h in range(2)]
    )
    pairs = jnp.broadcast_to(pairs[:, None], (2, count_across, tok_rows, 2 * HEAD_DIM))
    pairs = exchange(pairs.reshape(-1, tok_rows, 2 * HEAD_DIM), TOK).reshape(tokens, 2 * HEAD_DIM)
    own_queries = jnp.concatenate(in_order(of_head(queries, high), their_queries, high), axis=0)
    place = across * tok_rows + lax.iota(jnp.int32, tok_rows)
    places = jnp.concatenate([place, place + count_across * tok_rows])
    head_out = attend(own_queries, pairs[:, :HEAD_DIM], pairs[:, HEAD_DIM:], places)
    head_out = jnp.concatenate(in_order(head_out, swap(head_out, "tok_0"), high), axis=1)
    attended = copies(head_out, "row")

    codes = copies((code_first + ENTRIES * code_second).T, "tok_1")
    half_tokens = tok_rows
    share = half_tokens // count_lane
    own_target = target.reshape(2, count_across, count_lane, share, rows)
    own_target = lax.dynamic_index_in_dim(own_target, core, 0, keepdims=False)
    own_target = lax.dynamic_index_in_dim(own_target, lane, 1, keepdims=False)
    row_scales = jnp.broadcast_to(scales[None, None], (count_across, 8, rows))
    side = exchange(jnp.concatenate([own_target.astype(f32), row_scales], axis=1), "tok_1")
    own_target, row_scales = side[:, :share], side[:, share : share + 1]
    books = jnp.stack([book_first, book_second]).astype(f32).transpose(0, 2, 1)
    table = books.reshape(2, GROUP, 2, 128).transpose(0, 2, 1, 3).reshape(4, GROUP, 128)
    weight = dequantize(codes, table, row_scales)

    keep, send = project(core.astype(jnp.int32)[None], attended, weight)
    half_sum = (keep + swap(send, "col_1")).astype(bf16)
    parts = exchange(half_sum.reshape(count_lane, share, -1), "col_0")
    output = jnp.sum(parts.astype(f32), axis=0)
    wanted = own_target.transpose(1, 0, 2).reshape(share, -1)
    misfit_share = (output - wanted).astype(bf16)
    misfit_half = copies(misfit_share, "col_0").reshape(half_tokens, -1)
    misfit = jnp.concatenate(in_order(misfit_half, swap(misfit_half, "col_1"), core), axis=0)

    by_rows = misfit.reshape(2 * tok_rows, count_across, rows).transpose(1, 0, 2)
    by_tokens = exchange(by_rows, "tok_1").reshape(count_across, 2, tok_rows, rows)
    misfit_out = by_tokens.transpose(1, 0, 2, 3).reshape(tokens, rows)

    scale_part, bins = gradients(attended, misfit, weight, codes, row_scales, 1.0 / tokens)
    scale_part = jnp.sum(scale_part, axis=1) / row_scales[:, 0]
    scale_part = scale_part.reshape(count_across, -1, 128)
    extra = scale_part.shape[1]
    bins = jnp.broadcast_to(bins.reshape(1, -1, 128), (count_across, 2 * ENTRIES * GROUP // 128, 128))
    sums = jnp.sum(exchange(jnp.concatenate([scale_part, bins], axis=1), "tok_1"), axis=0)
    sums = jnp.sum(copies(sums, COL), axis=0)
    grad_scales = sums[:extra].reshape(rows)
    bins = jnp.sum(copies(sums[extra:], ("row", "tok_0")), axis=0)
    return misfit_out, grad_scales, bins.reshape(2, ENTRIES, GROUP)


def solution(mesh):
    split = Mesh(
        mesh.devices.reshape(4, 2, mesh.shape["row"], 2, 4),
        ("col_0", "col_1", "row", "tok_0", "tok_1"),
    )
    return jax.shard_map(
        local,
        mesh=split,
        in_specs=(
            P(TOK, COL_ROW),
            P(TOK, COL_ROW),
            P(TOK, COL_ROW),
            P(ROW_TOK, COL),
            P(ROW_TOK, COL),
            P(),
            P(),
            P(ROW_TOK),
            P(None, ROW_TOK),
        ),
        out_specs=(P(None, ROW_TOK), P(ROW_TOK), P()),
        check_vma=False,
    )
```

time: 374 us -> 238 us (0.64)
  matrix products: 77.5 us -> 0.86 us
  waiting for transfers between devices: 142 us -> 66.6 us
  blocking collectives: 90.7 us -> 18.9 us
  Pallas kernels: 0 us -> 69.9 us
  starting transfers between devices: 18.5 us -> 57.7 us
  between operations: 13.9 us -> 0.96 us
  local copies, waits for them, and re-layouts: 25.3 us -> 13.3 us
  other arithmetic: 3.29 us -> 7.31 us
    all_gather x3 -> x0, waiting for transfers between devices: 113 us -> none  [the longest x1 72.1 us: in_one_piece(): filled, at, done = (lax.all_gather(both, axis, axis=dim, tiled=True), 0, [])]
    psum x5 -> x0, blocking collectives: 81.7 us -> none  [by_axis(): array = lax.psum(array, axis)]
    dot_general x13 -> x2, matrix products: 77.5 us -> 0.86 us  [the longest x1 0.46 us: attend(): jnp.einsum('qk,kd->qd', exponent.astype(bf16), values, preferred_element_...]
    pallas_call x0 -> x3, Pallas kernels: none -> 69.9 us  [the longest x1 33.6 us: gradients(): pl.pallas_call(lambda *refs: grads_kernel(scaling, *refs), grid=(blocks,...]
    all_to_all x3 -> x8, waiting for transfers between devices: 28.8 us -> 55.4 us  [exchange(): return lax.all_to_all(pieces, axis, 0, 0, tiled=True)]
    all_to_all x3 -> x8, starting transfers between devices: 18.3 us -> 44.6 us  [exchange(): return lax.all_to_all(pieces, axis, 0, 0, tiled=True)]
    all_to_all x0 -> x2, blocking collectives: none -> 18.9 us  [exchange(): return lax.all_to_all(pieces, axis, 0, 0, tiled=True)]
    ppermute x0 -> x4, starting transfers between devices: none -> 13.2 us  [swap(): return lax.ppermute(array, axis, [(0, 1), (1, 0)])]
  transfers between devices with their start and end apart: 6 -> 12, of which waited for: 5 -> 9; matrix products, arithmetic and copies ran while one was open for 15% -> 5% of each run, Pallas kernels for 0% -> 13%
where the time goes in v1:
time: 238 us; the launch traced here: 236 us
  Pallas kernels  69.9 us (29%)
  waiting for transfers between devices  66.6 us (28%)
  starting transfers between devices  57.7 us (24%)
  blocking collectives  18.9 us (8%)
  local copies, waits for them, and re-layouts  13.3 us (6%)
  other arithmetic  7.31 us (3%)
    all_to_all x8, waiting for transfers between devices, exchange(): return lax.all_to_all(pieces, axis, 0, 0, tiled=True)  55.4 us
    all_to_all x8, starting transfers between devices, exchange(): return lax.all_to_all(pieces, axis, 0, 0, tiled=True)  44.6 us
    pallas_call x1, Pallas kernels, gradients(): pl.pallas_call(lambda *refs: grads_kernel(scaling, *refs), grid=(blocks,...  33.6 us
    pallas_call x1, Pallas kernels, dequantize(): pl.pallas_call(dequant_kernel, grid=(blocks,), in_specs=[pl.BlockSpec((No...  31.1 us
    all_to_all x2, blocking collectives, exchange(): return lax.all_to_all(pieces, axis, 0, 0, tiled=True)  18.9 us
    ppermute x4, starting transfers between devices, swap(): return lax.ppermute(array, axis, [(0, 1), (1, 0)])  13.2 us
    ppermute x4, waiting for transfers between devices, swap(): return lax.ppermute(array, axis, [(0, 1), (1, 0)])  11.1 us
    pallas_call x1, Pallas kernels, project(): pl.pallas_call(project_kernel, grid_spec=pltpu.PrefetchScalarGridSpec(num...  5.18 us
  transfers between devices with their start and end apart: 12, of which 9 were waited for; matrix products, arithmetic and copies ran while one was open for 5% of the time, Pallas kernels for 13%

profile of v1, /device:TPU:8, one launch (start us, length us, event | category | flops | bytes accessed | tf_op | source)
XLA Modules:
  0.0 235.6 jit_solution(14676678718676396284)
XLA Ops:
  1.5 6.8 %collective-permute-start = (bf16[128,128]{1,0:T(8,128)(2,1)S(1)}, bf16[128,128]{1,0:T(8,128)(2,1)S(1)}, u32[]{:S(2)}, u32[]{:S(2)}) collective-permute-start(bf16[128,128]{1,0:T(8,128)(2,1)S(1)} %constant_dynamic-slice_fusion), channel_id=1, source_target_pairs={{0,4},{4,0},{1,5},{5,1},{2,6},{6,2},{3,7},{7,3},{8,12},{12,8},{9,1... | collective-permute-start | bytes 98312 | tf_op jit(solution)/shard_map/ppermute | solution.py:32
  10.7 4.7 %all-to-all-start = ((bf16[8,128,256]{2,1,0:T(8,128)(2,1)}), bf16[8,128,256]{2,1,0:T(8,128)(2,1)S(1)}, u32[]{:S(2)}, u32[]{:S(2)}) async-start(bf16[8,128,256]{2,1,0:T(8,128)(2,1)} %bitcast.3), calls=%async_computation | async-start | bytes 1048576 | tf_op jit(solution)/shard_map/all_to_all | solution.py:24
  19.0 15.1 %all-to-all-done = bf16[8,128,256]{2,1,0:T(8,128)(2,1)S(1)} async-done(((bf16[8,128,256]{2,1,0:T(8,128)(2,1)}), bf16[8,128,256]{2,1,0:T(8,128)(2,1)S(1)}, u32[]{:S(2)}, u32[]{:S(2)}) %all-to-all-start) | async-done | bytes 524320 | tf_op jit(solution)/shard_map/all_to_all | solution.py:24
  34.1 3.3 %all-to-all-start.3 = ((f32[4,40,256]{2,1,0:T(8,128)}), f32[4,40,256]{2,1,0:T(8,128)S(1)}, u32[]{:S(2)}, u32[]{:S(2)}) async-start(f32[4,40,256]{2,1,0:T(8,128)} %pad_maximum_fusion.1), calls=%async_computation.3 | async-start | bytes 327680 | tf_op jit(solution)/shard_map/all_to_all | solution.py:24
  37.9 5.7 %all-to-all-done.3 = f32[4,40,256]{2,1,0:T(8,128)S(1)} async-done(((f32[4,40,256]{2,1,0:T(8,128)}), f32[4,40,256]{2,1,0:T(8,128)S(1)}, u32[]{:S(2)}, u32[]{:S(2)}) %all-to-all-start.3) | async-done | bytes 163872 | tf_op jit(solution)/shard_map/all_to_all | solution.py:24
  44.6 3.6 %all-to-all-start.2 = ((s32[4,256,256]{2,1,0:T(8,128)}), s32[4,256,256]{2,1,0:T(8,128)S(1)}, u32[]{:S(2)}, u32[]{:S(2)}) async-start(s32[4,256,256]{2,1,0:T(8,128)} %broadcast_in_dim.32), calls=%async_computation.2 | async-start | bytes 2097152 | tf_op jit(solution)/shard_map/all_to_all | solution.py:24
  49.2 2.5 %collective-permute-start.1 = (bf16[256,128]{0,1:T(8,128)(2,1)S(1)}, bf16[256,128]{0,1:T(8,128)(2,1)S(1)}, u32[]{:S(2)}, u32[]{:S(2)}) collective-permute-start(bf16[256,128]{0,1:T(8,128)(2,1)S(1)} %fusion), channel_id=1, source_target_pairs={{0,4},{4,0},{1,5},{5,1},{2,6},{6,2},{3,7},{7,3},{8,12},{12,8},{9,1... | collective-permute-start | bytes 196616 | tf_op jit(solution)/shard_map/ppermute | solution.py:32
  51.7 7.5 %collective-permute-done.1 = bf16[256,128]{0,1:T(8,128)(2,1)S(1)} collective-permute-done((bf16[256,128]{0,1:T(8,128)(2,1)S(1)}, bf16[256,128]{0,1:T(8,128)(2,1)S(1)}, u32[]{:S(2)}, u32[]{:S(2)}) %collective-permute-start.1) | collective-permute-done | bytes 65568 | tf_op jit(solution)/shard_map/ppermute | solution.py:32
  60.5 10.3 %all-to-all-start.1 = ((bf16[8,256,256]{2,1,0:T(8,128)(2,1)}), bf16[8,256,256]{2,1,0:T(8,128)(2,1)S(1)}, u32[]{:S(2)}, u32[]{:S(2)}) async-start(bf16[8,256,256]{2,1,0:T(8,128)(2,1)} %broadcast_in_dim.31), calls=%async_computation.1 | async-start | bytes 2097152 | tf_op jit(solution)/shard_map/all_to_all | solution.py:24
  72.1 31.1 %dequant.1.weight_ref.refs_2_ = bf16[4,2048,256]{2,1,0:T(8,128)(2,1)} custom-call(s32[4,256,256]{2,1,0:T(8,128)} %copy-done, f32[4,8,128]{2,1,0:T(8,128)} %bitcast.49, f32[4,1,256]{2,1,0:T(1,128)} %slice.36.scale_ref.refs_4_), custom_call_target="tpu_custom_call" | custom-call | tf_op jit(solution)/shard_map/dequant/pallas_call | solution.py:73
  104.2 5.2 %project.1 = (f32[128,1024]{1,0:T(8,128)}, f32[128,1024]{1,0:T(8,128)}) custom-call(s32[1]{0:T(128)} %bitcast.core_ref, bf16[8,256,256]{2,1,0:T(8,128)(2,1)} %copy-done.1, bf16[4,2048,256]{2,1,0:T(8,128)(2,1)} %dequant.1.weight_ref.refs_2_), custom_call_target="tpu_custom_call" | custom-call | tf_op jit(solution)/shard_map/project/pallas_call | solution.py:108
  111.3 2.1 collective-permute-done.2
  115.2 6.6 %all-to-all-start.4 = ((bf16[4,32,1024]{2,1,0:T(8,128)(2,1)}), bf16[4,32,1024]{2,1,0:T(8,128)(2,1)S(1)}, u32[]{:S(2)}, u32[]{:S(2)}) async-start(bf16[4,32,1024]{2,1,0:T(8,128)(2,1)} %bitcast.12), calls=%async_computation.4 | async-start | bytes 524288 | tf_op jit(solution)/shard_map/all_to_all | solution.py:24
  121.9 7.2 %all-to-all-done.4 = bf16[4,32,1024]{2,1,0:T(8,128)(2,1)S(1)} async-done(((bf16[4,32,1024]{2,1,0:T(8,128)(2,1)}), bf16[4,32,1024]{2,1,0:T(8,128)(2,1)S(1)}, u32[]{:S(2)}, u32[]{:S(2)}) %all-to-all-start.4) | async-done | bytes 262176 | tf_op jit(solution)/shard_map/all_to_all | solution.py:24
  129.2 10.8 %all_to_all.50 = bf16[4,32,1024]{2,1,0:T(8,128)(2,1)S(1)} all-to-all(bf16[4,32,1024]{2,1,0:T(8,128)(2,1)S(1)} %broadcast_in_dim.34), channel_id=1, replica_groups=mesh['col_0'=4,'col_1'=2,'row'=8,'tok_0'=2,'tok_1'=4] {'col_0'}, dimensions={0} | all-to-all | bytes 524288 | tf_op jit(solution)/shard_map/all_to_all | solution.py:24
  140.0 1.9 collective-permute-start.3
  144.3 33.6 %grads.1 = (f32[4,8,256]{2,1,0:T(8,128)}, f32[2,32,64]{2,1,0:T(8,128)}) custom-call(bf16[8,256,256]{2,1,0:T(8,128)(2,1)} %copy-done.1, bf16[256,1024]{1,0:T(8,128)(2,1)} %pad_maximum_fusion.refs_1_, bf16[4,2048,256]{2,1,0:T(8,128)(2,1)} %dequant.1.weight_ref.refs_2_, s32[4,256,256]{2,1,0:T(8,128)} %copy-done, f32[4,1,256]{2,1,0:T(1,128)} %slice.36.scale_ref.refs_4_), custom_call_target="tpu_custom_call" | custom-call | tf_op jit(solution)/shard_map/grads/pallas_call | solution.py:176
  179.6 8.1 %all_to_all.51 = f32[4,34,128]{2,1,0:T(8,128)S(1)} all-to-all(f32[4,34,128]{2,1,0:T(8,128)S(1)} %pad_maximum_fusion.4), channel_id=1, replica_groups=mesh['col_0'=4,'col_1'=2,'row'=8,'tok_0'=2,'tok_1'=4] {'tok_1'}, dimensions={0} | all-to-all | bytes 139264 | tf_op jit(solution)/shard_map/all_to_all | solution.py:24
  188.4 5.1 %all-to-all-start.8 = ((f32[8,34,128]{2,1,0:T(8,128)}), f32[8,34,128]{2,1,0:T(8,128)S(1)}, u32[]{:S(2)}, u32[]{:S(2)}) async-start(f32[8,34,128]{2,1,0:T(8,128)} %broadcast_in_dim.37), calls=%async_computation.8 | async-start | bytes 327680 | tf_op jit(solution)/shard_map/all_to_all | solution.py:24
  194.3 5.4 %all-to-all-done.8 = f32[8,34,128]{2,1,0:T(8,128)S(1)} async-done(((f32[8,34,128]{2,1,0:T(8,128)}), f32[8,34,128]{2,1,0:T(8,128)S(1)}, u32[]{:S(2)}, u32[]{:S(2)}) %all-to-all-start.8) | async-done | bytes 139296 | tf_op jit(solution)/shard_map/all_to_all | solution.py:24
  199.7 3.5 %all-to-all-start.6 = ((bf16[4,256,256]{2,1,0:T(8,128)(2,1)}), bf16[4,256,256]{2,1,0:T(8,128)(2,1)S(1)}, u32[]{:S(2)}, u32[]{:S(2)}) async-start(bf16[4,256,256]{2,1,0:T(8,128)(2,1)} %bitcast.41), calls=%async_computation.6 | async-start | bytes 1048576 | tf_op jit(solution)/shard_map/all_to_all | solution.py:24
  203.2 9.5 %all-to-all-done.6 = bf16[4,256,256]{2,1,0:T(8,128)(2,1)S(1)} async-done(((bf16[4,256,256]{2,1,0:T(8,128)(2,1)}), bf16[4,256,256]{2,1,0:T(8,128)(2,1)S(1)}, u32[]{:S(2)}, u32[]{:S(2)}) %all-to-all-start.6) | async-done | bytes 524320 | tf_op jit(solution)/shard_map/all_to_all | solution.py:24
  213.4 7.3 %all-to-all-start.9 = ((f32[16,32,128]{2,1,0:T(8,128)}), f32[16,32,128]{2,1,0:T(8,128)S(1)}, u32[]{:S(2)}, u32[]{:S(2)}) async-start(f32[16,32,128]{2,1,0:T(8,128)} %broadcast_in_dim.74), calls=%async_computation.9 | async-start | bytes 524288 | tf_op jit(solution)/shard_map/all_to_all | solution.py:24
  222.1 12.6 %all-to-all-done.9 = f32[16,32,128]{2,1,0:T(8,128)S(1)} async-done(((f32[16,32,128]{2,1,0:T(8,128)}), f32[16,32,128]{2,1,0:T(8,128)S(1)}, u32[]{:S(2)}, u32[]{:S(2)}) %all-to-all-start.9) | async-done | bytes 262176 | tf_op jit(solution)/shard_map/all_to_all | solution.py:24
  (70 shorter events, 24.9 us)
Async XLA Ops:
  0.6 18.3 %copy-start.3 = (bf16[128,256]{1,0:T(8,128)(2,1)S(1)}, bf16[128,256]{1,0:T(8,128)(2,1)}, u32[]{:S(2)}) copy-start(bf16[128,256]{1,0:T(8,128)(2,1)} %param.9) | copy-start | bytes 196612
  1.5 17.5 %collective-permute-start = (bf16[128,128]{1,0:T(8,128)(2,1)S(1)}, bf16[128,128]{1,0:T(8,128)(2,1)S(1)}, u32[]{:S(2)}, u32[]{:S(2)}) collective-permute-start(bf16[128,128]{1,0:T(8,128)(2,1)S(1)} %constant_dynamic-slice_fusion), channel_id=1, source_target_pairs={{0,4},{4,0},{1,5},{5,1},{2,6},{6,2},{3,7},{7,3},{8,12},{12,8},{9,1... | collective-permute-start | bytes 98312 | tf_op jit(solution)/shard_map/ppermute | solution.py:32
  10.7 23.4 %all-to-all-start = ((bf16[8,128,256]{2,1,0:T(8,128)(2,1)}), bf16[8,128,256]{2,1,0:T(8,128)(2,1)S(1)}, u32[]{:S(2)}, u32[]{:S(2)}) async-start(bf16[8,128,256]{2,1,0:T(8,128)(2,1)} %bitcast.3), calls=%async_computation | async-start | bytes 1048576 | tf_op jit(solution)/shard_map/all_to_all | solution.py:24
  34.1 9.5 %all-to-all-start.3 = ((f32[4,40,256]{2,1,0:T(8,128)}), f32[4,40,256]{2,1,0:T(8,128)S(1)}, u32[]{:S(2)}, u32[]{:S(2)}) async-start(f32[4,40,256]{2,1,0:T(8,128)} %pad_maximum_fusion.1), calls=%async_computation.3 | async-start | bytes 327680 | tf_op jit(solution)/shard_map/all_to_all | solution.py:24
  44.6 26.2 %copy-start.5 = (bf16[256,8]{0,1:T(8,128)(2,1)S(1)}, bf16[256,8]{0,1:T(8,128)(2,1)}, u32[]{:S(2)}) copy-start(bf16[256,8]{0,1:T(8,128)(2,1)} %param.15) | copy-start | bytes 12292
  44.6 26.2 %copy-start.6 = (bf16[256,8]{0,1:T(8,128)(2,1)S(1)}, bf16[256,8]{0,1:T(8,128)(2,1)}, u32[]{:S(2)}) copy-start(bf16[256,8]{0,1:T(8,128)(2,1)} %param.14) | copy-start | bytes 12292
  44.6 14.7 %all-to-all-start.2 = ((s32[4,256,256]{2,1,0:T(8,128)}), s32[4,256,256]{2,1,0:T(8,128)S(1)}, u32[]{:S(2)}, u32[]{:S(2)}) async-start(s32[4,256,256]{2,1,0:T(8,128)} %broadcast_in_dim.32), calls=%async_computation.2 | async-start | bytes 2097152 | tf_op jit(solution)/shard_map/all_to_all | solution.py:24
  49.2 10.1 %collective-permute-start.1 = (bf16[256,128]{0,1:T(8,128)(2,1)S(1)}, bf16[256,128]{0,1:T(8,128)(2,1)S(1)}, u32[]{:S(2)}, u32[]{:S(2)}) collective-permute-start(bf16[256,128]{0,1:T(8,128)(2,1)S(1)} %fusion), channel_id=1, source_target_pairs={{0,4},{4,0},{1,5},{5,1},{2,6},{6,2},{3,7},{7,3},{8,12},{12,8},{9,1... | collective-permute-start | bytes 196616 | tf_op jit(solution)/shard_map/ppermute | solution.py:32
  59.4 12.7 %copy-start = (s32[4,256,256]{2,1,0:T(8,128)}, s32[4,256,256]{2,1,0:T(8,128)S(1)}, u32[]{:S(2)}) copy-start(s32[4,256,256]{2,1,0:T(8,128)S(1)} %all-to-all-done.2.codes_ref.refs_3_) | copy-start | bytes 3145732
  60.5 42.7 %all-to-all-start.1 = ((bf16[8,256,256]{2,1,0:T(8,128)(2,1)}), bf16[8,256,256]{2,1,0:T(8,128)(2,1)S(1)}, u32[]{:S(2)}, u32[]{:S(2)}) async-start(bf16[8,256,256]{2,1,0:T(8,128)(2,1)} %broadcast_in_dim.31), calls=%async_computation.1 | async-start | bytes 2097152 | tf_op jit(solution)/shard_map/all_to_all | solution.py:24
  103.2 1.0 copy-start.1
  109.4 4.0 %collective-permute-start.2 = (f32[128,1024]{1,0:T(8,128)}, f32[128,1024]{1,0:T(8,128)S(1)}, u32[]{:S(2)}, u32[]{:S(2)}) collective-permute-start(f32[128,1024]{1,0:T(8,128)} %get-tuple-element.8), channel_id=1, source_target_pairs={{0,64},{64,0},{1,65},{65,1},{2,66},{66,2},{3,67},{67,3},{4,68},{68... | collective-permute-start | bytes 1572872 | tf_op jit(solution)/shard_map/ppermute | solution.py:32
  115.2 13.8 %all-to-all-start.4 = ((bf16[4,32,1024]{2,1,0:T(8,128)(2,1)}), bf16[4,32,1024]{2,1,0:T(8,128)(2,1)S(1)}, u32[]{:S(2)}, u32[]{:S(2)}) async-start(bf16[4,32,1024]{2,1,0:T(8,128)(2,1)} %bitcast.12), calls=%async_computation.4 | async-start | bytes 524288 | tf_op jit(solution)/shard_map/all_to_all | solution.py:24
  140.0 3.4 %collective-permute-start.3 = (bf16[128,1024]{1,0:T(8,128)(2,1)S(1)}, bf16[128,1024]{1,0:T(8,128)(2,1)S(1)}, u32[]{:S(2)}, u32[]{:S(2)}) collective-permute-start(bf16[128,1024]{1,0:T(8,128)(2,1)S(1)} %bitcast.44), channel_id=1, source_target_pairs={{0,64},{64,0},{1,65},{65,1},{2,66},{66,2},{3,67},{67,3},{4,68},{68... | collective-permute-start | bytes 786440 | tf_op jit(solution)/shard_map/ppermute | solution.py:32
  143.5 36.1 %copy-start.4 = (f32[4,1,256]{2,1,0:T(1,128)S(1)}, f32[4,1,256]{2,1,0:T(1,128)}, u32[]{:S(2)}) copy-start(f32[4,1,256]{2,1,0:T(1,128)} %slice.36.scale_ref.refs_4_) | copy-start | bytes 12292
  144.3 49.2 %copy-start.2 = (bf16[256,1024]{1,0:T(8,128)(2,1)S(1)}, bf16[256,1024]{1,0:T(8,128)(2,1)}, u32[]{:S(2)}) copy-start(bf16[256,1024]{1,0:T(8,128)(2,1)} %pad_maximum_fusion.refs_1_) | copy-start | bytes 1572868
  188.4 11.3 %all-to-all-start.8 = ((f32[8,34,128]{2,1,0:T(8,128)}), f32[8,34,128]{2,1,0:T(8,128)S(1)}, u32[]{:S(2)}, u32[]{:S(2)}) async-start(f32[8,34,128]{2,1,0:T(8,128)} %broadcast_in_dim.37), calls=%async_computation.8 | async-start | bytes 327680 | tf_op jit(solution)/shard_map/all_to_all | solution.py:24
  199.7 13.0 %all-to-all-start.6 = ((bf16[4,256,256]{2,1,0:T(8,128)(2,1)}), bf16[4,256,256]{2,1,0:T(8,128)(2,1)S(1)}, u32[]{:S(2)}, u32[]{:S(2)}) async-start(bf16[4,256,256]{2,1,0:T(8,128)(2,1)} %bitcast.41), calls=%async_computation.6 | async-start | bytes 1048576 | tf_op jit(solution)/shard_map/all_to_all | solution.py:24
  213.4 21.3 %all-to-all-start.9 = ((f32[16,32,128]{2,1,0:T(8,128)}), f32[16,32,128]{2,1,0:T(8,128)S(1)}, u32[]{:S(2)}, u32[]{:S(2)}) async-start(f32[16,32,128]{2,1,0:T(8,128)} %broadcast_in_dim.74), calls=%async_computation.9 | async-start | bytes 524288 | tf_op jit(solution)/shard_map/all_to_all | solution.py:24

commit v2 on v1

v2 whole, which is shorter than its diff:
```python
import math

import jax
import jax.numpy as jnp
from jax import lax
from jax.experimental import pallas as pl
from jax.experimental.pallas import tpu as pltpu
from jax.sharding import Mesh
from jax.sharding import PartitionSpec as P


HEAD_DIM = 128
ENTRIES = 256
GROUP = 8
LOW = 8
HIGH = ENTRIES // LOW
TOK = ("tok_0", "tok_1")
ROW_TOK = ("row", "tok_0", "tok_1")
COL = ("col_0", "col_1")
COL_ROW = ("col_0", "col_1", "row")
f32, bf16 = jnp.float32, jnp.bfloat16


def exchange(pieces, axis):
    return lax.all_to_all(pieces, axis, 0, 0, tiled=True)


def copies(array, axis):
    pieces = jnp.broadcast_to(array[None], (lax.axis_size(axis), *array.shape))
    return exchange(pieces, axis)


def swap(array, axis):
    return lax.ppermute(array, axis, [(0, 1), (1, 0)])


def in_order(mine, theirs, place):
    first = place == 0
    return jnp.where(first, mine, theirs), jnp.where(first, theirs, mine)


def dequant_kernel(codes_ref, table_ref, scale_ref, out_ref):
    groups, rows = codes_ref.shape
    tables = [table_ref[i] for i in range(4)]
    scale = jnp.broadcast_to(scale_ref[...], (GROUP, rows))

    def group_rows(g):
        both = jnp.broadcast_to(codes_ref[pl.ds(g, 1), :], (GROUP, rows)).astype(jnp.int32)
        parts = []
        for at in range(0, rows, 128):
            packed = both[:, at : at + 128]
            total = None
            for book in range(2):
                code = (packed & 255) if book == 0 else (packed >> 8)
                place = code & 127
                near = jnp.take_along_axis(tables[2 * book], place, axis=1)
                far = jnp.take_along_axis(tables[2 * book + 1], place, axis=1)
                entry = jnp.where(code >= 128, far, near)
                total = entry if total is None else total + entry
            parts.append(total * scale[:, at : at + 128])
        return jnp.concatenate(parts, axis=1)

    def step(i, carry):
        for k in range(4):
            pair = [group_rows(i * 8 + 2 * k + n) for n in range(2)]
            start = pl.multiple_of(i * 64 + 16 * k, 16)
            out_ref[pl.ds(start, 16), :] = jnp.concatenate(pair, axis=0).astype(bf16)
        return carry

    lax.fori_loop(0, groups // 8, step, 0)


def dequantize(codes, table, scales):
    blocks, groups, rows = codes.shape
    return pl.pallas_call(
        dequant_kernel,
        grid=(blocks,),
        in_specs=[
            pl.BlockSpec((None, groups, rows), lambda i: (i, 0, 0)),
            pl.BlockSpec((4, GROUP, 128), lambda i: (0, 0, 0)),
            pl.BlockSpec((None, 1, rows), lambda i: (i, 0, 0)),
        ],
        out_specs=pl.BlockSpec((None, groups * GROUP, rows), lambda i: (i, 0, 0)),
        out_shape=jax.ShapeDtypeStruct((blocks, groups * GROUP, rows), bf16),
        cost_estimate=pl.CostEstimate(
            flops=blocks * 8_000_000_000, transcendentals=0, bytes_accessed=blocks * 1_500_000
        ),
        name="dequant",
    )(codes, table, scales)


def project_kernel(place_ref, att_ref, own_ref, others_ref, keep_ref, send_ref):
    steps, tokens, width = att_ref.shape
    half = tokens // 2

    def one(weight_ref):
        for out_ref, who in ((send_ref, 1 - place_ref[1]), (keep_ref, place_ref[1])):
            start = pl.multiple_of(who * half, half)
            total = None
            for z in range(steps):
                part = jnp.dot(
                    att_ref[z, pl.ds(start, half), :],
                    weight_ref[z * width : (z + 1) * width, :],
                    preferred_element_type=f32,
                )
                total = part if total is None else total + part
            out_ref[...] = total

    pl.when(pl.program_id(0) == 0)(lambda: one(own_ref))
    pl.when(pl.program_id(0) > 0)(lambda: one(others_ref))


def project(place, attended, own, others):
    steps, tokens, width = attended.shape
    blocks, depth, rows = others.shape
    blocks += 1
    out = jax.ShapeDtypeStruct((tokens // 2, blocks * rows), f32)
    out_spec = pl.BlockSpec((tokens // 2, rows), lambda i, place: (0, (place[0] + i) % blocks))
    return pl.pallas_call(
        project_kernel,
        grid_spec=pltpu.PrefetchScalarGridSpec(
            num_scalar_prefetch=1,
            grid=(blocks,),
            in_specs=[
                pl.BlockSpec((steps, tokens, width), lambda i, place: (0, 0, 0)),
                pl.BlockSpec((None, depth, rows), lambda i, place: (0, 0, 0)),
                pl.BlockSpec((None, depth, rows), lambda i, place: (jnp.maximum(i - 1, 0), 0, 0)),
            ],
            out_specs=[out_spec, out_spec],
        ),
        out_shape=[out, out],
        name="project",
    )(place, attended, own, others)


def bins_kernel(scaling, att_ref, misfit_ref, codes_ref, scale_ref, bins_ref, grad_ref, digit_ref):
    groups, rows = codes_ref.shape
    steps, _, width = att_ref.shape
    scale = scale_ref[...] * scaling
    misfit = misfit_ref[...]
    for z in range(steps):
        weight_grad = lax.dot_general(
            att_ref[z], misfit, (((0,), (0,)), ((), ())), preferred_element_type=f32
        )
        grad_ref[z * width : (z + 1) * width, :] = weight_grad * scale
    packed = codes_ref[...].astype(jnp.int32)
    for book in range(2):
        code = (packed & 255) if book == 0 else (packed >> 8)
        digit_ref[2 * book] = (code & (LOW - 1)).astype(f32)
        digit_ref[2 * book + 1] = (code >> 3).astype(f32)
    at = lax.broadcasted_iota(jnp.int32, (16, rows), 0)
    low_rows = [(2 * d + (at >= 8).astype(jnp.int32)).astype(f32).astype(bf16) for d in range(LOW // 2)]
    high_rows = [(16 * d + at).astype(f32).astype(bf16) for d in range(HIGH // 16)]
    zero, one = jnp.zeros((16, rows), bf16), jnp.ones((16, rows), bf16)
    chunk = 8

    def digit(which, g):
        return jnp.broadcast_to(digit_ref[which, pl.ds(g, 1), :], (16, rows)).astype(bf16)

    def step(i, totals):
        twice = []
        for k in range(chunk):
            entry = grad_ref[pl.ds(pl.multiple_of((i * chunk + k) * GROUP, GROUP), GROUP), :]
            twice.append(jnp.concatenate([entry, entry], axis=0).astype(bf16))
        done = []
        for book in range(2):
            highs, lows = [], []
            for k in range(chunk):
                low, high = digit(2 * book, i * chunk + k), digit(2 * book + 1, i * chunk + k)
                lows.append(
                    jnp.concatenate([jnp.where(low == r, twice[k], zero) for r in low_rows], axis=0)
                )
                highs.append(
                    jnp.concatenate([jnp.where(high == r, one, zero) for r in high_rows], axis=0)
                )
            part = lax.dot_general(
                jnp.concatenate(highs, axis=1),
                jnp.concatenate(lows, axis=1),
                (((1,), (1,)), ((), ())),
                preferred_element_type=f32,
            )
            done.append(totals[book] + part)
        return tuple(done)

    empty = jnp.zeros((HIGH, LOW * GROUP), f32)
    totals = lax.fori_loop(0, groups // chunk, step, (empty, empty), unroll=2)

    @pl.when(pl.program_id(0) == 0)
    def _():
        bins_ref[...] = jnp.zeros_like(bins_ref)

    for book in range(2):
        bins_ref[book] += totals[book]


def bin_gradients(attended, misfit, codes, scales, scaling):
    steps, tokens, width = attended.shape
    blocks, groups, rows = codes.shape
    return pl.pallas_call(
        lambda *refs: bins_kernel(scaling, *refs),
        grid=(blocks,),
        in_specs=[
            pl.BlockSpec((steps, tokens, width), lambda i: (0, 0, 0)),
            pl.BlockSpec((tokens, rows), lambda i: (0, i)),
            pl.BlockSpec((None, groups, rows), lambda i: (i, 0, 0)),
            pl.BlockSpec((None, 1, rows), lambda i: (i, 0, 0)),
        ],
        out_specs=pl.BlockSpec((2, HIGH, LOW * GROUP), lambda i: (0, 0, 0)),
        out_shape=jax.ShapeDtypeStruct((2, HIGH, LOW * GROUP), f32),
        scratch_shapes=[
            pltpu.VMEM((steps * width, rows), f32),
            pltpu.VMEM((4, groups, rows), f32),
        ],
        cost_estimate=pl.CostEstimate(
            flops=blocks * 8_000_000_000, transcendentals=0, bytes_accessed=blocks * 2_000_000
        ),
        name="bins",
    )(attended, misfit, codes, scales)


def attend(queries, keys, values, places):
    scores = jnp.einsum("qd,kd->qk", queries, keys, preferred_element_type=f32) / math.sqrt(HEAD_DIM)
    allowed = lax.iota(jnp.int32, keys.shape[0])[None, :] <= places[:, None]
    row_max = jnp.max(jnp.where(allowed, scores, -1e30), axis=-1, keepdims=True)
    exponent = jnp.where(allowed, jnp.exp(scores - row_max), 0.0)
    row_sum = jnp.sum(exponent, axis=-1, keepdims=True)
    weighted = jnp.einsum("qk,kd->qd", exponent.astype(bf16), values, preferred_element_type=f32)
    return (weighted / row_sum).astype(bf16)


def device_part(
    queries, key_rows, values, code_first, code_second, book_first, book_second, scales, target
):
    tok_rows, _ = queries.shape
    high, across = lax.axis_index("tok_0"), lax.axis_index("tok_1")
    count_across = lax.axis_size("tok_1")
    lane, core = lax.axis_index("col_0"), lax.axis_index("col_1")
    count_lane = lax.axis_size("col_0")
    rows = code_first.shape[0]
    tokens = lax.axis_size(TOK) * tok_rows

    def of_head(array, head):
        return lax.dynamic_slice_in_dim(array, head * HEAD_DIM, HEAD_DIM, 1)

    their_queries = swap(of_head(queries, 1 - high), "tok_0")
    pairs = jnp.stack(
        [jnp.concatenate([of_head(key_rows, h), of_head(values, h)], axis=1) for h in range(2)]
    )
    pairs = jnp.broadcast_to(pairs[:, None], (2, count_across, tok_rows, 2 * HEAD_DIM))
    pairs = exchange(pairs.reshape(-1, tok_rows, 2 * HEAD_DIM), TOK)
    pairs = pairs.reshape(tokens, 2 * HEAD_DIM)
    own_queries = jnp.concatenate(in_order(of_head(queries, high), their_queries, high), axis=0)
    place = across * tok_rows + lax.iota(jnp.int32, tok_rows)
    places = jnp.concatenate([place, place + count_across * tok_rows])
    head_out = attend(own_queries, pairs[:, :HEAD_DIM], pairs[:, HEAD_DIM:], places)
    head_out = jnp.concatenate(in_order(head_out, swap(head_out, "tok_0"), high), axis=1)
    attended = copies(head_out, "row")

    own_codes = (code_first + ENTRIES * code_second).T.astype(f32)
    share = tok_rows // count_lane
    wanted = target.reshape(2, count_across, count_lane, share, rows)
    wanted = lax.dynamic_index_in_dim(wanted, core, 0, keepdims=False)
    wanted = lax.dynamic_index_in_dim(wanted, lane, 1, keepdims=False).astype(f32)
    groups = own_codes.shape[0]
    own_scales = jnp.broadcast_to(scales[None, None], (count_across, 8, rows))
    sent = jnp.broadcast_to(own_codes[None], (count_across, groups, rows))
    sent = jnp.concatenate([sent, own_scales, wanted], axis=1)
    sent, _ = lax.optimization_barrier((sent, pairs))
    side = exchange(sent, "tok_1")
    codes, row_scales, wanted = side[:, :groups], side[:, groups : groups + 1], side[:, groups + 8 :]
    books = jnp.stack([book_first, book_second]).astype(f32).transpose(0, 2, 1)
    table = books.reshape(2, GROUP, 2, 128).transpose(0, 2, 1, 3).reshape(4, GROUP, 128)
    own_weight = dequantize(own_codes[None], table, scales[None, None])
    following = (across + 1 + lax.iota(jnp.int32, count_across - 1)) % count_across
    other_codes = [lax.dynamic_slice_in_dim(codes, following[k], 1, 0) for k in range(3)]
    other_scales = [lax.dynamic_slice_in_dim(row_scales, following[k], 1, 0) for k in range(3)]
    other_codes, other_scales = jnp.concatenate(other_codes), jnp.concatenate(other_scales)
    other_weight = dequantize(other_codes, table, other_scales)

    keep, send = project(jnp.stack([across, core]), attended, own_weight, other_weight)
    half_sum = (keep + swap(send, "col_1")).astype(bf16)
    parts = exchange(half_sum.reshape(count_lane, share, -1), "col_0")
    output = jnp.sum(parts.astype(f32), axis=0)
    wanted = wanted.transpose(1, 0, 2).reshape(share, -1)
    misfit_share = (output - wanted).astype(bf16)
    misfit_half = copies(misfit_share, "col_0").reshape(tok_rows, -1)
    other_half = swap(misfit_half, "col_1")
    misfit = jnp.concatenate(in_order(misfit_half, other_half, core), axis=0)

    by_rows = misfit.reshape(2 * tok_rows, count_across, rows).transpose(1, 0, 2)
    by_tokens = exchange(by_rows, "tok_1").reshape(count_across, 2, tok_rows, rows)

    scale_part = jnp.sum(misfit_share.astype(f32) * output, axis=0).reshape(count_across, rows)
    scale_part = scale_part / (row_scales[:, 0] * tokens)
    bins = bin_gradients(attended, misfit, codes, row_scales, 1.0 / tokens)

    peers = COL + ("tok_1",)
    count_col = lax.axis_size(COL)
    scale_part = scale_part.reshape(count_across, count_col, -1).transpose(1, 0, 2)
    piece = scale_part.shape[2]
    scale_part = scale_part.reshape(count_col * count_across, 1, piece)
    bins = bins.reshape(count_col * count_across, 1, 128)
    scale_part = jnp.pad(scale_part, ((0, 0), (0, 0), (0, 128 - piece)))
    sums = jnp.concatenate([bins, scale_part], axis=1)
    sums, by_tokens = lax.optimization_barrier((sums, by_tokens))
    sums = jnp.sum(exchange(sums, peers), axis=0)
    bins = jnp.sum(copies(sums[:1], ("row", "tok_0")), axis=0)
    done = copies(jnp.concatenate([bins, sums[1:]], axis=0), peers)
    grad_scales = done[:, 1, :piece].reshape(count_col, count_across, piece)
    grad_scales = lax.dynamic_index_in_dim(grad_scales, across, 1, keepdims=False).reshape(rows)
    misfit_out = by_tokens.transpose(1, 0, 2, 3).reshape(tokens, rows)
    return misfit_out, grad_scales, done[:, 0].reshape(2, ENTRIES, GROUP)


def solution(mesh):
    split = Mesh(
        mesh.devices.reshape(4, 2, mesh.shape["row"], 2, 4),
        ("col_0", "col_1", "row", "tok_0", "tok_1"),
    )
    return jax.shard_map(
        device_part,
        mesh=split,
        in_specs=(
            P(TOK, COL_ROW),
            P(TOK, COL_ROW),
            P(TOK, COL_ROW),
            P(ROW_TOK, COL),
            P(ROW_TOK, COL),
            P(),
            P(),
            P(ROW_TOK),
            P(None, ROW_TOK),
        ),
        out_specs=(P(None, ROW_TOK), P(ROW_TOK), P()),
        check_vma=False,
    )
```

time: 238 us -> 225 us (0.945)
  the two profiles are of different devices: /device:TPU:8 before, /device:TPU:1 now
where the time goes in v2:
time: 225 us; the launch traced here: 223 us
  Pallas kernels  70.2 us (31%)
  starting transfers between devices  59.5 us (26%)
  waiting for transfers between devices  34.3 us (15%)
  blocking collectives  31.5 us (14%)
  local copies, waits for them, and re-layouts  11.9 us (5%)
  other arithmetic  8.15 us (4%)
  between operations  6.85 us (3%)
    all_to_all x7, starting transfers between devices, exchange(): return lax.all_to_all(pieces, axis, 0, 0, tiled=True)  39.9 us
    pallas_call x2, Pallas kernels, dequantize(): pl.pallas_call(dequant_kernel, grid=(blocks,), in_specs=[pl.BlockSpec((No...  33.3 us
    all_to_all x2, blocking collectives, exchange(): return lax.all_to_all(pieces, axis, 0, 0, tiled=True)  31.5 us
    pallas_call x1, Pallas kernels, bin_gradients(): pl.pallas_call(lambda *refs: bins_kernel(scaling, *refs), grid=(blocks,),...  30.7 us
    all_to_all x7, waiting for transfers between devices, exchange(): return lax.all_to_all(pieces, axis, 0, 0, tiled=True)  25.5 us
    ppermute x4, starting transfers between devices, swap(): return lax.ppermute(array, axis, [(0, 1), (1, 0)])  19.6 us
    ppermute x4, waiting for transfers between devices, swap(): return lax.ppermute(array, axis, [(0, 1), (1, 0)])  8.8 us
    pallas_call x1, Pallas kernels, project(): pl.pallas_call(project_kernel, grid_spec=pltpu.PrefetchScalarGridSpec(num...  6.19 us
  transfers between devices with their start and end apart: 11, of which 8 were waited for; matrix products, arithmetic and copies ran while one was open for 5% of the time, Pallas kernels for 29%

profile of v2, /device:TPU:1, one launch (start us, length us, event | category | flops | bytes accessed | tf_op | source)
XLA Modules:
  0.0 223.3 jit_solution(8899771055415821086)
XLA Ops:
  3.1 10.2 %all-to-all-start = ((bf16[8,128,256]{2,1,0:T(8,128)(2,1)}), bf16[8,128,256]{2,1,0:T(8,128)(2,1)S(1)}, u32[]{:S(2)}, u32[]{:S(2)}) async-start(bf16[8,128,256]{2,1,0:T(8,128)(2,1)} %bitcast.2), calls=%async_computation | async-start | bytes 1048576 | tf_op jit(solution)/shard_map/all_to_all | solution.py:25
  13.4 7.3 %collective-permute-start = (bf16[128,128]{1,0:T(8,128)(2,1)S(1)}, bf16[128,128]{1,0:T(8,128)(2,1)S(1)}, u32[]{:S(2)}, u32[]{:S(2)}) collective-permute-start(bf16[128,128]{1,0:T(8,128)(2,1)S(1)} %constant_dynamic-slice_fusion.6), channel_id=1, source_target_pairs={{0,4},{4,0},{1,5},{5,1},{2,6},{6,2},{3,7},{7,3},{8,12},{12,8},{9,1... | collective-permute-start | bytes 98312 | tf_op jit(solution)/shard_map/ppermute | solution.py:34
  25.2 9.3 %dequant.2.own_ref = bf16[1,2048,256]{2,1,0:T(8,128)(2,1)} custom-call(f32[1,256,256]{2,1,0:T(8,128)} %get-tuple-element.36.codes_ref, f32[4,8,128]{2,1,0:T(8,128)} %bitcast.78, f32[1,1,256]{2,1,0:T(1,128)} %bitcast.84), custom_call_target="tpu_custom_call" | custom-call | flops 8000000000 | bytes 1500000 | tf_op jit(solution)/shard_map/dequant/pallas_call | solution.py:75
  40.4 4.0 %all-to-all-start.2 = ((f32[4,296,256]{2,1,0:T(8,128)}), f32[4,296,256]{2,1,0:T(8,128)S(1)}, u32[]{:S(2)}, u32[]{:S(2)}) async-start(f32[4,296,256]{2,1,0:T(8,128)} %pad_maximum_fusion), calls=%async_computation.2 | async-start | bytes 2424832 | tf_op jit(solution)/shard_map/all_to_all | solution.py:25
  45.6 2.2 collective-permute-start.1
  48.5 6.1 %collective-permute-done.1 = bf16[256,128]{0,1:T(8,128)(2,1)S(1)} collective-permute-done((bf16[256,128]{0,1:T(8,128)(2,1)S(1)}, bf16[256,128]{0,1:T(8,128)(2,1)S(1)}, u32[]{:S(2)}, u32[]{:S(2)}) %collective-permute-start.1) | collective-permute-done | bytes 65568 | tf_op jit(solution)/shard_map/ppermute | solution.py:34
  54.7 4.8 %all-to-all-done.2 = f32[4,296,256]{2,1,0:T(8,128)S(1)} async-done(((f32[4,296,256]{2,1,0:T(8,128)}), f32[4,296,256]{2,1,0:T(8,128)S(1)}, u32[]{:S(2)}, u32[]{:S(2)}) %all-to-all-start.2) | async-done | bytes 1212448 | tf_op jit(solution)/shard_map/all_to_all | solution.py:25
  60.6 10.0 %all-to-all-start.1 = ((bf16[8,256,256]{2,1,0:T(8,128)(2,1)}), bf16[8,256,256]{2,1,0:T(8,128)(2,1)S(1)}, u32[]{:S(2)}, u32[]{:S(2)}) async-start(bf16[8,256,256]{2,1,0:T(8,128)(2,1)} %broadcast_in_dim.30), calls=%async_computation.1 | async-start | bytes 2097152 | tf_op jit(solution)/shard_map/all_to_all | solution.py:25
  72.8 24.0 %dequant.3.others_ref = bf16[3,2048,256]{2,1,0:T(8,128)(2,1)} custom-call(f32[3,256,256]{2,1,0:T(8,128)} %pad_maximum_fusion.1.codes_ref, f32[4,8,128]{2,1,0:T(8,128)} %bitcast.79, f32[3,1,256]{2,1,0:T(1,128)} %pad_maximum_fusion.6.scale_ref), custom_call_target="tpu_custom_call" | custom-call | flops 24000000000 | bytes 4500000 | tf_op jit(solution)/shard_map/dequant/pallas_call | solution.py:75
  98.7 6.2 %project.1 = (f32[128,1024]{1,0:T(8,128)}, f32[128,1024]{1,0:T(8,128)}) custom-call(s32[2]{0:T(128)} %pad_add_fusion.1.place_ref, bf16[8,256,256]{2,1,0:T(8,128)(2,1)} %copy-done, bf16[1,2048,256]{2,1,0:T(8,128)(2,1)} %dequant.2.own_ref, bf16[3,2048,256]{2,1,0:T(8,128)(2,1)} %dequant.3.others_ref), custom_call_target="tpu_custom_call" | custom-call | tf_op jit(solution)/shard_map/project/pallas_call | solution.py:119
  104.9 4.6 %collective-permute-start.2 = (f32[128,1024]{1,0:T(8,128)}, f32[128,1024]{1,0:T(8,128)S(1)}, u32[]{:S(2)}, u32[]{:S(2)}) collective-permute-start(f32[128,1024]{1,0:T(8,128)} %get-tuple-element.10), channel_id=1, source_target_pairs={{0,64},{64,0},{1,65},{65,1},{2,66},{66,2},{3,67},{67,3},{4,68},{68... | collective-permute-start | bytes 1572872 | tf_op jit(solution)/shard_map/ppermute | solution.py:34
  109.4 1.7 collective-permute-done.2
  111.2 1.8 add_convert_fusion
  113.0 3.4 %all-to-all-start.3 = ((bf16[4,32,1024]{2,1,0:T(8,128)(2,1)}), bf16[4,32,1024]{2,1,0:T(8,128)(2,1)S(1)}, u32[]{:S(2)}, u32[]{:S(2)}) async-start(bf16[4,32,1024]{2,1,0:T(8,128)(2,1)} %bitcast.18), calls=%async_computation.3 | async-start | bytes 524288 | tf_op jit(solution)/shard_map/all_to_all | solution.py:25
  116.4 7.3 %all-to-all-done.3 = bf16[4,32,1024]{2,1,0:T(8,128)(2,1)S(1)} async-done(((bf16[4,32,1024]{2,1,0:T(8,128)(2,1)}), bf16[4,32,1024]{2,1,0:T(8,128)(2,1)S(1)}, u32[]{:S(2)}, u32[]{:S(2)}) %all-to-all-start.3) | async-done | bytes 262176 | tf_op jit(solution)/shard_map/all_to_all | solution.py:25
  124.5 3.5 %all-to-all-start.4 = ((bf16[4,32,1024]{2,1,0:T(8,128)(2,1)}), bf16[4,32,1024]{2,1,0:T(8,128)(2,1)S(1)}, u32[]{:S(2)}, u32[]{:S(2)}) async-start(bf16[4,32,1024]{2,1,0:T(8,128)(2,1)} %broadcast_in_dim.35), calls=%async_computation.4 | async-start | bytes 524288 | tf_op jit(solution)/shard_map/all_to_all | solution.py:25
  128.1 5.6 %all-to-all-done.4 = bf16[4,32,1024]{2,1,0:T(8,128)(2,1)S(1)} async-done(((bf16[4,32,1024]{2,1,0:T(8,128)(2,1)}), bf16[4,32,1024]{2,1,0:T(8,128)(2,1)S(1)}, u32[]{:S(2)}, u32[]{:S(2)}) %all-to-all-start.4) | async-done | bytes 262176 | tf_op jit(solution)/shard_map/all_to_all | solution.py:25
  133.7 5.6 %collective-permute-start.3 = (bf16[128,1024]{1,0:T(8,128)(2,1)S(1)}, bf16[128,1024]{1,0:T(8,128)(2,1)S(1)}, u32[]{:S(2)}, u32[]{:S(2)}) collective-permute-start(bf16[128,1024]{1,0:T(8,128)(2,1)S(1)} %bitcast.70), channel_id=1, source_target_pairs={{0,64},{64,0},{1,65},{65,1},{2,66},{66,2},{3,67},{67,3},{4,68},{68... | collective-permute-start | bytes 786440 | tf_op jit(solution)/shard_map/ppermute | solution.py:34
  141.4 3.5 %all-to-all-start.5 = ((bf16[4,256,256]{2,1,0:T(8,128)(2,1)}), bf16[4,256,256]{2,1,0:T(8,128)(2,1)S(1)}, u32[]{:S(2)}, u32[]{:S(2)}) async-start(bf16[4,256,256]{2,1,0:T(8,128)(2,1)} %bitcast.66), calls=%async_computation.5 | async-start | bytes 1048576 | tf_op jit(solution)/shard_map/all_to_all | solution.py:25
  144.9 30.7 %bins.1 = f32[2,32,64]{2,1,0:T(8,128)} custom-call(bf16[8,256,256]{2,1,0:T(8,128)(2,1)} %copy-done, bf16[256,1024]{1,0:T(8,128)(2,1)} %copy-done.2, f32[4,256,256]{2,1,0:T(8,128)} %copy-done.1, f32[4,1,256]{2,1,0:T(1,128)} %copy-done.6), custom_call_target="tpu_custom_call" | custom-call | flops 32000000000 | bytes 8000000 | tf_op jit(solution)/shard_map/bins/pallas_call | solution.py:199
  176.5 14.0 %all_to_all.45 = f32[32,2,128]{2,1,0:T(2,128)S(1)} all-to-all(f32[32,2,128]{2,1,0:T(2,128)S(1)} %copy.70), channel_id=1, replica_groups=mesh['col_0'=4,'col_1'=2,'row'=8,'tok_0'=2,'tok_1'=4] {'col_0','col_1','..., dimensions={0} | all-to-all | bytes 65536 | tf_op jit(solution)/shard_map/all_to_all | solution.py:25
  190.5 17.5 %all_to_all.46 = f32[16,1,128]{2,1,0:T(1,128)S(1)} all-to-all(f32[16,1,128]{2,1,0:T(1,128)S(1)} %broadcast_in_dim.71), channel_id=1, replica_groups=mesh['col_0'=4,'col_1'=2,'row'=8,'tok_0'=2,'tok_1'=4] {'row','tok_0'}, dimensions={0} | all-to-all | bytes 16384 | tf_op jit(solution)/shard_map/all_to_all | solution.py:25
  208.7 5.3 %all-to-all-start.8 = ((f32[32,2,128]{2,1,0:T(2,128)}), f32[32,2,128]{2,1,0:T(2,128)S(1)}, u32[]{:S(2)}, u32[]{:S(2)}) async-start(f32[32,2,128]{2,1,0:T(2,128)} %broadcast_in_dim.72), calls=%async_computation.8 | async-start | bytes 65536 | tf_op jit(solution)/shard_map/all_to_all | solution.py:25
  214.8 6.8 %all-to-all-done.8 = f32[32,2,128]{2,1,0:T(2,128)S(1)} async-done(((f32[32,2,128]{2,1,0:T(2,128)}), f32[32,2,128]{2,1,0:T(2,128)S(1)}, u32[]{:S(2)}, u32[]{:S(2)}) %all-to-all-start.8) | async-done | bytes 32800 | tf_op jit(solution)/shard_map/all_to_all | solution.py:25
  (89 shorter events, 21.1 us)
Async XLA Ops:
  1.4 12.0 %copy-start.5 = (bf16[128,256]{1,0:T(8,128)(2,1)S(1)}, bf16[128,256]{1,0:T(8,128)(2,1)}, u32[]{:S(2)}) copy-start(bf16[128,256]{1,0:T(8,128)(2,1)} %param.9) | copy-start | bytes 196612
  1.4 19.3 %copy-start.3 = (s32[256,256]{1,0:T(8,128)S(1)}, s32[256,256]{1,0:T(8,128)}, u32[]{:S(2)}) copy-start(s32[256,256]{1,0:T(8,128)} %param.13) | copy-start | bytes 786436
  2.3 18.5 %copy-start.4 = (s32[256,256]{1,0:T(8,128)S(1)}, s32[256,256]{1,0:T(8,128)}, u32[]{:S(2)}) copy-start(s32[256,256]{1,0:T(8,128)} %param.12) | copy-start | bytes 786436
  3.1 18.5 %copy-start.7 = (bf16[256,8]{0,1:T(8,128)(2,1)S(1)}, bf16[256,8]{0,1:T(8,128)(2,1)}, u32[]{:S(2)}) copy-start(bf16[256,8]{0,1:T(8,128)(2,1)} %param.15) | copy-start | bytes 12292
  3.1 18.5 %copy-start.8 = (bf16[256,8]{0,1:T(8,128)(2,1)S(1)}, bf16[256,8]{0,1:T(8,128)(2,1)}, u32[]{:S(2)}) copy-start(bf16[256,8]{0,1:T(8,128)(2,1)} %param.14) | copy-start | bytes 12292
  3.1 37.2 %all-to-all-start = ((bf16[8,128,256]{2,1,0:T(8,128)(2,1)}), bf16[8,128,256]{2,1,0:T(8,128)(2,1)S(1)}, u32[]{:S(2)}, u32[]{:S(2)}) async-start(bf16[8,128,256]{2,1,0:T(8,128)(2,1)} %bitcast.2), calls=%async_computation | async-start | bytes 1048576 | tf_op jit(solution)/shard_map/all_to_all | solution.py:25
  13.4 26.9 %collective-permute-start = (bf16[128,128]{1,0:T(8,128)(2,1)S(1)}, bf16[128,128]{1,0:T(8,128)(2,1)S(1)}, u32[]{:S(2)}, u32[]{:S(2)}) collective-permute-start(bf16[128,128]{1,0:T(8,128)(2,1)S(1)} %constant_dynamic-slice_fusion.6), channel_id=1, source_target_pairs={{0,4},{4,0},{1,5},{5,1},{2,6},{6,2},{3,7},{7,3},{8,12},{12,8},{9,1... | collective-permute-start | bytes 98312 | tf_op jit(solution)/shard_map/ppermute | solution.py:34
  21.7 2.3 %copy-start.9 = (f32[256]{0:T(256)S(1)}, f32[256]{0:T(256)}, u32[]{:S(2)}) copy-start(f32[256]{0:T(256)} %param.16) | copy-start | bytes 3076
  40.4 19.1 %all-to-all-start.2 = ((f32[4,296,256]{2,1,0:T(8,128)}), f32[4,296,256]{2,1,0:T(8,128)S(1)}, u32[]{:S(2)}, u32[]{:S(2)}) async-start(f32[4,296,256]{2,1,0:T(8,128)} %pad_maximum_fusion), calls=%async_computation.2 | async-start | bytes 2424832 | tf_op jit(solution)/shard_map/all_to_all | solution.py:25
  45.6 8.9 %collective-permute-start.1 = (bf16[256,128]{0,1:T(8,128)(2,1)S(1)}, bf16[256,128]{0,1:T(8,128)(2,1)S(1)}, u32[]{:S(2)}, u32[]{:S(2)}) collective-permute-start(bf16[256,128]{0,1:T(8,128)(2,1)S(1)} %fusion), channel_id=1, source_target_pairs={{0,4},{4,0},{1,5},{5,1},{2,6},{6,2},{3,7},{7,3},{8,12},{12,8},{9,1... | collective-permute-start | bytes 196616 | tf_op jit(solution)/shard_map/ppermute | solution.py:34
  60.6 37.1 %all-to-all-start.1 = ((bf16[8,256,256]{2,1,0:T(8,128)(2,1)}), bf16[8,256,256]{2,1,0:T(8,128)(2,1)S(1)}, u32[]{:S(2)}, u32[]{:S(2)}) async-start(bf16[8,256,256]{2,1,0:T(8,128)(2,1)} %broadcast_in_dim.30), calls=%async_computation.1 | async-start | bytes 2097152 | tf_op jit(solution)/shard_map/all_to_all | solution.py:25
  70.6 0.6 copy-start.6
  70.8 2.0 copy-start.1
  97.7 1.0 copy-start
  104.9 6.3 %collective-permute-start.2 = (f32[128,1024]{1,0:T(8,128)}, f32[128,1024]{1,0:T(8,128)S(1)}, u32[]{:S(2)}, u32[]{:S(2)}) collective-permute-start(f32[128,1024]{1,0:T(8,128)} %get-tuple-element.10), channel_id=1, source_target_pairs={{0,64},{64,0},{1,65},{65,1},{2,66},{66,2},{3,67},{67,3},{4,68},{68... | collective-permute-start | bytes 1572872 | tf_op jit(solution)/shard_map/ppermute | solution.py:34
  113.0 10.8 %all-to-all-start.3 = ((bf16[4,32,1024]{2,1,0:T(8,128)(2,1)}), bf16[4,32,1024]{2,1,0:T(8,128)(2,1)S(1)}, u32[]{:S(2)}, u32[]{:S(2)}) async-start(bf16[4,32,1024]{2,1,0:T(8,128)(2,1)} %bitcast.18), calls=%async_computation.3 | async-start | bytes 524288 | tf_op jit(solution)/shard_map/all_to_all | solution.py:25
  124.5 9.1 %all-to-all-start.4 = ((bf16[4,32,1024]{2,1,0:T(8,128)(2,1)}), bf16[4,32,1024]{2,1,0:T(8,128)(2,1)S(1)}, u32[]{:S(2)}, u32[]{:S(2)}) async-start(bf16[4,32,1024]{2,1,0:T(8,128)(2,1)} %broadcast_in_dim.35), calls=%async_computation.4 | async-start | bytes 524288 | tf_op jit(solution)/shard_map/all_to_all | solution.py:25
  133.7 6.7 %collective-permute-start.3 = (bf16[128,1024]{1,0:T(8,128)(2,1)S(1)}, bf16[128,1024]{1,0:T(8,128)(2,1)S(1)}, u32[]{:S(2)}, u32[]{:S(2)}) collective-permute-start(bf16[128,1024]{1,0:T(8,128)(2,1)S(1)} %bitcast.70), channel_id=1, source_target_pairs={{0,64},{64,0},{1,65},{65,1},{2,66},{66,2},{3,67},{67,3},{4,68},{68... | collective-permute-start | bytes 786440 | tf_op jit(solution)/shard_map/ppermute | solution.py:34
  140.5 4.4 %copy-start.2 = (bf16[256,1024]{1,0:T(8,128)(2,1)}, bf16[256,1024]{1,0:T(8,128)(2,1)S(1)}, u32[]{:S(2)}) copy-start(bf16[256,1024]{1,0:T(8,128)(2,1)S(1)} %pad_maximum_fusion.2.refs_1_) | copy-start | bytes 1572868
  141.4 35.0 %all-to-all-start.5 = ((bf16[4,256,256]{2,1,0:T(8,128)(2,1)}), bf16[4,256,256]{2,1,0:T(8,128)(2,1)S(1)}, u32[]{:S(2)}, u32[]{:S(2)}) async-start(bf16[4,256,256]{2,1,0:T(8,128)(2,1)} %bitcast.66), calls=%async_computation.5 | async-start | bytes 1048576 | tf_op jit(solution)/shard_map/all_to_all | solution.py:25
  208.7 13.0 %all-to-all-start.8 = ((f32[32,2,128]{2,1,0:T(2,128)}), f32[32,2,128]{2,1,0:T(2,128)S(1)}, u32[]{:S(2)}, u32[]{:S(2)}) async-start(f32[32,2,128]{2,1,0:T(2,128)} %broadcast_in_dim.72), calls=%async_computation.8 | async-start | bytes 65536 | tf_op jit(solution)/shard_map/all_to_all | solution.py:25

commit v3 on v2

v3 whole, which is shorter than its diff:
```python
import math

import jax
import jax.numpy as jnp
from jax import lax
from jax.experimental import pallas as pl
from jax.experimental.pallas import tpu as pltpu
from jax.sharding import Mesh
from jax.sharding import PartitionSpec as P


HEAD_DIM = 128
ENTRIES = 256
GROUP = 8
LOW = 8
HIGH = ENTRIES // LOW
TOK = ("tok_0", "tok_1")
ROW_TOK = ("row", "tok_0", "tok_1")
COL = ("col_0", "col_1")
COL_ROW = ("col_0", "col_1", "row")
f32, bf16 = jnp.float32, jnp.bfloat16


def exchange(pieces, axis):
    return lax.all_to_all(pieces, axis, 0, 0, tiled=True)


def copies(array, axis):
    pieces = jnp.broadcast_to(array[None], (lax.axis_size(axis), *array.shape))
    return exchange(pieces, axis)


def swap(array, axis):
    return lax.ppermute(array, axis, [(0, 1), (1, 0)])


def in_order(mine, theirs, place):
    first = place == 0
    return jnp.where(first, mine, theirs), jnp.where(first, theirs, mine)


def dequant_kernel(block_ref, table_ref, *refs):
    weight_ref, plan_ref = refs[-2:]
    groups, rows = weight_ref.shape[0] // GROUP, weight_ref.shape[1]
    tables = [table_ref[i] for i in range(4)]
    plan_ref[...] = block_ref[: groups + 8, :]
    scale = jnp.broadcast_to(block_ref[groups : groups + 1, :], (GROUP, rows))

    def group_rows(g):
        both = jnp.broadcast_to(block_ref[pl.ds(g, 1), :], (GROUP, rows)).astype(jnp.int32)
        parts = []
        for at in range(0, rows, 128):
            packed = both[:, at : at + 128]
            total = None
            for book in range(2):
                code = (packed & 255) if book == 0 else (packed >> 8)
                place = code & 127
                near = jnp.take_along_axis(tables[2 * book], place, axis=1)
                far = jnp.take_along_axis(tables[2 * book + 1], place, axis=1)
                entry = jnp.where(code >= 128, far, near)
                total = entry if total is None else total + entry
            parts.append(total * scale[:, at : at + 128])
        return jnp.concatenate(parts, axis=1)

    def step(i, carry):
        for k in range(4):
            pair = [group_rows(i * 8 + 2 * k + n) for n in range(2)]
            start = pl.multiple_of(i * 64 + 16 * k, 16)
            weight_ref[pl.ds(start, 16), :] = jnp.concatenate(pair, axis=0).astype(bf16)
        return carry

    lax.fori_loop(0, groups // 8, step, 0)


def dequantize(block, table, at, blocks, groups, before=()):
    rows = block.shape[1]
    return pl.pallas_call(
        dequant_kernel,
        grid=(1,),
        in_specs=[
            pl.BlockSpec(block.shape, lambda i: (0, 0)),
            pl.BlockSpec((4, GROUP, 128), lambda i: (0, 0, 0)),
        ]
        + [pl.BlockSpec(memory_space=pl.ANY)] * len(before),
        out_specs=[
            pl.BlockSpec((None, groups * GROUP, rows), lambda i: (at, 0, 0)),
            pl.BlockSpec((None, groups + 8, rows), lambda i: (at, 0, 0)),
        ],
        out_shape=[
            jax.ShapeDtypeStruct((blocks, groups * GROUP, rows), bf16),
            jax.ShapeDtypeStruct((blocks, groups + 8, rows), f32),
        ],
        input_output_aliases={2: 0, 3: 1} if before else {},
        cost_estimate=pl.CostEstimate(
            flops=8_000_000_000, transcendentals=0, bytes_accessed=1_500_000
        ),
        name="dequant",
    )(block, table, *before)


def project_kernel(place_ref, att_ref, weight_ref, keep_ref, send_ref, all_ref):
    steps, tokens, width = att_ref.shape
    half = tokens // 2
    total = None
    for z in range(steps):
        part = jnp.dot(
            att_ref[z], weight_ref[z * width : (z + 1) * width, :], preferred_element_type=f32
        )
        total = part if total is None else total + part
    all_ref[...] = total
    keep_ref[...] = all_ref[pl.ds(pl.multiple_of(place_ref[1] * half, half), half), :]
    send_ref[...] = all_ref[pl.ds(pl.multiple_of((1 - place_ref[1]) * half, half), half), :]


def project(place, attended, weight):
    steps, tokens, width = attended.shape
    blocks, depth, rows = weight.shape
    out = jax.ShapeDtypeStruct((tokens // 2, blocks * rows), f32)
    out_spec = pl.BlockSpec((tokens // 2, rows), lambda i, place: (0, (place[0] + i) % blocks))
    return pl.pallas_call(
        project_kernel,
        grid_spec=pltpu.PrefetchScalarGridSpec(
            num_scalar_prefetch=1,
            grid=(blocks,),
            in_specs=[
                pl.BlockSpec((steps, tokens, width), lambda i, place: (0, 0, 0)),
                pl.BlockSpec((None, depth, rows), lambda i, place: (i, 0, 0)),
            ],
            out_specs=[out_spec, out_spec],
            scratch_shapes=[pltpu.VMEM((tokens, rows), f32)],
        ),
        out_shape=[out, out],
        name="project",
    )(place, attended, weight)


def bins_kernel(scaling, place_ref, att_ref, misfit_ref, plan_ref, bins_ref, grad_ref, digit_ref):
    groups, rows = digit_ref.shape[1:]
    steps, _, width = att_ref.shape
    scale = plan_ref[groups : groups + 1, :] * scaling
    misfit = misfit_ref[...]
    for z in range(steps):
        weight_grad = lax.dot_general(
            att_ref[z], misfit, (((0,), (0,)), ((), ())), preferred_element_type=f32
        )
        grad_ref[z * width : (z + 1) * width, :] = weight_grad * scale
    packed = plan_ref[:groups, :].astype(jnp.int32)
    for book in range(2):
        code = (packed & 255) if book == 0 else (packed >> 8)
        digit_ref[2 * book] = (code & (LOW - 1)).astype(f32)
        digit_ref[2 * book + 1] = (code >> 3).astype(f32)
    at = lax.broadcasted_iota(jnp.int32, (16, rows), 0)
    low_rows = [(2 * d + (at >= 8).astype(jnp.int32)).astype(f32).astype(bf16) for d in range(LOW // 2)]
    high_rows = [(16 * d + at).astype(f32).astype(bf16) for d in range(HIGH // 16)]
    zero, one = jnp.zeros((16, rows), bf16), jnp.ones((16, rows), bf16)
    chunk = 8

    def digit(which, g):
        return jnp.broadcast_to(digit_ref[which, pl.ds(g, 1), :], (16, rows)).astype(bf16)

    def step(i, totals):
        twice = []
        for k in range(chunk):
            entry = grad_ref[pl.ds(pl.multiple_of((i * chunk + k) * GROUP, GROUP), GROUP), :]
            twice.append(jnp.concatenate([entry, entry], axis=0).astype(bf16))
        done = []
        for book in range(2):
            highs, lows = [], []
            for k in range(chunk):
                low, high = digit(2 * book, i * chunk + k), digit(2 * book + 1, i * chunk + k)
                lows.append(
                    jnp.concatenate([jnp.where(low == r, twice[k], zero) for r in low_rows], axis=0)
                )
                highs.append(
                    jnp.concatenate([jnp.where(high == r, one, zero) for r in high_rows], axis=0)
                )
            part = lax.dot_general(
                jnp.concatenate(highs, axis=1),
                jnp.concatenate(lows, axis=1),
                (((1,), (1,)), ((), ())),
                preferred_element_type=f32,
            )
            done.append(totals[book] + part)
        return tuple(done)

    empty = jnp.zeros((HIGH, LOW * GROUP), f32)
    totals = lax.fori_loop(0, groups // chunk, step, (empty, empty), unroll=2)

    @pl.when(pl.program_id(0) == 0)
    def _():
        bins_ref[...] = jnp.zeros_like(bins_ref)

    for book in range(2):
        bins_ref[book] += totals[book]


def bin_gradients(place, attended, misfit, plan, scaling):
    steps, tokens, width = attended.shape
    blocks, depth, rows = plan.shape
    return pl.pallas_call(
        lambda *refs: bins_kernel(scaling, *refs),
        grid_spec=pltpu.PrefetchScalarGridSpec(
            num_scalar_prefetch=1,
            grid=(blocks,),
            in_specs=[
                pl.BlockSpec((steps, tokens, width), lambda i, place: (0, 0, 0)),
                pl.BlockSpec((tokens, rows), lambda i, place: (0, (place[0] + i) % blocks)),
                pl.BlockSpec((None, depth, rows), lambda i, place: (i, 0, 0)),
            ],
            out_specs=pl.BlockSpec((2, HIGH, LOW * GROUP), lambda i, place: (0, 0, 0)),
            scratch_shapes=[
                pltpu.VMEM((steps * width, rows), f32),
                pltpu.VMEM((4, depth - 8, rows), f32),
            ],
        ),
        out_shape=jax.ShapeDtypeStruct((2, HIGH, LOW * GROUP), f32),
        cost_estimate=pl.CostEstimate(
            flops=blocks * 8_000_000_000, transcendentals=0, bytes_accessed=blocks * 2_000_000
        ),
        name="bins",
    )(place, attended, misfit, plan)


def attend(queries, keys, values, query_places, key_places):
    scores = jnp.einsum("qd,kd->qk", queries, keys, preferred_element_type=f32) / math.sqrt(HEAD_DIM)
    allowed = key_places[None, :] <= query_places[:, None]
    row_max = jnp.max(jnp.where(allowed, scores, -1e30), axis=-1, keepdims=True)
    exponent = jnp.where(allowed, jnp.exp(scores - row_max), 0.0)
    row_sum = jnp.sum(exponent, axis=-1, keepdims=True)
    weighted = jnp.einsum("qk,kd->qd", exponent.astype(bf16), values, preferred_element_type=f32)
    return (weighted / row_sum).astype(bf16)


def device_part(
    queries, key_rows, values, code_first, code_second, book_first, book_second, scales, target
):
    tok_rows, _ = queries.shape
    high, across = lax.axis_index("tok_0"), lax.axis_index("tok_1")
    count_across = lax.axis_size("tok_1")
    lane, core = lax.axis_index("col_0"), lax.axis_index("col_1")
    count_lane, count_col = lax.axis_size("col_0"), lax.axis_size(COL)
    rows = code_first.shape[0]
    tokens = lax.axis_size(TOK) * tok_rows

    def of_head(head):
        picked = [
            lax.dynamic_slice_in_dim(array, head * HEAD_DIM, HEAD_DIM, 1)
            for array in (queries, key_rows, values)
        ]
        return jnp.concatenate(picked, axis=1)

    mine = of_head(high)
    both = jnp.concatenate(in_order(mine, swap(of_head(1 - high), "tok_0"), high))
    pairs = copies(both[:, HEAD_DIM:], "tok_1")
    block = lax.iota(jnp.int32, 2)[:, None] * (count_across * tok_rows)
    block = block + lax.iota(jnp.int32, tok_rows)[None, :]
    query_places = (block + across * tok_rows).reshape(-1)
    key_places = lax.iota(jnp.int32, count_across)[:, None, None] * tok_rows + block[None]
    pairs = pairs.reshape(tokens, 2 * HEAD_DIM)
    head_out = attend(
        both[:, :HEAD_DIM], pairs[:, :HEAD_DIM], pairs[:, HEAD_DIM:], query_places, key_places.reshape(-1)
    )
    other_out = swap(head_out, "tok_0")
    attended = copies(jnp.concatenate(in_order(head_out, other_out, high), axis=1), "row")

    own_codes = (code_first + ENTRIES * code_second).T.astype(f32)
    groups = own_codes.shape[0]
    share = tok_rows // count_lane
    wanted = target.reshape(2, count_across, count_lane, share, rows)
    wanted = lax.dynamic_index_in_dim(wanted, core, 0, keepdims=False)
    wanted = lax.dynamic_index_in_dim(wanted, lane, 1, keepdims=False).astype(f32)
    own_scales = jnp.broadcast_to(scales[None], (8, rows))

    def block_for(peer):
        part = lax.dynamic_index_in_dim(wanted, peer, 0, keepdims=False)
        return jnp.concatenate([own_codes, own_scales, part], axis=0)

    own_block = block_for(across)
    books = jnp.stack([book_first, book_second]).astype(f32).transpose(0, 2, 1)
    table = books.reshape(2, GROUP, 2, 128).transpose(0, 2, 1, 3).reshape(4, GROUP, 128)
    received = [own_block]
    built = dequantize(own_block, table, 0, count_across, groups)
    for k in range(1, count_across):
        sent, _ = lax.optimization_barrier((block_for((across + count_across - k) % count_across), pairs))
        route = [((i + k) % count_across, i) for i in range(count_across)]
        received.append(lax.ppermute(sent, "tok_1", route))
        built = dequantize(received[k], table, k, count_across, groups, built)
    weight, plan = built

    place = jnp.stack([across, core])
    keep, send = project(place, attended, weight)
    half_sum = (keep + swap(send, "col_1")).astype(bf16)
    parts = exchange(half_sum.reshape(count_lane, share, -1), "col_0")
    output = jnp.sum(parts.astype(f32), axis=0)
    wanted = jnp.stack([block[groups + 8 :] for block in received] * 2)
    wanted = lax.dynamic_slice_in_dim(wanted, (count_across - across) % count_across, count_across, 0)
    wanted = wanted.transpose(1, 0, 2).reshape(share, -1)
    misfit_share = (output - wanted).astype(bf16)
    misfit_half = copies(misfit_share, "col_0").reshape(tok_rows, -1)
    other_half = swap(misfit_half, "col_1")
    misfit = jnp.concatenate(in_order(misfit_half, other_half, core), axis=0)

    by_rows = misfit.reshape(2 * tok_rows, count_across, rows).transpose(1, 0, 2)
    by_tokens = exchange(by_rows, "tok_1").reshape(count_across, 2, tok_rows, rows)

    scale_part = jnp.sum(misfit_share.astype(f32) * output, axis=0).reshape(count_across, -1, 128)
    extra = scale_part.shape[1]
    bins = bin_gradients(place, attended, misfit, plan, 1.0 / tokens)

    bins = jnp.broadcast_to(bins.reshape(1, -1, 128), (count_across, 2 * ENTRIES * GROUP // 128, 128))
    sums = jnp.concatenate([bins, scale_part], axis=1)
    sums, by_tokens = lax.optimization_barrier((sums, by_tokens))
    sums = jnp.sum(exchange(sums, "tok_1"), axis=0)
    upper = sums.astype(bf16)
    lower = (sums[-extra:] - upper[-extra:].astype(f32)).astype(bf16)
    sums = copies(jnp.concatenate([upper, lower]), COL + ("tok_0",)).astype(f32)
    scale_sums = lax.dynamic_index_in_dim(sums.reshape(count_col, 2, -1, 128), high, 1, keepdims=False)
    scale_sums = jnp.sum(scale_sums[:, -2 * extra :], axis=0)
    scale_sums = (scale_sums[:extra] + scale_sums[extra:]).reshape(rows)
    bins = jnp.sum(sums[:, : -2 * extra], axis=0).astype(bf16)
    bins = jnp.sum(copies(bins, "row").astype(f32), axis=0)
    misfit_out = by_tokens.transpose(1, 0, 2, 3).reshape(tokens, rows)
    return misfit_out, scale_sums / (scales * tokens), bins.reshape(2, ENTRIES, GROUP)


def solution(mesh):
    split = Mesh(
        mesh.devices.reshape(4, 2, mesh.shape["row"], 2, 4),
        ("col_0", "col_1", "row", "tok_0", "tok_1"),
    )
    return jax.shard_map(
        device_part,
        mesh=split,
        in_specs=(
            P(TOK, COL_ROW),
            P(TOK, COL_ROW),
            P(TOK, COL_ROW),
            P(ROW_TOK, COL),
            P(ROW_TOK, COL),
            P(),
            P(),
            P(ROW_TOK),
            P(None, ROW_TOK),
        ),
        out_specs=(P(None, ROW_TOK), P(ROW_TOK), P()),
        check_vma=False,
    )
```

time: 225 us -> 220 us (0.978)
  blocking collectives: 31.5 us -> 18 us
  starting transfers between devices: 59.5 us -> 67.1 us
  local copies, waits for them, and re-layouts: 11.9 us -> 19.1 us
  between operations: 6.85 us -> 1.06 us
  Pallas kernels: 70.2 us -> 74.6 us
  waiting for transfers between devices: 34.3 us -> 30.4 us
    all_to_all x2, blocking collectives: 31.5 us -> 18 us  [exchange(): return lax.all_to_all(pieces, axis, 0, 0, tiled=True)]
    ppermute x0 -> x3, starting transfers between devices: none -> 7.79 us  [device_part(): received.append(lax.ppermute(sent, 'tok_1', route))]
    ppermute x4, waiting for transfers between devices: 8.8 us -> 1.28 us  [swap(): return lax.ppermute(array, axis, [(0, 1), (1, 0)])]
    unnamed x24 -> x23, local copies, waits for them, and re-layouts: 2.41 us -> 9.88 us
    pallas_call x3 -> x5, Pallas kernels: 64 us -> 68.7 us  [the longest x4 37.3 us: dequantize(): pl.pallas_call(dequant_kernel, grid=(1,), in_specs=[pl.BlockSpec(block.sh...]
    all_to_all x7 -> x6, waiting for transfers between devices: 25.5 us -> 29.1 us  [exchange(): return lax.all_to_all(pieces, axis, 0, 0, tiled=True)]
    all_to_all x7 -> x6, starting transfers between devices: 39.9 us -> 38.3 us  [exchange(): return lax.all_to_all(pieces, axis, 0, 0, tiled=True)]
  transfers between devices with their start and end apart: 11 -> 13, of which waited for: 8 -> 6; matrix products, arithmetic and copies ran while one was open for 5% -> 7% of each run, Pallas kernels for 29% -> 31%
where the time goes in v3:
time: 220 us; the launch traced here: 218 us
  Pallas kernels  74.6 us (34%)
  starting transfers between devices  67.1 us (30%)
  waiting for transfers between devices  30.4 us (14%)
  local copies, waits for them, and re-layouts  19.1 us (9%)
  blocking collectives  18 us (8%)
  other arithmetic  7 us (3%)
    all_to_all x6, starting transfers between devices, exchange(): return lax.all_to_all(pieces, axis, 0, 0, tiled=True)  38.3 us
    pallas_call x4, Pallas kernels, dequantize(): pl.pallas_call(dequant_kernel, grid=(1,), in_specs=[pl.BlockSpec(block.sh...  37.3 us
    pallas_call x1, Pallas kernels, bin_gradients(): pl.pallas_call(lambda *refs: bins_kernel(scaling, *refs), grid_spec=pltpu...  31.4 us
    all_to_all x6, waiting for transfers between devices, exchange(): return lax.all_to_all(pieces, axis, 0, 0, tiled=True)  29.1 us
    ppermute x4, starting transfers between devices, swap(): return lax.ppermute(array, axis, [(0, 1), (1, 0)])  21 us
    all_to_all x2, blocking collectives, exchange(): return lax.all_to_all(pieces, axis, 0, 0, tiled=True)  18 us
    unnamed x23, local copies, waits for them, and re-layouts  9.88 us
    ppermute x3, starting transfers between devices, device_part(): received.append(lax.ppermute(sent, 'tok_1', route))  7.79 us
  transfers between devices with their start and end apart: 13, of which 6 were waited for; matrix products, arithmetic and copies ran while one was open for 7% of the time, Pallas kernels for 31%

profile of v3, /device:TPU:1, one launch (start us, length us, event | category | flops | bytes accessed | tf_op | source)
XLA Modules:
  0.0 218.1 jit_solution(15398260234090509574)
XLA Ops:
  2.3 8.3 %collective-permute-start = (bf16[128,384]{1,0:T(8,128)(2,1)S(1)}, bf16[128,384]{1,0:T(8,128)(2,1)S(1)}, u32[]{:S(2)}, u32[]{:S(2)}) collective-permute-start(bf16[128,384]{1,0:T(8,128)(2,1)S(1)} %pad_maximum_fusion.9), channel_id=1, source_target_pairs={{0,4},{4,0},{1,5},{5,1},{2,6},{6,2},{3,7},{7,3},{8,12},{12,8},{9,1... | collective-permute-start | bytes 294920 | tf_op jit(solution)/shard_map/ppermute | solution.py:34
  16.6 9.3 %dequant.4 = (bf16[4,2048,256]{2,1,0:T(8,128)(2,1)}, f32[4,264,256]{2,1,0:T(8,128)}) custom-call(f32[296,256]{1,0:T(8,128)} %get-tuple-element.47.block_ref, f32[4,8,128]{2,1,0:T(8,128)} %bitcast.93), custom_call_target="tpu_custom_call" | custom-call | flops 8000000000 | bytes 1500000 | tf_op jit(solution)/shard_map/dequant/pallas_call | solution.py:77
  26.8 4.0 %all-to-all-start = ((bf16[4,256,256]{2,1,0:T(8,128)(2,1)}), bf16[4,256,256]{2,1,0:T(8,128)(2,1)S(1)}, u32[]{:S(2)}, u32[]{:S(2)}) async-start(bf16[4,256,256]{2,1,0:T(8,128)(2,1)} %broadcast_in_dim.23), calls=%async_computation | async-start | bytes 1048576 | tf_op jit(solution)/shard_map/all_to_all | solution.py:25
  31.0 7.9 %all-to-all-done = bf16[4,256,256]{2,1,0:T(8,128)(2,1)S(1)} async-done(((bf16[4,256,256]{2,1,0:T(8,128)(2,1)}), bf16[4,256,256]{2,1,0:T(8,128)(2,1)S(1)}, u32[]{:S(2)}, u32[]{:S(2)}) %all-to-all-start) | async-done | bytes 524320 | tf_op jit(solution)/shard_map/all_to_all | solution.py:25
  40.1 1.9 collective-permute-start.1
  42.6 2.8 %collective-permute-start.4 = (f32[296,256]{1,0:T(8,128)S(1)}, f32[296,256]{1,0:T(8,128)S(1)}, u32[]{:S(2)}, u32[]{:S(2)}) collective-permute-start(f32[296,256]{1,0:T(8,128)S(1)} %get-tuple-element.20), channel_id=1, source_target_pairs={{1,0},{2,1},{3,2},{0,3},{5,4},{6,5},{7,6},{4,7},{9,8},{10,9},{11,1... | collective-permute-start | bytes 909320 | tf_op jit(solution)/shard_map/ppermute | solution.py:286
  45.4 3.1 %collective-permute-start.3 = (f32[296,256]{1,0:T(8,128)S(1)}, f32[296,256]{1,0:T(8,128)S(1)}, u32[]{:S(2)}, u32[]{:S(2)}) collective-permute-start(f32[296,256]{1,0:T(8,128)S(1)} %get-tuple-element.19), channel_id=1, source_target_pairs={{2,0},{3,1},{0,2},{1,3},{6,4},{7,5},{4,6},{5,7},{10,8},{11,9},{8,1... | collective-permute-start | bytes 909320 | tf_op jit(solution)/shard_map/ppermute | solution.py:286
  51.7 10.2 %all-to-all-start.1 = ((bf16[8,256,256]{2,1,0:T(8,128)(2,1)}), bf16[8,256,256]{2,1,0:T(8,128)(2,1)S(1)}, u32[]{:S(2)}, u32[]{:S(2)}) async-start(bf16[8,256,256]{2,1,0:T(8,128)(2,1)} %broadcast_in_dim.26), calls=%async_computation.1 | async-start | bytes 2097152 | tf_op jit(solution)/shard_map/all_to_all | solution.py:25
  62.7 9.3 %dequant.5 = (bf16[4,2048,256]{2,1,0:T(8,128)(2,1)}, f32[4,264,256]{2,1,0:T(8,128)}) custom-call(f32[296,256]{1,0:T(8,128)} %copy-done.4, f32[4,8,128]{2,1,0:T(8,128)} %bitcast.94, bf16[4,2048,256]{2,1,0:T(8,128)(2,1)} %get-tuple-element.21.refs_0_, f32[4,264,256]{2,1,0:T(8,128)} %get-tuple-element.22.refs_1_), custom_call_target="tpu_custom_call", output_to_operand_aliasing={{0}: (2, {}), {1}: (3, {})} | custom-call | flops 8000000000 | bytes 1500000 | tf_op jit(solution)/shard_map/dequant/pallas_call | solution.py:77
  72.7 9.3 %dequant.6 = (bf16[4,2048,256]{2,1,0:T(8,128)(2,1)}, f32[4,264,256]{2,1,0:T(8,128)}) custom-call(f32[296,256]{1,0:T(8,128)} %copy-done.2, f32[4,8,128]{2,1,0:T(8,128)} %bitcast.95, bf16[4,2048,256]{2,1,0:T(8,128)(2,1)} %get-tuple-element.23.refs_0_, f32[4,264,256]{2,1,0:T(8,128)} %get-tuple-element.24.refs_1_), custom_call_target="tpu_custom_call", output_to_operand_aliasing={{0}: (2, {}), {1}: (3, {})} | custom-call | flops 8000000000 | bytes 1500000 | tf_op jit(solution)/shard_map/dequant/pallas_call | solution.py:77
  84.3 9.3 %dequant.7 = (bf16[4,2048,256]{2,1,0:T(8,128)(2,1)}, f32[4,264,256]{2,1,0:T(8,128)}) custom-call(f32[296,256]{1,0:T(8,128)} %copy-done.3, f32[4,8,128]{2,1,0:T(8,128)} %bitcast.96, bf16[4,2048,256]{2,1,0:T(8,128)(2,1)} %get-tuple-element.25.refs_0_, f32[4,264,256]{2,1,0:T(8,128)} %get-tuple-element.26.refs_1_), custom_call_target="tpu_custom_call", output_to_operand_aliasing={{0}: (2, {}), {1}: (3, {})} | custom-call | flops 8000000000 | bytes 1500000 | tf_op jit(solution)/shard_map/dequant/pallas_call | solution.py:77
  94.6 5.9 %project.1 = (f32[128,1024]{1,0:T(8,128)}, f32[128,1024]{1,0:T(8,128)}) custom-call(s32[2]{0:T(128)} %pad_add_fusion.place_ref.refs_0_, bf16[8,256,256]{2,1,0:T(8,128)(2,1)} %copy-done, bf16[4,2048,256]{2,1,0:T(8,128)(2,1)} %get-tuple-element.27.weight_ref), custom_call_target="tpu_custom_call" | custom-call | tf_op jit(solution)/shard_map/project/pallas_call | solution.py:120
  100.5 5.2 %collective-permute-start.5 = (f32[128,1024]{1,0:T(8,128)}, f32[128,1024]{1,0:T(8,128)S(1)}, u32[]{:S(2)}, u32[]{:S(2)}) collective-permute-start(f32[128,1024]{1,0:T(8,128)} %get-tuple-element.29), channel_id=1, source_target_pairs={{0,64},{64,0},{1,65},{65,1},{2,66},{66,2},{3,67},{67,3},{4,68},{68... | collective-permute-start | bytes 1572872 | tf_op jit(solution)/shard_map/ppermute | solution.py:34
  109.3 4.4 %all-to-all-start.2 = ((bf16[4,32,1024]{2,1,0:T(8,128)(2,1)}), bf16[4,32,1024]{2,1,0:T(8,128)(2,1)S(1)}, u32[]{:S(2)}, u32[]{:S(2)}) async-start(bf16[4,32,1024]{2,1,0:T(8,128)(2,1)} %bitcast.15), calls=%async_computation.2 | async-start | bytes 524288 | tf_op jit(solution)/shard_map/all_to_all | solution.py:25
  115.2 5.9 %all-to-all-done.2 = bf16[4,32,1024]{2,1,0:T(8,128)(2,1)S(1)} async-done(((bf16[4,32,1024]{2,1,0:T(8,128)(2,1)}), bf16[4,32,1024]{2,1,0:T(8,128)(2,1)S(1)}, u32[]{:S(2)}, u32[]{:S(2)}) %all-to-all-start.2) | async-done | bytes 262176 | tf_op jit(solution)/shard_map/all_to_all | solution.py:25
  121.2 9.4 %all_to_all.40 = bf16[4,32,1024]{2,1,0:T(8,128)(2,1)S(1)} all-to-all(bf16[4,32,1024]{2,1,0:T(8,128)(2,1)S(1)} %broadcast_in_dim.28), channel_id=1, replica_groups=mesh['col_0'=4,'col_1'=2,'row'=8,'tok_0'=2,'tok_1'=4] {'col_0'}, dimensions={0} | all-to-all | bytes 524288 | tf_op jit(solution)/shard_map/all_to_all | solution.py:25
  130.6 5.6 %collective-permute-start.6 = (bf16[128,1024]{1,0:T(8,128)(2,1)S(1)}, bf16[128,1024]{1,0:T(8,128)(2,1)S(1)}, u32[]{:S(2)}, u32[]{:S(2)}) collective-permute-start(bf16[128,1024]{1,0:T(8,128)(2,1)S(1)} %bitcast.84), channel_id=1, source_target_pairs={{0,64},{64,0},{1,65},{65,1},{2,66},{66,2},{3,67},{67,3},{4,68},{68... | collective-permute-start | bytes 786440 | tf_op jit(solution)/shard_map/ppermute | solution.py:34
  138.3 4.5 %all-to-all-start.4 = ((bf16[4,256,256]{2,1,0:T(8,128)(2,1)}), bf16[4,256,256]{2,1,0:T(8,128)(2,1)S(1)}, u32[]{:S(2)}, u32[]{:S(2)}) async-start(bf16[4,256,256]{2,1,0:T(8,128)(2,1)} %bitcast.78), calls=%async_computation.4 | async-start | bytes 1048576 | tf_op jit(solution)/shard_map/all_to_all | solution.py:25
  142.8 31.4 %bins.1 = f32[2,32,64]{2,1,0:T(8,128)} custom-call(s32[2]{0:T(128)} %pad_add_fusion.place_ref.refs_0_, bf16[8,256,256]{2,1,0:T(8,128)(2,1)} %copy-done, bf16[256,1024]{1,0:T(8,128)(2,1)} %copy-done.1, f32[4,264,256]{2,1,0:T(8,128)} %get-tuple-element.30.refs_3_), custom_call_target="tpu_custom_call" | custom-call | flops 32000000000 | bytes 8000000 | tf_op jit(solution)/shard_map/bins/pallas_call | solution.py:200
  175.1 8.6 %all_to_all.41 = f32[4,34,128]{2,1,0:T(8,128)S(1)} all-to-all(f32[4,34,128]{2,1,0:T(8,128)S(1)} %pad_maximum_fusion.10), channel_id=1, replica_groups=mesh['col_0'=4,'col_1'=2,'row'=8,'tok_0'=2,'tok_1'=4] {'tok_1'}, dimensions={0} | all-to-all | bytes 139264 | tf_op jit(solution)/shard_map/all_to_all | solution.py:25
  184.5 8.3 %all-to-all-start.6 = ((bf16[16,36,128]{2,1,0:T(8,128)(2,1)}), bf16[16,36,128]{2,1,0:T(8,128)(2,1)S(1)}, u32[]{:S(2)}, u32[]{:S(2)}) async-start(bf16[16,36,128]{2,1,0:T(8,128)(2,1)} %broadcast_in_dim.31), calls=%async_computation.6 | async-start | bytes 327680 | tf_op jit(solution)/shard_map/all_to_all | solution.py:25
  193.6 8.8 %all-to-all-done.6 = bf16[16,36,128]{2,1,0:T(8,128)(2,1)S(1)} async-done(((bf16[16,36,128]{2,1,0:T(8,128)(2,1)}), bf16[16,36,128]{2,1,0:T(8,128)(2,1)S(1)}, u32[]{:S(2)}, u32[]{:S(2)}) %all-to-all-start.6) | async-done | bytes 147488 | tf_op jit(solution)/shard_map/all_to_all | solution.py:25
  203.0 6.9 %all-to-all-start.7 = ((bf16[8,32,128]{2,1,0:T(8,128)(2,1)}), bf16[8,32,128]{2,1,0:T(8,128)(2,1)S(1)}, u32[]{:S(2)}, u32[]{:S(2)}) async-start(bf16[8,32,128]{2,1,0:T(8,128)(2,1)} %broadcast_in_dim.32), calls=%async_computation.7 | async-start | bytes 131072 | tf_op jit(solution)/shard_map/all_to_all | solution.py:25
  210.6 6.6 %all-to-all-done.7 = bf16[8,32,128]{2,1,0:T(8,128)(2,1)S(1)} async-done(((bf16[8,32,128]{2,1,0:T(8,128)(2,1)}), bf16[8,32,128]{2,1,0:T(8,128)(2,1)S(1)}, u32[]{:S(2)}, u32[]{:S(2)}) %all-to-all-start.7) | async-done | bytes 65568 | tf_op jit(solution)/shard_map/all_to_all | solution.py:25
  (88 shorter events, 30.1 us)
Async XLA Ops:
  2.3 23.6 %collective-permute-start = (bf16[128,384]{1,0:T(8,128)(2,1)S(1)}, bf16[128,384]{1,0:T(8,128)(2,1)S(1)}, u32[]{:S(2)}, u32[]{:S(2)}) collective-permute-start(bf16[128,384]{1,0:T(8,128)(2,1)S(1)} %pad_maximum_fusion.9), channel_id=1, source_target_pairs={{0,4},{4,0},{1,5},{5,1},{2,6},{6,2},{3,7},{7,3},{8,12},{12,8},{9,1... | collective-permute-start | bytes 294920 | tf_op jit(solution)/shard_map/ppermute | solution.py:34
  26.8 12.1 %all-to-all-start = ((bf16[4,256,256]{2,1,0:T(8,128)(2,1)}), bf16[4,256,256]{2,1,0:T(8,128)(2,1)S(1)}, u32[]{:S(2)}, u32[]{:S(2)}) async-start(bf16[4,256,256]{2,1,0:T(8,128)(2,1)} %broadcast_in_dim.23), calls=%async_computation | async-start | bytes 1048576 | tf_op jit(solution)/shard_map/all_to_all | solution.py:25
  40.1 10.4 %collective-permute-start.1 = (bf16[256,128]{0,1:T(8,128)(2,1)S(1)}, bf16[256,128]{0,1:T(8,128)(2,1)S(1)}, u32[]{:S(2)}, u32[]{:S(2)}) collective-permute-start(bf16[256,128]{0,1:T(8,128)(2,1)S(1)} %fusion), channel_id=1, source_target_pairs={{0,4},{4,0},{1,5},{5,1},{2,6},{6,2},{3,7},{7,3},{8,12},{12,8},{9,1... | collective-permute-start | bytes 196616 | tf_op jit(solution)/shard_map/ppermute | solution.py:34
  42.6 19.3 %collective-permute-start.4 = (f32[296,256]{1,0:T(8,128)S(1)}, f32[296,256]{1,0:T(8,128)S(1)}, u32[]{:S(2)}, u32[]{:S(2)}) collective-permute-start(f32[296,256]{1,0:T(8,128)S(1)} %get-tuple-element.20), channel_id=1, source_target_pairs={{1,0},{2,1},{3,2},{0,3},{5,4},{6,5},{7,6},{4,7},{9,8},{10,9},{11,1... | collective-permute-start | bytes 909320 | tf_op jit(solution)/shard_map/ppermute | solution.py:286
  45.4 26.6 %collective-permute-start.3 = (f32[296,256]{1,0:T(8,128)S(1)}, f32[296,256]{1,0:T(8,128)S(1)}, u32[]{:S(2)}, u32[]{:S(2)}) collective-permute-start(f32[296,256]{1,0:T(8,128)S(1)} %get-tuple-element.19), channel_id=1, source_target_pairs={{2,0},{3,1},{0,2},{1,3},{6,4},{7,5},{4,6},{5,7},{10,8},{11,9},{8,1... | collective-permute-start | bytes 909320 | tf_op jit(solution)/shard_map/ppermute | solution.py:286
  48.5 35.0 %collective-permute-start.2 = (f32[296,256]{1,0:T(8,128)S(1)}, f32[296,256]{1,0:T(8,128)S(1)}, u32[]{:S(2)}, u32[]{:S(2)}) collective-permute-start(f32[296,256]{1,0:T(8,128)S(1)} %get-tuple-element.18), channel_id=1, source_target_pairs={{3,0},{0,1},{1,2},{2,3},{7,4},{4,5},{5,6},{6,7},{11,8},{8,9},{9,10... | collective-permute-start | bytes 909320 | tf_op jit(solution)/shard_map/ppermute | solution.py:286
  51.7 41.9 %all-to-all-start.1 = ((bf16[8,256,256]{2,1,0:T(8,128)(2,1)}), bf16[8,256,256]{2,1,0:T(8,128)(2,1)S(1)}, u32[]{:S(2)}, u32[]{:S(2)}) async-start(bf16[8,256,256]{2,1,0:T(8,128)(2,1)} %broadcast_in_dim.26), calls=%async_computation.1 | async-start | bytes 2097152 | tf_op jit(solution)/shard_map/all_to_all | solution.py:25
  61.9 0.7 copy-start.4
  72.0 0.7 copy-start.2
  83.5 0.7 copy-start.3
  93.6 1.0 copy-start
  100.5 7.0 %collective-permute-start.5 = (f32[128,1024]{1,0:T(8,128)}, f32[128,1024]{1,0:T(8,128)S(1)}, u32[]{:S(2)}, u32[]{:S(2)}) collective-permute-start(f32[128,1024]{1,0:T(8,128)} %get-tuple-element.29), channel_id=1, source_target_pairs={{0,64},{64,0},{1,65},{65,1},{2,66},{66,2},{3,67},{67,3},{4,68},{68... | collective-permute-start | bytes 1572872 | tf_op jit(solution)/shard_map/ppermute | solution.py:34
  109.3 11.8 %all-to-all-start.2 = ((bf16[4,32,1024]{2,1,0:T(8,128)(2,1)}), bf16[4,32,1024]{2,1,0:T(8,128)(2,1)S(1)}, u32[]{:S(2)}, u32[]{:S(2)}) async-start(bf16[4,32,1024]{2,1,0:T(8,128)(2,1)} %bitcast.15), calls=%async_computation.2 | async-start | bytes 524288 | tf_op jit(solution)/shard_map/all_to_all | solution.py:25
  130.6 6.7 %collective-permute-start.6 = (bf16[128,1024]{1,0:T(8,128)(2,1)S(1)}, bf16[128,1024]{1,0:T(8,128)(2,1)S(1)}, u32[]{:S(2)}, u32[]{:S(2)}) collective-permute-start(bf16[128,1024]{1,0:T(8,128)(2,1)S(1)} %bitcast.84), channel_id=1, source_target_pairs={{0,64},{64,0},{1,65},{65,1},{2,66},{66,2},{3,67},{67,3},{4,68},{68... | collective-permute-start | bytes 786440 | tf_op jit(solution)/shard_map/ppermute | solution.py:34
  137.4 5.4 %copy-start.1 = (bf16[256,1024]{1,0:T(8,128)(2,1)}, bf16[256,1024]{1,0:T(8,128)(2,1)S(1)}, u32[]{:S(2)}) copy-start(bf16[256,1024]{1,0:T(8,128)(2,1)S(1)} %pad_maximum_fusion.refs_2_) | copy-start | bytes 1572868
  138.3 36.8 %all-to-all-start.4 = ((bf16[4,256,256]{2,1,0:T(8,128)(2,1)}), bf16[4,256,256]{2,1,0:T(8,128)(2,1)S(1)}, u32[]{:S(2)}, u32[]{:S(2)}) async-start(bf16[4,256,256]{2,1,0:T(8,128)(2,1)} %bitcast.78), calls=%async_computation.4 | async-start | bytes 1048576 | tf_op jit(solution)/shard_map/all_to_all | solution.py:25
  142.8 67.2 %copy-start.5 = (f32[256]{0:T(256)S(1)}, f32[256]{0:T(256)}, u32[]{:S(2)}) copy-start(f32[256]{0:T(256)} %param.16) | copy-start | bytes 3076
  184.5 17.8 %all-to-all-start.6 = ((bf16[16,36,128]{2,1,0:T(8,128)(2,1)}), bf16[16,36,128]{2,1,0:T(8,128)(2,1)S(1)}, u32[]{:S(2)}, u32[]{:S(2)}) async-start(bf16[16,36,128]{2,1,0:T(8,128)(2,1)} %broadcast_in_dim.31), calls=%async_computation.6 | async-start | bytes 327680 | tf_op jit(solution)/shard_map/all_to_all | solution.py:25
  203.0 14.2 %all-to-all-start.7 = ((bf16[8,32,128]{2,1,0:T(8,128)(2,1)}), bf16[8,32,128]{2,1,0:T(8,128)(2,1)S(1)}, u32[]{:S(2)}, u32[]{:S(2)}) async-start(bf16[8,32,128]{2,1,0:T(8,128)(2,1)} %broadcast_in_dim.32), calls=%async_computation.7 | async-start | bytes 131072 | tf_op jit(solution)/shard_map/all_to_all | solution.py:25

commit v4 on v3

--- a/solution.py
+++ b/solution.py
@@ -39,47 +39,84 @@
     return jnp.where(first, mine, theirs), jnp.where(first, theirs, mine)
 
 
-def dequant_kernel(block_ref, table_ref, *refs):
-    weight_ref, plan_ref = refs[-2:]
+def dequant_kernel(block_ref, first_ref, second_ref, *refs):
+    weight_ref, plan_ref, digit_ref = refs[-3:]
     groups, rows = weight_ref.shape[0] // GROUP, weight_ref.shape[1]
-    tables = [table_ref[i] for i in range(4)]
+    tables, by_digit = [], []
+    lanes = lax.broadcasted_iota(jnp.int32, (GROUP, 128), 1)
+    for book_ref in (first_ref, second_ref):
+        halves = [book_ref[:, start : start + 128].astype(f32) for start in (0, 128)]
+        tables += halves
+        digit_rows = []
+        for d in range(LOW):
+            place = (lanes * LOW + d) & 127
+            near, far = (
+                jnp.take_along_axis(half, place, axis=1, mode="promise_in_bounds") for half in halves
+            )
+            digit_rows.append(jnp.where(lanes < 128 // LOW, near, far))
+        by_digit.append(jnp.concatenate(digit_rows, axis=0)[:, :HIGH].astype(bf16))
     plan_ref[...] = block_ref[: groups + 8, :]
     scale = jnp.broadcast_to(block_ref[groups : groups + 1, :], (GROUP, rows))
-
-    def group_rows(g):
+    packed = block_ref[:groups, :].astype(jnp.int32)
+    for book in range(2):
+        code = (packed & 255) if book == 0 else (packed >> 8)
+        digit_ref[2 * book] = (code & (LOW - 1)).astype(f32)
+        digit_ref[2 * book + 1] = (code >> 3).astype(f32)
+    at = lax.broadcasted_iota(jnp.int32, (16, rows), 0)
+    high_rows = [(16 * d + at).astype(f32).astype(bf16) for d in range(HIGH // 16)]
+    zero, one = jnp.zeros((16, rows), bf16), jnp.ones((16, rows), bf16)
+
+    def picked(book, half, place):
+        return jnp.take_along_axis(tables[2 * book + half], place, axis=1, mode="promise_in_bounds")
+
+    def by_gather(g):
         both = jnp.broadcast_to(block_ref[pl.ds(g, 1), :], (GROUP, rows)).astype(jnp.int32)
         parts = []
-        for at in range(0, rows, 128):
-            packed = both[:, at : at + 128]
+        for start in range(0, rows, 128):
+            packed = both[:, start : start + 128]
             total = None
             for book in range(2):
                 code = (packed & 255) if book == 0 else (packed >> 8)
                 place = code & 127
-                near = jnp.take_along_axis(tables[2 * book], place, axis=1)
-                far = jnp.take_along_axis(tables[2 * book + 1], place, axis=1)
-                entry = jnp.where(code >= 128, far, near)
+                entry = jnp.where(code >= 128, picked(book, 1, place), picked(book, 0, place))
                 total = entry if total is None else total + entry
-            parts.append(total * scale[:, at : at + 128])
+            parts.append(total * scale[:, start : start + 128])
         return jnp.concatenate(parts, axis=1)
 
+    def by_product(g):
+        total = None
+        for book in range(2):
+            high = jnp.broadcast_to(digit_ref[2 * book + 1, pl.ds(g, 1), :], (16, rows)).astype(bf16)
+            hot = jnp.concatenate([jnp.where(high == r, one, zero) for r in high_rows], axis=0)
+            near = jnp.dot(by_digit[book], hot, preferred_element_type=f32)
+            low = jnp.broadcast_to(digit_ref[2 * book, pl.ds(g, 1), :], (GROUP, rows))
+            entry = near[:GROUP]
+            for d in range(1, LOW):
+                entry = jnp.where(low == float(d), near[d * GROUP : (d + 1) * GROUP], entry)
+            total = entry if total is None else total + entry
+        return total * scale
+
+    chunk = 16
+
     def step(i, carry):
-        for k in range(4):
-            pair = [group_rows(i * 8 + 2 * k + n) for n in range(2)]
-            start = pl.multiple_of(i * 64 + 16 * k, 16)
-            weight_ref[pl.ds(start, 16), :] = jnp.concatenate(pair, axis=0).astype(bf16)
+        for k in range(0, chunk, 2):
+            g = i * chunk + k
+            pair = jnp.concatenate([by_gather(g), by_product(g + 1)], axis=0)
+            weight_ref[pl.ds(pl.multiple_of(g * GROUP, 16), 16), :] = pair.astype(bf16)
         return carry
 
-    lax.fori_loop(0, groups // 8, step, 0)
-
-
-def dequantize(block, table, at, blocks, groups, before=()):
+    lax.fori_loop(0, groups // chunk, step, 0, unroll=2)
+
+
+def dequantize(block, books, at, blocks, groups, before=()):
     rows = block.shape[1]
     return pl.pallas_call(
         dequant_kernel,
         grid=(1,),
         in_specs=[
             pl.BlockSpec(block.shape, lambda i: (0, 0)),
-            pl.BlockSpec((4, GROUP, 128), lambda i: (0, 0, 0)),
+            pl.BlockSpec(books[0].shape, lambda i: (0, 0)),
+            pl.BlockSpec(books[1].shape, lambda i: (0, 0)),
         ]
         + [pl.BlockSpec(memory_space=pl.ANY)] * len(before),
         out_specs=[
@@ -90,12 +127,13 @@
             jax.ShapeDtypeStruct((blocks, groups * GROUP, rows), bf16),
             jax.ShapeDtypeStruct((blocks, groups + 8, rows), f32),
         ],
-        input_output_aliases={2: 0, 3: 1} if before else {},
+        scratch_shapes=[pltpu.VMEM((4, groups, rows), f32)],
+        input_output_aliases={3: 0, 4: 1} if before else {},
         cost_estimate=pl.CostEstimate(
             flops=8_000_000_000, transcendentals=0, bytes_accessed=1_500_000
         ),
         name="dequant",
-    )(block, table, *before)
+    )(block, *books, *before)
 
 
 def project_kernel(place_ref, att_ref, weight_ref, keep_ref, send_ref, all_ref):
@@ -276,15 +314,14 @@
         return jnp.concatenate([own_codes, own_scales, part], axis=0)
 
     own_block = block_for(across)
-    books = jnp.stack([book_first, book_second]).astype(f32).transpose(0, 2, 1)
-    table = books.reshape(2, GROUP, 2, 128).transpose(0, 2, 1, 3).reshape(4, GROUP, 128)
+    books = (book_first.T, book_second.T)
     received = [own_block]
-    built = dequantize(own_block, table, 0, count_across, groups)
+    built = dequantize(own_block, books, 0, count_across, groups)
     for k in range(1, count_across):
         sent, _ = lax.optimization_barrier((block_for((across + count_across - k) % count_across), pairs))
         route = [((i + k) % count_across, i) for i in range(count_across)]
         received.append(lax.ppermute(sent, "tok_1", route))
-        built = dequantize(received[k], table, k, count_across, groups, built)
+        built = dequantize(received[k], books, k, count_across, groups, built)
     weight, plan = built
 
     place = jnp.stack([across, core])
@@ -300,8 +337,16 @@
     other_half = swap(misfit_half, "col_1")
     misfit = jnp.concatenate(in_order(misfit_half, other_half, core), axis=0)
 
-    by_rows = misfit.reshape(2 * tok_rows, count_across, rows).transpose(1, 0, 2)
-    by_tokens = exchange(by_rows, "tok_1").reshape(count_across, 2, tok_rows, rows)
+    def misfit_for(peer):
+        return lax.dynamic_slice_in_dim(misfit, peer * rows, rows, 1).reshape(2, 1, tok_rows, rows)
+
+    def into(result, piece, peer):
+        return lax.dynamic_update_slice_in_dim(result, piece, peer, 1)
+
+    out_pieces = [misfit_for(across)]
+    for k in range(1, count_across):
+        route = [(i, (i + k) % count_across) for i in range(count_across)]
+        out_pieces.append(lax.ppermute(misfit_for((across + k) % count_across), "tok_1", route))
 
     scale_part = jnp.sum(misfit_share.astype(f32) * output, axis=0).reshape(count_across, -1, 128)
     extra = scale_part.shape[1]
@@ -309,7 +354,6 @@
 
     bins = jnp.broadcast_to(bins.reshape(1, -1, 128), (count_across, 2 * ENTRIES * GROUP // 128, 128))
     sums = jnp.concatenate([bins, scale_part], axis=1)
-    sums, by_tokens = lax.optimization_barrier((sums, by_tokens))
     sums = jnp.sum(exchange(sums, "tok_1"), axis=0)
     upper = sums.astype(bf16)
     lower = (sums[-extra:] - upper[-extra:].astype(f32)).astype(bf16)
@@ -318,9 +362,12 @@
     scale_sums = jnp.sum(scale_sums[:, -2 * extra :], axis=0)
     scale_sums = (scale_sums[:extra] + scale_sums[extra:]).reshape(rows)
     bins = jnp.sum(sums[:, : -2 * extra], axis=0).astype(bf16)
+    out_pieces, bins = lax.optimization_barrier((out_pieces, bins))
+    misfit_out = jnp.zeros((2, count_across, tok_rows, rows), bf16)
+    for k in range(count_across):
+        misfit_out = into(misfit_out, out_pieces[k], (across + count_across - k) % count_across)
     bins = jnp.sum(copies(bins, "row").astype(f32), axis=0)
-    misfit_out = by_tokens.transpose(1, 0, 2, 3).reshape(tokens, rows)
-    return misfit_out, scale_sums / (scales * tokens), bins.reshape(2, ENTRIES, GROUP)
+    return misfit_out.reshape(tokens, rows), scale_sums / (scales * tokens), bins.reshape(2, ENTRIES, GROUP)
 
 
 def solution(mesh):

time: 220 us -> 205 us (0.932)
  the two profiles are of different devices: /device:TPU:1 before, /device:TPU:8 now
where the time goes in v4:
time: 205 us; the launch traced here: 203 us
  starting transfers between devices  62.2 us (30%)
  Pallas kernels  60.1 us (29%)
  waiting for transfers between devices  34.1 us (17%)
  blocking collectives  20.9 us (10%)
  local copies, waits for them, and re-layouts  17.5 us (9%)
  other arithmetic  6.56 us (3%)
    pallas_call x1, Pallas kernels, bin_gradients(): pl.pallas_call(lambda *refs: bins_kernel(scaling, *refs), grid_spec=pltpu...  31.4 us
    all_to_all x5, starting transfers between devices, exchange(): return lax.all_to_all(pieces, axis, 0, 0, tiled=True)  31 us
    all_to_all x5, waiting for transfers between devices, exchange(): return lax.all_to_all(pieces, axis, 0, 0, tiled=True)  27.6 us
    pallas_call x4, Pallas kernels, dequantize(): pl.pallas_call(dequant_kernel, grid=(1,), in_specs=[pl.BlockSpec(block.sh...  22.8 us
    all_to_all x2, blocking collectives, exchange(): return lax.all_to_all(pieces, axis, 0, 0, tiled=True)  20.9 us
    ppermute x4, starting transfers between devices, swap(): return lax.ppermute(array, axis, [(0, 1), (1, 0)])  13.6 us
    unnamed x24, local copies, waits for them, and re-layouts  9.9 us
    ppermute x3, starting transfers between devices, device_part(): lax.ppermute(misfit_for((across + k) % count_across), 'tok_1', route)  9.31 us
  transfers between devices with their start and end apart: 15, of which 8 were waited for; matrix products, arithmetic and copies ran while one was open for 6% of the time, Pallas kernels for 11%

profile of v4, /device:TPU:8, one launch (start us, length us, event | category | flops | bytes accessed | tf_op | source)
XLA Modules:
  0.0 203.3 jit_solution(13044076013392913197)
XLA Ops:
  2.3 6.8 %collective-permute-start = (bf16[128,384]{1,0:T(8,128)(2,1)S(1)}, bf16[128,384]{1,0:T(8,128)(2,1)S(1)}, u32[]{:S(2)}, u32[]{:S(2)}) collective-permute-start(bf16[128,384]{1,0:T(8,128)(2,1)S(1)} %pad_maximum_fusion.9), channel_id=1, source_target_pairs={{0,4},{4,0},{1,5},{5,1},{2,6},{6,2},{3,7},{7,3},{8,12},{12,8},{9,1... | collective-permute-start | bytes 294920 | tf_op jit(solution)/shard_map/ppermute | solution.py:34
  13.9 5.7 %dequant.4 = (bf16[4,2048,256]{2,1,0:T(8,128)(2,1)}, f32[4,264,256]{2,1,0:T(8,128)}) custom-call(f32[296,256]{1,0:T(8,128)} %get-tuple-element.54.block_ref, bf16[8,256]{1,0:T(8,128)(2,1)} %bitcast.88, bf16[8,256]{1,0:T(8,128)(2,1)} %bitcast.92), custom_call_target="tpu_custom_call" | custom-call | flops 8000000000 | bytes 1500000 | tf_op jit(solution)/shard_map/dequant/pallas_call | solution.py:113
  20.4 4.3 %all-to-all-start = ((bf16[4,256,256]{2,1,0:T(8,128)(2,1)}), bf16[4,256,256]{2,1,0:T(8,128)(2,1)S(1)}, u32[]{:S(2)}, u32[]{:S(2)}) async-start(bf16[4,256,256]{2,1,0:T(8,128)(2,1)} %broadcast_in_dim.26), calls=%async_computation | async-start | bytes 1048576 | tf_op jit(solution)/shard_map/all_to_all | solution.py:25
  24.9 9.0 %all-to-all-done = bf16[4,256,256]{2,1,0:T(8,128)(2,1)S(1)} async-done(((bf16[4,256,256]{2,1,0:T(8,128)(2,1)}), bf16[4,256,256]{2,1,0:T(8,128)(2,1)S(1)}, u32[]{:S(2)}, u32[]{:S(2)}) %all-to-all-start) | async-done | bytes 524320 | tf_op jit(solution)/shard_map/all_to_all | solution.py:25
  35.2 2.9 %collective-permute-start.1 = (bf16[256,128]{0,1:T(8,128)(2,1)S(1)}, bf16[256,128]{0,1:T(8,128)(2,1)S(1)}, u32[]{:S(2)}, u32[]{:S(2)}) collective-permute-start(bf16[256,128]{0,1:T(8,128)(2,1)S(1)} %fusion), channel_id=1, source_target_pairs={{0,4},{4,0},{1,5},{5,1},{2,6},{6,2},{3,7},{7,3},{8,12},{12,8},{9,1... | collective-permute-start | bytes 196616 | tf_op jit(solution)/shard_map/ppermute | solution.py:34
  38.7 3.1 %collective-permute-start.4 = (f32[296,256]{1,0:T(8,128)S(1)}, f32[296,256]{1,0:T(8,128)S(1)}, u32[]{:S(2)}, u32[]{:S(2)}) collective-permute-start(f32[296,256]{1,0:T(8,128)S(1)} %get-tuple-element.23), channel_id=1, source_target_pairs={{1,0},{2,1},{3,2},{0,3},{5,4},{6,5},{7,6},{4,7},{9,8},{10,9},{11,1... | collective-permute-start | bytes 909320 | tf_op jit(solution)/shard_map/ppermute | solution.py:323
  41.8 3.4 %collective-permute-start.3 = (f32[296,256]{1,0:T(8,128)S(1)}, f32[296,256]{1,0:T(8,128)S(1)}, u32[]{:S(2)}, u32[]{:S(2)}) collective-permute-start(f32[296,256]{1,0:T(8,128)S(1)} %get-tuple-element.22), channel_id=1, source_target_pairs={{2,0},{3,1},{0,2},{1,3},{6,4},{7,5},{4,6},{5,7},{10,8},{11,9},{8,1... | collective-permute-start | bytes 909320 | tf_op jit(solution)/shard_map/ppermute | solution.py:323
  48.4 10.3 %all-to-all-start.1 = ((bf16[8,256,256]{2,1,0:T(8,128)(2,1)}), bf16[8,256,256]{2,1,0:T(8,128)(2,1)S(1)}, u32[]{:S(2)}, u32[]{:S(2)}) async-start(bf16[8,256,256]{2,1,0:T(8,128)(2,1)} %broadcast_in_dim.29), calls=%async_computation.1 | async-start | bytes 2097152 | tf_op jit(solution)/shard_map/all_to_all | solution.py:25
  59.4 5.7 %dequant.5 = (bf16[4,2048,256]{2,1,0:T(8,128)(2,1)}, f32[4,264,256]{2,1,0:T(8,128)}) custom-call(f32[296,256]{1,0:T(8,128)} %copy-done.4, bf16[8,256]{1,0:T(8,128)(2,1)} %bitcast.89, bf16[8,256]{1,0:T(8,128)(2,1)} %bitcast.93, bf16[4,2048,256]{2,1,0:T(8,128)(2,1)} %get-tuple-element.24.refs_0_, ...), custom_call_target="tpu_custom_call", output_to_operand_aliasing={{0}: (3, {}), {1}: (4, {})} | custom-call | flops 8000000000 | bytes 1500000 | tf_op jit(solution)/shard_map/dequant/pallas_call | solution.py:113
  65.9 5.7 %dequant.6 = (bf16[4,2048,256]{2,1,0:T(8,128)(2,1)}, f32[4,264,256]{2,1,0:T(8,128)}) custom-call(f32[296,256]{1,0:T(8,128)} %copy-done.2, bf16[8,256]{1,0:T(8,128)(2,1)} %bitcast.90, bf16[8,256]{1,0:T(8,128)(2,1)} %bitcast.94, bf16[4,2048,256]{2,1,0:T(8,128)(2,1)} %get-tuple-element.26.refs_0_, ...), custom_call_target="tpu_custom_call", output_to_operand_aliasing={{0}: (3, {}), {1}: (4, {})} | custom-call | flops 8000000000 | bytes 1500000 | tf_op jit(solution)/shard_map/dequant/pallas_call | solution.py:113
  73.8 5.7 %dequant.7 = (bf16[4,2048,256]{2,1,0:T(8,128)(2,1)}, f32[4,264,256]{2,1,0:T(8,128)}) custom-call(f32[296,256]{1,0:T(8,128)} %copy-done.3, bf16[8,256]{1,0:T(8,128)(2,1)} %bitcast.91, bf16[8,256]{1,0:T(8,128)(2,1)} %bitcast.95, bf16[4,2048,256]{2,1,0:T(8,128)(2,1)} %get-tuple-element.28.refs_0_, ...), custom_call_target="tpu_custom_call", output_to_operand_aliasing={{0}: (3, {}), {1}: (4, {})} | custom-call | flops 8000000000 | bytes 1500000 | tf_op jit(solution)/shard_map/dequant/pallas_call | solution.py:113
  79.5 5.4 %all-to-all-done.1.att_ref.refs_1_ = bf16[8,256,256]{2,1,0:T(8,128)(2,1)S(1)} async-done(((bf16[8,256,256]{2,1,0:T(8,128)(2,1)}), bf16[8,256,256]{2,1,0:T(8,128)(2,1)S(1)}, u32[]{:S(2)}, u32[]{:S(2)}) %all-to-all-start.1) | async-done | bytes 1048608 | tf_op jit(solution)/shard_map/all_to_all | solution.py:25
  85.9 5.9 %project.1 = (f32[128,1024]{1,0:T(8,128)}, f32[128,1024]{1,0:T(8,128)}) custom-call(s32[2]{0:T(128)} %pad_add_fusion.place_ref.refs_0_, bf16[8,256,256]{2,1,0:T(8,128)(2,1)} %copy-done, bf16[4,2048,256]{2,1,0:T(8,128)(2,1)} %get-tuple-element.30.weight_ref), custom_call_target="tpu_custom_call" | custom-call | tf_op jit(solution)/shard_map/project/pallas_call | solution.py:158
  97.6 5.3 %all-to-all-start.2 = ((bf16[4,32,1024]{2,1,0:T(8,128)(2,1)}), bf16[4,32,1024]{2,1,0:T(8,128)(2,1)S(1)}, u32[]{:S(2)}, u32[]{:S(2)}) async-start(bf16[4,32,1024]{2,1,0:T(8,128)(2,1)} %bitcast.13), calls=%async_computation.2 | async-start | bytes 524288 | tf_op jit(solution)/shard_map/all_to_all | solution.py:25
  104.5 5.7 %all-to-all-done.2 = bf16[4,32,1024]{2,1,0:T(8,128)(2,1)S(1)} async-done(((bf16[4,32,1024]{2,1,0:T(8,128)(2,1)}), bf16[4,32,1024]{2,1,0:T(8,128)(2,1)S(1)}, u32[]{:S(2)}, u32[]{:S(2)}) %all-to-all-start.2) | async-done | bytes 262176 | tf_op jit(solution)/shard_map/all_to_all | solution.py:25
  110.2 10.8 %all_to_all.35 = bf16[4,32,1024]{2,1,0:T(8,128)(2,1)S(1)} all-to-all(bf16[4,32,1024]{2,1,0:T(8,128)(2,1)S(1)} %broadcast_in_dim.31), channel_id=1, replica_groups=mesh['col_0'=4,'col_1'=2,'row'=8,'tok_0'=2,'tok_1'=4] {'col_0'}, dimensions={0} | all-to-all | bytes 524288 | tf_op jit(solution)/shard_map/all_to_all | solution.py:25
  125.4 31.4 %bins.1 = f32[2,32,64]{2,1,0:T(8,128)} custom-call(s32[2]{0:T(128)} %pad_add_fusion.place_ref.refs_0_, bf16[8,256,256]{2,1,0:T(8,128)(2,1)} %copy-done, bf16[256,1024]{1,0:T(8,128)(2,1)} %pad_maximum_fusion.refs_2_, f32[4,264,256]{2,1,0:T(8,128)} %get-tuple-element.33.refs_3_), custom_call_target="tpu_custom_call" | custom-call | flops 32000000000 | bytes 8000000 | tf_op jit(solution)/shard_map/bins/pallas_call | solution.py:238
  157.6 10.0 %all_to_all.36 = f32[4,34,128]{2,1,0:T(8,128)S(1)} all-to-all(f32[4,34,128]{2,1,0:T(8,128)S(1)} %pad_maximum_fusion.10), channel_id=1, replica_groups=mesh['col_0'=4,'col_1'=2,'row'=8,'tok_0'=2,'tok_1'=4] {'tok_1'}, dimensions={0} | all-to-all | bytes 139264 | tf_op jit(solution)/shard_map/all_to_all | solution.py:25
  168.4 7.7 %all-to-all-start.5 = ((bf16[16,36,128]{2,1,0:T(8,128)(2,1)}), bf16[16,36,128]{2,1,0:T(8,128)(2,1)S(1)}, u32[]{:S(2)}, u32[]{:S(2)}) async-start(bf16[16,36,128]{2,1,0:T(8,128)(2,1)} %broadcast_in_dim.34), calls=%async_computation.5 | async-start | bytes 327680 | tf_op jit(solution)/shard_map/all_to_all | solution.py:25
  178.7 4.0 %collective-permute-start.8 = (bf16[2,1,128,256]{3,2,1,0:T(8,128)(2,1)S(1)}, bf16[2,1,128,256]{3,2,1,0:T(8,128)(2,1)S(1)}, u32[]{:S(2)}, u32[]{:S(2)}) collective-permute-start(bf16[2,1,128,256]{3,2,1,0:T(8,128)(2,1)S(1)} %bitcast.82), channel_id=1, source_target_pairs={{0,2},{1,3},{2,0},{3,1},{4,6},{5,7},{6,4},{7,5},{8,10},{9,11},{10,... | collective-permute-start | bytes 393224 | tf_op jit(solution)/shard_map/ppermute | solution.py:349
  182.7 2.9 %collective-permute-start.9 = (bf16[2,1,128,256]{3,2,1,0:T(8,128)(2,1)S(1)}, bf16[2,1,128,256]{3,2,1,0:T(8,128)(2,1)S(1)}, u32[]{:S(2)}, u32[]{:S(2)}) collective-permute-start(bf16[2,1,128,256]{3,2,1,0:T(8,128)(2,1)S(1)} %bitcast.81), channel_id=1, source_target_pairs={{0,3},{1,0},{2,1},{3,2},{4,7},{5,4},{6,5},{7,6},{8,11},{9,8},{10,9... | collective-permute-start | bytes 393224 | tf_op jit(solution)/shard_map/ppermute | solution.py:349
  187.6 2.5 %collective-permute-done.9 = bf16[2,1,128,256]{3,2,1,0:T(8,128)(2,1)S(1)} collective-permute-done((bf16[2,1,128,256]{3,2,1,0:T(8,128)(2,1)S(1)}, bf16[2,1,128,256]{3,2,1,0:T(8,128)(2,1)S(1)}, u32[]{:S(2)}, u32[]{:S(2)}) %collective-permute-start.9) | collective-permute-done | bytes 131104 | tf_op jit(solution)/shard_map/ppermute | solution.py:349
  190.8 3.3 %all-to-all-start.6 = ((bf16[8,32,128]{2,1,0:T(8,128)(2,1)}), bf16[8,32,128]{2,1,0:T(8,128)(2,1)S(1)}, u32[]{:S(2)}, u32[]{:S(2)}) async-start(bf16[8,32,128]{2,1,0:T(8,128)(2,1)} %broadcast_in_dim.35), calls=%async_computation.6 | async-start | bytes 131072 | tf_op jit(solution)/shard_map/all_to_all | solution.py:25
  194.9 7.5 %all-to-all-done.6 = bf16[8,32,128]{2,1,0:T(8,128)(2,1)S(1)} async-done(((bf16[8,32,128]{2,1,0:T(8,128)(2,1)}), bf16[8,32,128]{2,1,0:T(8,128)(2,1)S(1)}, u32[]{:S(2)}, u32[]{:S(2)}) %all-to-all-start.6) | async-done | bytes 65568 | tf_op jit(solution)/shard_map/all_to_all | solution.py:25
  (93 shorter events, 37.1 us)
Async XLA Ops:
  2.3 17.3 %collective-permute-start = (bf16[128,384]{1,0:T(8,128)(2,1)S(1)}, bf16[128,384]{1,0:T(8,128)(2,1)S(1)}, u32[]{:S(2)}, u32[]{:S(2)}) collective-permute-start(bf16[128,384]{1,0:T(8,128)(2,1)S(1)} %pad_maximum_fusion.9), channel_id=1, source_target_pairs={{0,4},{4,0},{1,5},{5,1},{2,6},{6,2},{3,7},{7,3},{8,12},{12,8},{9,1... | collective-permute-start | bytes 294920 | tf_op jit(solution)/shard_map/ppermute | solution.py:34
  20.4 13.5 %all-to-all-start = ((bf16[4,256,256]{2,1,0:T(8,128)(2,1)}), bf16[4,256,256]{2,1,0:T(8,128)(2,1)S(1)}, u32[]{:S(2)}, u32[]{:S(2)}) async-start(bf16[4,256,256]{2,1,0:T(8,128)(2,1)} %broadcast_in_dim.26), calls=%async_computation | async-start | bytes 1048576 | tf_op jit(solution)/shard_map/all_to_all | solution.py:25
  35.2 12.0 %collective-permute-start.1 = (bf16[256,128]{0,1:T(8,128)(2,1)S(1)}, bf16[256,128]{0,1:T(8,128)(2,1)S(1)}, u32[]{:S(2)}, u32[]{:S(2)}) collective-permute-start(bf16[256,128]{0,1:T(8,128)(2,1)S(1)} %fusion), channel_id=1, source_target_pairs={{0,4},{4,0},{1,5},{5,1},{2,6},{6,2},{3,7},{7,3},{8,12},{12,8},{9,1... | collective-permute-start | bytes 196616 | tf_op jit(solution)/shard_map/ppermute | solution.py:34
  38.7 19.9 %collective-permute-start.4 = (f32[296,256]{1,0:T(8,128)S(1)}, f32[296,256]{1,0:T(8,128)S(1)}, u32[]{:S(2)}, u32[]{:S(2)}) collective-permute-start(f32[296,256]{1,0:T(8,128)S(1)} %get-tuple-element.23), channel_id=1, source_target_pairs={{1,0},{2,1},{3,2},{0,3},{5,4},{6,5},{7,6},{4,7},{9,8},{10,9},{11,1... | collective-permute-start | bytes 909320 | tf_op jit(solution)/shard_map/ppermute | solution.py:323
  41.8 23.4 %collective-permute-start.3 = (f32[296,256]{1,0:T(8,128)S(1)}, f32[296,256]{1,0:T(8,128)S(1)}, u32[]{:S(2)}, u32[]{:S(2)}) collective-permute-start(f32[296,256]{1,0:T(8,128)S(1)} %get-tuple-element.22), channel_id=1, source_target_pairs={{2,0},{3,1},{0,2},{1,3},{6,4},{7,5},{4,6},{5,7},{10,8},{11,9},{8,1... | collective-permute-start | bytes 909320 | tf_op jit(solution)/shard_map/ppermute | solution.py:323
  45.2 27.9 %collective-permute-start.2 = (f32[296,256]{1,0:T(8,128)S(1)}, f32[296,256]{1,0:T(8,128)S(1)}, u32[]{:S(2)}, u32[]{:S(2)}) collective-permute-start(f32[296,256]{1,0:T(8,128)S(1)} %get-tuple-element.21), channel_id=1, source_target_pairs={{3,0},{0,1},{1,2},{2,3},{7,4},{4,5},{5,6},{6,7},{11,8},{8,9},{9,10... | collective-permute-start | bytes 909320 | tf_op jit(solution)/shard_map/ppermute | solution.py:323
  48.4 36.6 %all-to-all-start.1 = ((bf16[8,256,256]{2,1,0:T(8,128)(2,1)}), bf16[8,256,256]{2,1,0:T(8,128)(2,1)S(1)}, u32[]{:S(2)}, u32[]{:S(2)}) async-start(bf16[8,256,256]{2,1,0:T(8,128)(2,1)} %broadcast_in_dim.29), calls=%async_computation.1 | async-start | bytes 2097152 | tf_op jit(solution)/shard_map/all_to_all | solution.py:25
  58.7 0.7 copy-start.4
  65.2 0.7 copy-start.2
  73.1 0.7 copy-start.3
  84.9 1.0 copy-start
  91.8 4.0 %collective-permute-start.5 = (f32[128,1024]{1,0:T(8,128)}, f32[128,1024]{1,0:T(8,128)S(1)}, u32[]{:S(2)}, u32[]{:S(2)}) collective-permute-start(f32[128,1024]{1,0:T(8,128)} %get-tuple-element.32), channel_id=1, source_target_pairs={{0,64},{64,0},{1,65},{65,1},{2,66},{66,2},{3,67},{67,3},{4,68},{68... | collective-permute-start | bytes 1572872 | tf_op jit(solution)/shard_map/ppermute | solution.py:34
  97.6 12.5 %all-to-all-start.2 = ((bf16[4,32,1024]{2,1,0:T(8,128)(2,1)}), bf16[4,32,1024]{2,1,0:T(8,128)(2,1)S(1)}, u32[]{:S(2)}, u32[]{:S(2)}) async-start(bf16[4,32,1024]{2,1,0:T(8,128)(2,1)} %bitcast.13), calls=%async_computation.2 | async-start | bytes 524288 | tf_op jit(solution)/shard_map/all_to_all | solution.py:25
  121.1 3.4 %collective-permute-start.6 = (bf16[128,1024]{1,0:T(8,128)(2,1)S(1)}, bf16[128,1024]{1,0:T(8,128)(2,1)S(1)}, u32[]{:S(2)}, u32[]{:S(2)}) collective-permute-start(bf16[128,1024]{1,0:T(8,128)(2,1)S(1)} %bitcast.74), channel_id=1, source_target_pairs={{0,64},{64,0},{1,65},{65,1},{2,66},{66,2},{3,67},{67,3},{4,68},{68... | collective-permute-start | bytes 786440 | tf_op jit(solution)/shard_map/ppermute | solution.py:34
  125.4 68.8 %copy-start.5 = (f32[256]{0:T(256)S(1)}, f32[256]{0:T(256)}, u32[]{:S(2)}) copy-start(f32[256]{0:T(256)} %param.16) | copy-start | bytes 3076
  168.4 17.1 %all-to-all-start.5 = ((bf16[16,36,128]{2,1,0:T(8,128)(2,1)}), bf16[16,36,128]{2,1,0:T(8,128)(2,1)S(1)}, u32[]{:S(2)}, u32[]{:S(2)}) async-start(bf16[16,36,128]{2,1,0:T(8,128)(2,1)} %broadcast_in_dim.34), calls=%async_computation.5 | async-start | bytes 327680 | tf_op jit(solution)/shard_map/all_to_all | solution.py:25
  176.2 11.4 %collective-permute-start.7 = (bf16[2,1,128,256]{3,2,1,0:T(8,128)(2,1)S(1)}, bf16[2,1,128,256]{3,2,1,0:T(8,128)(2,1)S(1)}, u32[]{:S(2)}, u32[]{:S(2)}) collective-permute-start(bf16[2,1,128,256]{3,2,1,0:T(8,128)(2,1)S(1)} %bitcast.83), channel_id=1, source_target_pairs={{0,1},{1,2},{2,3},{3,0},{4,5},{5,6},{6,7},{7,4},{8,9},{9,10},{10,1... | collective-permute-start | bytes 393224 | tf_op jit(solution)/shard_map/ppermute | solution.py:349
  178.7 9.0 %collective-permute-start.8 = (bf16[2,1,128,256]{3,2,1,0:T(8,128)(2,1)S(1)}, bf16[2,1,128,256]{3,2,1,0:T(8,128)(2,1)S(1)}, u32[]{:S(2)}, u32[]{:S(2)}) collective-permute-start(bf16[2,1,128,256]{3,2,1,0:T(8,128)(2,1)S(1)} %bitcast.82), channel_id=1, source_target_pairs={{0,2},{1,3},{2,0},{3,1},{4,6},{5,7},{6,4},{7,5},{8,10},{9,11},{10,... | collective-permute-start | bytes 393224 | tf_op jit(solution)/shard_map/ppermute | solution.py:349
  182.7 7.5 %collective-permute-start.9 = (bf16[2,1,128,256]{3,2,1,0:T(8,128)(2,1)S(1)}, bf16[2,1,128,256]{3,2,1,0:T(8,128)(2,1)S(1)}, u32[]{:S(2)}, u32[]{:S(2)}) collective-permute-start(bf16[2,1,128,256]{3,2,1,0:T(8,128)(2,1)S(1)} %bitcast.81), channel_id=1, source_target_pairs={{0,3},{1,0},{2,1},{3,2},{4,7},{5,4},{6,5},{7,6},{8,11},{9,8},{10,9... | collective-permute-start | bytes 393224 | tf_op jit(solution)/shard_map/ppermute | solution.py:349
  190.8 11.7 %all-to-all-start.6 = ((bf16[8,32,128]{2,1,0:T(8,128)(2,1)}), bf16[8,32,128]{2,1,0:T(8,128)(2,1)S(1)}, u32[]{:S(2)}, u32[]{:S(2)}) async-start(bf16[8,32,128]{2,1,0:T(8,128)(2,1)} %broadcast_in_dim.35), calls=%async_computation.6 | async-start | bytes 131072 | tf_op jit(solution)/shard_map/all_to_all | solution.py:25
  194.9 8.4 %copy-start.1 = (bf16[2,4,128,256]{3,2,1,0:T(8,128)(2,1)}, bf16[2,4,128,256]{3,2,1,0:T(8,128)(2,1)S(1)}, u32[]{:S(2)}) copy-start(bf16[2,4,128,256]{3,2,1,0:T(8,128)(2,1)S(1)} %constant_dynamic-update-slice_fusion) | copy-start | bytes 1572868

commit v5 on v4

--- a/solution.py
+++ b/solution.py
@@ -28,6 +28,11 @@
 def copies(array, axis):
     pieces = jnp.broadcast_to(array[None], (lax.axis_size(axis), *array.shape))
     return exchange(pieces, axis)
+
+
+def in_two(array, axis):
+    upper = array.astype(bf16)
+    return jnp.concatenate([upper, (array - upper.astype(f32)).astype(bf16)], axis=axis)
 
 
 def swap(array, axis):
@@ -55,7 +60,7 @@
             )
             digit_rows.append(jnp.where(lanes < 128 // LOW, near, far))
         by_digit.append(jnp.concatenate(digit_rows, axis=0)[:, :HIGH].astype(bf16))
-    plan_ref[...] = block_ref[: groups + 8, :]
+    plan_ref[...] = block_ref[...]
     scale = jnp.broadcast_to(block_ref[groups : groups + 1, :], (GROUP, rows))
     packed = block_ref[:groups, :].astype(jnp.int32)
     for book in range(2):
@@ -121,11 +126,11 @@
         + [pl.BlockSpec(memory_space=pl.ANY)] * len(before),
         out_specs=[
             pl.BlockSpec((None, groups * GROUP, rows), lambda i: (at, 0, 0)),
-            pl.BlockSpec((None, groups + 8, rows), lambda i: (at, 0, 0)),
+            pl.BlockSpec((None, *block.shape), lambda i: (at, 0, 0)),
         ],
         out_shape=[
             jax.ShapeDtypeStruct((blocks, groups * GROUP, rows), bf16),
-            jax.ShapeDtypeStruct((blocks, groups + 8, rows), f32),
+            jax.ShapeDtypeStruct((blocks, *block.shape), f32),
         ],
         scratch_shapes=[pltpu.VMEM((4, groups, rows), f32)],
         input_output_aliases={3: 0, 4: 1} if before else {},
@@ -136,7 +141,7 @@
     )(block, *books, *before)
 
 
-def project_kernel(place_ref, att_ref, weight_ref, keep_ref, send_ref, all_ref):
+def project_kernel(core_ref, att_ref, weight_ref, keep_ref, send_ref, all_ref):
     steps, tokens, width = att_ref.shape
     half = tokens // 2
     total = None
@@ -146,33 +151,33 @@
         )
         total = part if total is None else total + part
     all_ref[...] = total
-    keep_ref[...] = all_ref[pl.ds(pl.multiple_of(place_ref[1] * half, half), half), :]
-    send_ref[...] = all_ref[pl.ds(pl.multiple_of((1 - place_ref[1]) * half, half), half), :]
-
-
-def project(place, attended, weight):
+    keep_ref[...] = all_ref[pl.ds(pl.multiple_of(core_ref[0] * half, half), half), :]
+    send_ref[...] = all_ref[pl.ds(pl.multiple_of((1 - core_ref[0]) * half, half), half), :]
+
+
+def project(core, attended, weight):
     steps, tokens, width = attended.shape
     blocks, depth, rows = weight.shape
     out = jax.ShapeDtypeStruct((tokens // 2, blocks * rows), f32)
-    out_spec = pl.BlockSpec((tokens // 2, rows), lambda i, place: (0, (place[0] + i) % blocks))
+    out_spec = pl.BlockSpec((tokens // 2, rows), lambda i, core: (0, i))
     return pl.pallas_call(
         project_kernel,
         grid_spec=pltpu.PrefetchScalarGridSpec(
             num_scalar_prefetch=1,
             grid=(blocks,),
             in_specs=[
-                pl.BlockSpec((steps, tokens, width), lambda i, place: (0, 0, 0)),
-                pl.BlockSpec((None, depth, rows), lambda i, place: (i, 0, 0)),
+                pl.BlockSpec((steps, tokens, width), lambda i, core: (0, 0, 0)),
+                pl.BlockSpec((None, depth, rows), lambda i, core: (i, 0, 0)),
             ],
             out_specs=[out_spec, out_spec],
             scratch_shapes=[pltpu.VMEM((tokens, rows), f32)],
         ),
         out_shape=[out, out],
         name="project",
-    )(place, attended, weight)
-
-
-def bins_kernel(scaling, place_ref, att_ref, misfit_ref, plan_ref, bins_ref, grad_ref, digit_ref):
+    )(core, attended, weight)
+
+
+def bins_kernel(scaling, att_ref, misfit_ref, plan_ref, bins_ref, grad_ref, digit_ref):
     groups, rows = digit_ref.shape[1:]
     steps, _, width = att_ref.shape
     scale = plan_ref[groups : groups + 1, :] * scaling
@@ -232,31 +237,28 @@
         bins_ref[book] += totals[book]
 
 
-def bin_gradients(place, attended, misfit, plan, scaling):
+def bin_gradients(attended, misfit, plan, groups, scaling):
     steps, tokens, width = attended.shape
     blocks, depth, rows = plan.shape
     return pl.pallas_call(
         lambda *refs: bins_kernel(scaling, *refs),
-        grid_spec=pltpu.PrefetchScalarGridSpec(
-            num_scalar_prefetch=1,
-            grid=(blocks,),
-            in_specs=[
-                pl.BlockSpec((steps, tokens, width), lambda i, place: (0, 0, 0)),
-                pl.BlockSpec((tokens, rows), lambda i, place: (0, (place[0] + i) % blocks)),
-                pl.BlockSpec((None, depth, rows), lambda i, place: (i, 0, 0)),
-            ],
-            out_specs=pl.BlockSpec((2, HIGH, LOW * GROUP), lambda i, place: (0, 0, 0)),
-            scratch_shapes=[
-                pltpu.VMEM((steps * width, rows), f32),
-                pltpu.VMEM((4, depth - 8, rows), f32),
-            ],
-        ),
+        grid=(blocks,),
+        in_specs=[
+            pl.BlockSpec((steps, tokens, width), lambda i: (0, 0, 0)),
+            pl.BlockSpec((tokens, rows), lambda i: (0, i)),
+            pl.BlockSpec((None, depth, rows), lambda i: (i, 0, 0)),
+        ],
+        out_specs=pl.BlockSpec((2, HIGH, LOW * GROUP), lambda i: (0, 0, 0)),
         out_shape=jax.ShapeDtypeStruct((2, HIGH, LOW * GROUP), f32),
+        scratch_shapes=[
+            pltpu.VMEM((steps * width, rows), f32),
+            pltpu.VMEM((4, groups, rows), f32),
+        ],
         cost_estimate=pl.CostEstimate(
             flops=blocks * 8_000_000_000, transcendentals=0, bytes_accessed=blocks * 2_000_000
         ),
         name="bins",
-    )(place, attended, misfit, plan)
+    )(attended, misfit, plan)
 
 
 def attend(queries, keys, values, query_places, key_places):
@@ -324,50 +326,51 @@
         built = dequantize(received[k], books, k, count_across, groups, built)
     weight, plan = built
 
-    place = jnp.stack([across, core])
-    keep, send = project(place, attended, weight)
+    keep, send = project(core[None], attended, weight)
     half_sum = (keep + swap(send, "col_1")).astype(bf16)
     parts = exchange(half_sum.reshape(count_lane, share, -1), "col_0")
     output = jnp.sum(parts.astype(f32), axis=0)
-    wanted = jnp.stack([block[groups + 8 :] for block in received] * 2)
-    wanted = lax.dynamic_slice_in_dim(wanted, (count_across - across) % count_across, count_across, 0)
-    wanted = wanted.transpose(1, 0, 2).reshape(share, -1)
-    misfit_share = (output - wanted).astype(bf16)
+    misfit_share = (output - plan[:, groups + 8 :].transpose(1, 0, 2).reshape(share, -1)).astype(bf16)
     misfit_half = copies(misfit_share, "col_0").reshape(tok_rows, -1)
     other_half = swap(misfit_half, "col_1")
     misfit = jnp.concatenate(in_order(misfit_half, other_half, core), axis=0)
 
-    def misfit_for(peer):
-        return lax.dynamic_slice_in_dim(misfit, peer * rows, rows, 1).reshape(2, 1, tok_rows, rows)
-
-    def into(result, piece, peer):
-        return lax.dynamic_update_slice_in_dim(result, piece, peer, 1)
-
-    out_pieces = [misfit_for(across)]
-    for k in range(1, count_across):
+    out_pieces = []
+    for k in range(count_across):
+        piece = misfit[:, k * rows : (k + 1) * rows].reshape(2, 1, tok_rows, rows)
         route = [(i, (i + k) % count_across) for i in range(count_across)]
-        out_pieces.append(lax.ppermute(misfit_for((across + k) % count_across), "tok_1", route))
+        out_pieces.append(lax.ppermute(piece, "tok_1", route) if k else piece)
 
     scale_part = jnp.sum(misfit_share.astype(f32) * output, axis=0).reshape(count_across, -1, 128)
     extra = scale_part.shape[1]
-    bins = bin_gradients(place, attended, misfit, plan, 1.0 / tokens)
-
-    bins = jnp.broadcast_to(bins.reshape(1, -1, 128), (count_across, 2 * ENTRIES * GROUP // 128, 128))
-    sums = jnp.concatenate([bins, scale_part], axis=1)
-    sums = jnp.sum(exchange(sums, "tok_1"), axis=0)
-    upper = sums.astype(bf16)
-    lower = (sums[-extra:] - upper[-extra:].astype(f32)).astype(bf16)
-    sums = copies(jnp.concatenate([upper, lower]), COL + ("tok_0",)).astype(f32)
-    scale_sums = lax.dynamic_index_in_dim(sums.reshape(count_col, 2, -1, 128), high, 1, keepdims=False)
-    scale_sums = jnp.sum(scale_sums[:, -2 * extra :], axis=0)
-    scale_sums = (scale_sums[:extra] + scale_sums[extra:]).reshape(rows)
-    bins = jnp.sum(sums[:, : -2 * extra], axis=0).astype(bf16)
-    out_pieces, bins = lax.optimization_barrier((out_pieces, bins))
+    scale_part = jnp.concatenate([scale_part, scale_part], axis=0)
+    start = (count_across - across) % count_across
+    scale_part = in_two(lax.dynamic_slice_in_dim(scale_part, start, count_across, 0), 1)
+    bins = bin_gradients(attended, misfit, plan, groups, 1.0 / tokens)
+
+    count_row = lax.axis_size("row")
+    bins = bins.reshape(-1, 128).astype(bf16)
+    bins = jnp.broadcast_to(bins[None, None], (count_row, count_across, *bins.shape))
+    scale_part = jnp.broadcast_to(scale_part[None], (count_row, *scale_part.shape))
+    sums = jnp.concatenate([bins, scale_part], axis=2).reshape(count_row * count_across, -1, 128)
+    sums = exchange(sums, ("row", "tok_1"))
+    own_row = sums.reshape(count_row, count_across, -1, 128)[:, :, -2 * extra :]
+    own_row = lax.dynamic_index_in_dim(own_row, lax.axis_index("row"), 0, keepdims=False)
+    own_row = jnp.sum(own_row.astype(f32), axis=0)
+    scale_part = in_two(own_row[:extra] + own_row[extra:], 0)
+    bins = jnp.sum(sums[:, : -2 * extra].astype(f32), axis=0).astype(bf16)
+    sums = copies(jnp.concatenate([bins, scale_part]), COL + ("tok_0",))
+    scale_part = sums.reshape(count_col, 2, -1, 128)[:, :, -2 * extra :]
+    scale_part = lax.dynamic_index_in_dim(scale_part, high, 1, keepdims=False)
+    scale_part = jnp.sum(scale_part.astype(f32), axis=0)
+    grad_scales = (scale_part[:extra] + scale_part[extra:]).reshape(rows) / (scales * tokens)
+    grad_books = jnp.sum(sums[:, : -2 * extra].astype(f32), axis=0).reshape(2, ENTRIES, GROUP)
+
     misfit_out = jnp.zeros((2, count_across, tok_rows, rows), bf16)
     for k in range(count_across):
-        misfit_out = into(misfit_out, out_pieces[k], (across + count_across - k) % count_across)
-    bins = jnp.sum(copies(bins, "row").astype(f32), axis=0)
-    return misfit_out.reshape(tokens, rows), scale_sums / (scales * tokens), bins.reshape(2, ENTRIES, GROUP)
+        peer = (across + count_across - k) % count_across
+        misfit_out = lax.dynamic_update_slice_in_dim(misfit_out, out_pieces[k], peer, 1)
+    return misfit_out.reshape(tokens, rows), grad_scales, grad_books
 
 
 def solution(mesh):

time: 205 us -> 199 us (0.971)
  the two profiles are of different devices: /device:TPU:8 before, /device:TPU:1 now
where the time goes in v5:
time: 199 us; the launch traced here: 198 us
  starting transfers between devices  80.2 us (40%)
  Pallas kernels  58.6 us (29%)
  waiting for transfers between devices  37.4 us (19%)
  local copies, waits for them, and re-layouts  11.5 us (6%)
  other arithmetic  8.33 us (4%)
    all_to_all x6, waiting for transfers between devices, exchange(): return lax.all_to_all(pieces, axis, 0, 0, tiled=True)  35.6 us
    all_to_all x6, starting transfers between devices, exchange(): return lax.all_to_all(pieces, axis, 0, 0, tiled=True)  32.5 us
    pallas_call x1, Pallas kernels, bin_gradients(): pl.pallas_call(lambda *refs: bins_kernel(scaling, *refs), grid=(blocks,),...  30.7 us
    ppermute x4, starting transfers between devices, swap(): return lax.ppermute(array, axis, [(0, 1), (1, 0)])  29.4 us
    pallas_call x4, Pallas kernels, dequantize(): pl.pallas_call(dequant_kernel, grid=(1,), in_specs=[pl.BlockSpec(block.sh...  22.8 us
    ppermute x3, starting transfers between devices, device_part(): out_pieces.append(lax.ppermute(piece, 'tok_1', route) if k else piece)  10.5 us
    ppermute x3, starting transfers between devices, device_part(): received.append(lax.ppermute(sent, 'tok_1', route))  7.8 us
    unnamed x18, local copies, waits for them, and re-layouts  5.98 us
  transfers between devices with their start and end apart: 16, of which 8 were waited for; matrix products, arithmetic and copies ran while one was open for 4% of the time, Pallas kernels for 12%

profile of v5, /device:TPU:1, one launch (start us, length us, event | category | flops | bytes accessed | tf_op | source)
XLA Modules:
  0.0 198.1 jit_solution(10315055531499737683)
XLA Ops:
  2.3 8.3 %collective-permute-start = (bf16[128,384]{1,0:T(8,128)(2,1)S(1)}, bf16[128,384]{1,0:T(8,128)(2,1)S(1)}, u32[]{:S(2)}, u32[]{:S(2)}) collective-permute-start(bf16[128,384]{1,0:T(8,128)(2,1)S(1)} %pad_maximum_fusion.10), channel_id=1, source_target_pairs={{0,4},{4,0},{1,5},{5,1},{2,6},{6,2},{3,7},{7,3},{8,12},{12,8},{9,1... | collective-permute-start | bytes 294920 | tf_op jit(solution)/shard_map/ppermute | solution.py:39
  13.8 4.0 %all-to-all-start = ((bf16[4,256,256]{2,1,0:T(8,128)(2,1)}), bf16[4,256,256]{2,1,0:T(8,128)(2,1)S(1)}, u32[]{:S(2)}, u32[]{:S(2)}) async-start(bf16[4,256,256]{2,1,0:T(8,128)(2,1)} %broadcast_in_dim.27), calls=%async_computation | async-start | bytes 1048576 | tf_op jit(solution)/shard_map/all_to_all | solution.py:25
  18.8 6.0 %all-to-all-done = bf16[4,256,256]{2,1,0:T(8,128)(2,1)S(1)} async-done(((bf16[4,256,256]{2,1,0:T(8,128)(2,1)}), bf16[4,256,256]{2,1,0:T(8,128)(2,1)S(1)}, u32[]{:S(2)}, u32[]{:S(2)}) %all-to-all-start) | async-done | bytes 524320 | tf_op jit(solution)/shard_map/all_to_all | solution.py:25
  26.0 9.0 %collective-permute-start.1 = (bf16[256,128]{0,1:T(8,128)(2,1)S(1)}, bf16[256,128]{0,1:T(8,128)(2,1)S(1)}, u32[]{:S(2)}, u32[]{:S(2)}) collective-permute-start(bf16[256,128]{0,1:T(8,128)(2,1)S(1)} %fusion), channel_id=1, source_target_pairs={{0,4},{4,0},{1,5},{5,1},{2,6},{6,2},{3,7},{7,3},{8,12},{12,8},{9,1... | collective-permute-start | bytes 196616 | tf_op jit(solution)/shard_map/ppermute | solution.py:39
  35.1 5.7 %dequant.4 = (bf16[4,2048,256]{2,1,0:T(8,128)(2,1)}, f32[4,296,256]{2,1,0:T(8,128)}) custom-call(f32[296,256]{1,0:T(8,128)} %get-tuple-element.45.block_ref, bf16[8,256]{1,0:T(8,128)(2,1)} %bitcast.73, bf16[8,256]{1,0:T(8,128)(2,1)} %bitcast.77), custom_call_target="tpu_custom_call" | custom-call | flops 8000000000 | bytes 1500000 | tf_op jit(solution)/shard_map/dequant/pallas_call | solution.py:118
  49.8 8.0 %all-to-all-start.1 = ((bf16[8,256,256]{2,1,0:T(8,128)(2,1)}), bf16[8,256,256]{2,1,0:T(8,128)(2,1)S(1)}, u32[]{:S(2)}, u32[]{:S(2)}) async-start(bf16[8,256,256]{2,1,0:T(8,128)(2,1)} %broadcast_in_dim.30), calls=%async_computation.1 | async-start | bytes 2097152 | tf_op jit(solution)/shard_map/all_to_all | solution.py:25
  58.5 5.7 %dequant.5 = (bf16[4,2048,256]{2,1,0:T(8,128)(2,1)}, f32[4,296,256]{2,1,0:T(8,128)}) custom-call(f32[296,256]{1,0:T(8,128)} %copy-done.6, bf16[8,256]{1,0:T(8,128)(2,1)} %bitcast.74, bf16[8,256]{1,0:T(8,128)(2,1)} %bitcast.78, bf16[4,2048,256]{2,1,0:T(8,128)(2,1)} %get-tuple-element.19.refs_0_, ...), custom_call_target="tpu_custom_call", output_to_operand_aliasing={{0}: (3, {}), {1}: (4, {})} | custom-call | flops 8000000000 | bytes 1500000 | tf_op jit(solution)/shard_map/dequant/pallas_call | solution.py:118
  64.9 5.7 %dequant.6 = (bf16[4,2048,256]{2,1,0:T(8,128)(2,1)}, f32[4,296,256]{2,1,0:T(8,128)}) custom-call(f32[296,256]{1,0:T(8,128)} %copy-done.5, bf16[8,256]{1,0:T(8,128)(2,1)} %bitcast.75, bf16[8,256]{1,0:T(8,128)(2,1)} %bitcast.79, bf16[4,2048,256]{2,1,0:T(8,128)(2,1)} %get-tuple-element.21.refs_0_, ...), custom_call_target="tpu_custom_call", output_to_operand_aliasing={{0}: (3, {}), {1}: (4, {})} | custom-call | flops 8000000000 | bytes 1500000 | tf_op jit(solution)/shard_map/dequant/pallas_call | solution.py:118
  71.3 5.7 %dequant.7 = (bf16[4,2048,256]{2,1,0:T(8,128)(2,1)}, f32[4,296,256]{2,1,0:T(8,128)}) custom-call(f32[296,256]{1,0:T(8,128)} %copy-done.4, bf16[8,256]{1,0:T(8,128)(2,1)} %bitcast.76, bf16[8,256]{1,0:T(8,128)(2,1)} %bitcast.80, bf16[4,2048,256]{2,1,0:T(8,128)(2,1)} %get-tuple-element.23.refs_0_, ...), custom_call_target="tpu_custom_call", output_to_operand_aliasing={{0}: (3, {}), {1}: (4, {})} | custom-call | flops 8000000000 | bytes 1500000 | tf_op jit(solution)/shard_map/dequant/pallas_call | solution.py:118
  77.1 5.9 %all-to-all-done.1.att_ref.refs_0_ = bf16[8,256,256]{2,1,0:T(8,128)(2,1)S(1)} async-done(((bf16[8,256,256]{2,1,0:T(8,128)(2,1)}), bf16[8,256,256]{2,1,0:T(8,128)(2,1)S(1)}, u32[]{:S(2)}, u32[]{:S(2)}) %all-to-all-start.1) | async-done | bytes 1048608 | tf_op jit(solution)/shard_map/all_to_all | solution.py:25
  83.9 5.1 %project.1 = (f32[128,1024]{1,0:T(8,128)}, f32[128,1024]{1,0:T(8,128)}) custom-call(s32[1]{0:T(128)} %bitcast.core_ref, bf16[8,256,256]{2,1,0:T(8,128)(2,1)} %copy-done, bf16[4,2048,256]{2,1,0:T(8,128)(2,1)} %get-tuple-element.25.weight_ref), custom_call_target="tpu_custom_call" | custom-call | tf_op jit(solution)/shard_map/project/pallas_call | solution.py:163
  89.1 6.5 %collective-permute-start.5 = (f32[128,1024]{1,0:T(8,128)}, f32[128,1024]{1,0:T(8,128)S(1)}, u32[]{:S(2)}, u32[]{:S(2)}) collective-permute-start(f32[128,1024]{1,0:T(8,128)} %get-tuple-element.27), channel_id=1, source_target_pairs={{0,64},{64,0},{1,65},{65,1},{2,66},{66,2},{3,67},{67,3},{4,68},{68... | collective-permute-start | bytes 1572872 | tf_op jit(solution)/shard_map/ppermute | solution.py:39
  99.1 6.2 %all-to-all-start.2 = ((bf16[4,32,1024]{2,1,0:T(8,128)(2,1)}), bf16[4,32,1024]{2,1,0:T(8,128)(2,1)S(1)}, u32[]{:S(2)}, u32[]{:S(2)}) async-start(bf16[4,32,1024]{2,1,0:T(8,128)(2,1)} %bitcast.12), calls=%async_computation.2 | async-start | bytes 524288 | tf_op jit(solution)/shard_map/all_to_all | solution.py:25
  106.3 6.5 %all-to-all-done.2 = bf16[4,32,1024]{2,1,0:T(8,128)(2,1)S(1)} async-done(((bf16[4,32,1024]{2,1,0:T(8,128)(2,1)}), bf16[4,32,1024]{2,1,0:T(8,128)(2,1)S(1)}, u32[]{:S(2)}, u32[]{:S(2)}) %all-to-all-start.2) | async-done | bytes 262176 | tf_op jit(solution)/shard_map/all_to_all | solution.py:25
  113.5 3.4 %all-to-all-start.3 = ((bf16[4,32,1024]{2,1,0:T(8,128)(2,1)}), bf16[4,32,1024]{2,1,0:T(8,128)(2,1)S(1)}, u32[]{:S(2)}, u32[]{:S(2)}) async-start(bf16[4,32,1024]{2,1,0:T(8,128)(2,1)} %broadcast_in_dim.32), calls=%async_computation.3 | async-start | bytes 524288 | tf_op jit(solution)/shard_map/all_to_all | solution.py:25
  117.0 5.6 %all-to-all-done.3 = bf16[4,32,1024]{2,1,0:T(8,128)(2,1)S(1)} async-done(((bf16[4,32,1024]{2,1,0:T(8,128)(2,1)}), bf16[4,32,1024]{2,1,0:T(8,128)(2,1)S(1)}, u32[]{:S(2)}, u32[]{:S(2)}) %all-to-all-start.3) | async-done | bytes 262176 | tf_op jit(solution)/shard_map/all_to_all | solution.py:25
  122.6 5.6 %collective-permute-start.6 = (bf16[128,1024]{1,0:T(8,128)(2,1)S(1)}, bf16[128,1024]{1,0:T(8,128)(2,1)S(1)}, u32[]{:S(2)}, u32[]{:S(2)}) collective-permute-start(bf16[128,1024]{1,0:T(8,128)(2,1)S(1)} %bitcast.59), channel_id=1, source_target_pairs={{0,64},{64,0},{1,65},{65,1},{2,66},{66,2},{3,67},{67,3},{4,68},{68... | collective-permute-start | bytes 786440 | tf_op jit(solution)/shard_map/ppermute | solution.py:39
  130.3 30.7 %bins.1 = f32[2,32,64]{2,1,0:T(8,128)} custom-call(bf16[8,256,256]{2,1,0:T(8,128)(2,1)} %copy-done, bf16[256,1024]{1,0:T(8,128)(2,1)} %pad_maximum_fusion.refs_1_, f32[4,296,256]{2,1,0:T(8,128)} %get-tuple-element.28.refs_2_), custom_call_target="tpu_custom_call" | custom-call | flops 32000000000 | bytes 8000000 | tf_op jit(solution)/shard_map/bins/pallas_call | solution.py:243
  162.6 4.6 %all-to-all-start.4 = ((bf16[32,36,128]{2,1,0:T(8,128)(2,1)}), bf16[32,36,128]{2,1,0:T(8,128)(2,1)S(1)}, u32[]{:S(2)}, u32[]{:S(2)}) async-start(bf16[32,36,128]{2,1,0:T(8,128)(2,1)} %bitcast.24), calls=%async_computation.4 | async-start | bytes 655360 | tf_op jit(solution)/shard_map/all_to_all | solution.py:25
  167.3 3.1 %collective-permute-start.7 = (bf16[2,1,128,256]{3,2,0,1:T(8,128)(2,1)S(1)}, bf16[2,1,128,256]{3,2,0,1:T(8,128)(2,1)S(1)}, u32[]{:S(2)}, u32[]{:S(2)}) collective-permute-start(bf16[2,1,128,256]{3,2,0,1:T(8,128)(2,1)S(1)} %bitcast.68), channel_id=1, source_target_pairs={{0,1},{1,2},{2,3},{3,0},{4,5},{5,6},{6,7},{7,4},{8,9},{9,10},{10,1... | collective-permute-start | bytes 393224 | tf_op jit(solution)/shard_map/ppermute | solution.py:342
  170.5 4.3 %collective-permute-start.8 = (bf16[2,1,128,256]{3,2,0,1:T(8,128)(2,1)S(1)}, bf16[2,1,128,256]{3,2,0,1:T(8,128)(2,1)S(1)}, u32[]{:S(2)}, u32[]{:S(2)}) collective-permute-start(bf16[2,1,128,256]{3,2,0,1:T(8,128)(2,1)S(1)} %bitcast.67), channel_id=1, source_target_pairs={{0,2},{1,3},{2,0},{3,1},{4,6},{5,7},{6,4},{7,5},{8,10},{9,11},{10,... | collective-permute-start | bytes 393224 | tf_op jit(solution)/shard_map/ppermute | solution.py:342
  174.8 3.1 %collective-permute-start.9 = (bf16[2,1,128,256]{3,2,0,1:T(8,128)(2,1)S(1)}, bf16[2,1,128,256]{3,2,0,1:T(8,128)(2,1)S(1)}, u32[]{:S(2)}, u32[]{:S(2)}) collective-permute-start(bf16[2,1,128,256]{3,2,0,1:T(8,128)(2,1)S(1)} %bitcast.66), channel_id=1, source_target_pairs={{0,3},{1,0},{2,1},{3,2},{4,7},{5,4},{6,5},{7,6},{8,11},{9,8},{10,9... | collective-permute-start | bytes 393224 | tf_op jit(solution)/shard_map/ppermute | solution.py:342
  180.8 6.2 %all-to-all-start.5 = ((bf16[16,36,128]{2,1,0:T(8,128)(2,1)}), bf16[16,36,128]{2,1,0:T(8,128)(2,1)S(1)}, u32[]{:S(2)}, u32[]{:S(2)}) async-start(bf16[16,36,128]{2,1,0:T(8,128)(2,1)} %broadcast_in_dim.35), calls=%async_computation.5 | async-start | bytes 327680 | tf_op jit(solution)/shard_map/all_to_all | solution.py:25
  187.1 9.5 %all-to-all-done.5 = bf16[16,36,128]{2,1,0:T(8,128)(2,1)S(1)} async-done(((bf16[16,36,128]{2,1,0:T(8,128)(2,1)}), bf16[16,36,128]{2,1,0:T(8,128)(2,1)S(1)}, u32[]{:S(2)}, u32[]{:S(2)}) %all-to-all-start.5) | async-done | bytes 147488 | tf_op jit(solution)/shard_map/all_to_all | solution.py:25
  (88 shorter events, 32.4 us)
Async XLA Ops:
  0.6 11.1 %copy-start.2 = (s32[256,256]{1,0:T(8,128)S(1)}, s32[256,256]{1,0:T(8,128)}, u32[]{:S(2)}) copy-start(s32[256,256]{1,0:T(8,128)} %param.12) | copy-start | bytes 786436
  2.3 10.6 %collective-permute-start = (bf16[128,384]{1,0:T(8,128)(2,1)S(1)}, bf16[128,384]{1,0:T(8,128)(2,1)S(1)}, u32[]{:S(2)}, u32[]{:S(2)}) collective-permute-start(bf16[128,384]{1,0:T(8,128)(2,1)S(1)} %pad_maximum_fusion.10), channel_id=1, source_target_pairs={{0,4},{4,0},{1,5},{5,1},{2,6},{6,2},{3,7},{7,3},{8,12},{12,8},{9,1... | collective-permute-start | bytes 294920 | tf_op jit(solution)/shard_map/ppermute | solution.py:39
  12.9 5.0 %copy-start.3 = (f32[256]{0:T(256)S(1)}, f32[256]{0:T(256)}, u32[]{:S(2)}) copy-start(f32[256]{0:T(256)} %param.16) | copy-start | bytes 3076
  13.8 11.0 %all-to-all-start = ((bf16[4,256,256]{2,1,0:T(8,128)(2,1)}), bf16[4,256,256]{2,1,0:T(8,128)(2,1)S(1)}, u32[]{:S(2)}, u32[]{:S(2)}) async-start(bf16[4,256,256]{2,1,0:T(8,128)(2,1)} %broadcast_in_dim.27), calls=%async_computation | async-start | bytes 1048576 | tf_op jit(solution)/shard_map/all_to_all | solution.py:25
  26.0 22.6 %collective-permute-start.1 = (bf16[256,128]{0,1:T(8,128)(2,1)S(1)}, bf16[256,128]{0,1:T(8,128)(2,1)S(1)}, u32[]{:S(2)}, u32[]{:S(2)}) collective-permute-start(bf16[256,128]{0,1:T(8,128)(2,1)S(1)} %fusion), channel_id=1, source_target_pairs={{0,4},{4,0},{1,5},{5,1},{2,6},{6,2},{3,7},{7,3},{8,12},{12,8},{9,1... | collective-permute-start | bytes 196616 | tf_op jit(solution)/shard_map/ppermute | solution.py:39
  40.8 17.0 %collective-permute-start.4 = (f32[296,256]{1,0:T(8,128)S(1)}, f32[296,256]{1,0:T(8,128)S(1)}, u32[]{:S(2)}, u32[]{:S(2)}) collective-permute-start(f32[296,256]{1,0:T(8,128)S(1)} %get-tuple-element.18), channel_id=1, source_target_pairs={{1,0},{2,1},{3,2},{0,3},{5,4},{6,5},{7,6},{4,7},{9,8},{10,9},{11,1... | collective-permute-start | bytes 909320 | tf_op jit(solution)/shard_map/ppermute | solution.py:325
  43.7 20.6 %collective-permute-start.3 = (f32[296,256]{1,0:T(8,128)S(1)}, f32[296,256]{1,0:T(8,128)S(1)}, u32[]{:S(2)}, u32[]{:S(2)}) collective-permute-start(f32[296,256]{1,0:T(8,128)S(1)} %get-tuple-element.17), channel_id=1, source_target_pairs={{2,0},{3,1},{0,2},{1,3},{6,4},{7,5},{4,6},{5,7},{10,8},{11,9},{8,1... | collective-permute-start | bytes 909320 | tf_op jit(solution)/shard_map/ppermute | solution.py:325
  46.7 24.0 %collective-permute-start.2 = (f32[296,256]{1,0:T(8,128)S(1)}, f32[296,256]{1,0:T(8,128)S(1)}, u32[]{:S(2)}, u32[]{:S(2)}) collective-permute-start(f32[296,256]{1,0:T(8,128)S(1)} %get-tuple-element.16), channel_id=1, source_target_pairs={{3,0},{0,1},{1,2},{2,3},{7,4},{4,5},{5,6},{6,7},{11,8},{8,9},{9,10... | collective-permute-start | bytes 909320 | tf_op jit(solution)/shard_map/ppermute | solution.py:325
  49.8 33.1 %all-to-all-start.1 = ((bf16[8,256,256]{2,1,0:T(8,128)(2,1)}), bf16[8,256,256]{2,1,0:T(8,128)(2,1)S(1)}, u32[]{:S(2)}, u32[]{:S(2)}) async-start(bf16[8,256,256]{2,1,0:T(8,128)(2,1)} %broadcast_in_dim.30), calls=%async_computation.1 | async-start | bytes 2097152 | tf_op jit(solution)/shard_map/all_to_all | solution.py:25
  57.8 0.7 copy-start.6
  64.2 0.7 copy-start.5
  70.6 0.7 copy-start.4
  82.9 1.0 copy-start
  89.1 8.2 %collective-permute-start.5 = (f32[128,1024]{1,0:T(8,128)}, f32[128,1024]{1,0:T(8,128)S(1)}, u32[]{:S(2)}, u32[]{:S(2)}) collective-permute-start(f32[128,1024]{1,0:T(8,128)} %get-tuple-element.27), channel_id=1, source_target_pairs={{0,64},{64,0},{1,65},{65,1},{2,66},{66,2},{3,67},{67,3},{4,68},{68... | collective-permute-start | bytes 1572872 | tf_op jit(solution)/shard_map/ppermute | solution.py:39
  99.1 13.7 %all-to-all-start.2 = ((bf16[4,32,1024]{2,1,0:T(8,128)(2,1)}), bf16[4,32,1024]{2,1,0:T(8,128)(2,1)S(1)}, u32[]{:S(2)}, u32[]{:S(2)}) async-start(bf16[4,32,1024]{2,1,0:T(8,128)(2,1)} %bitcast.12), calls=%async_computation.2 | async-start | bytes 524288 | tf_op jit(solution)/shard_map/all_to_all | solution.py:25
  113.5 9.1 %all-to-all-start.3 = ((bf16[4,32,1024]{2,1,0:T(8,128)(2,1)}), bf16[4,32,1024]{2,1,0:T(8,128)(2,1)S(1)}, u32[]{:S(2)}, u32[]{:S(2)}) async-start(bf16[4,32,1024]{2,1,0:T(8,128)(2,1)} %broadcast_in_dim.32), calls=%async_computation.3 | async-start | bytes 524288 | tf_op jit(solution)/shard_map/all_to_all | solution.py:25
  122.6 6.7 %collective-permute-start.6 = (bf16[128,1024]{1,0:T(8,128)(2,1)S(1)}, bf16[128,1024]{1,0:T(8,128)(2,1)S(1)}, u32[]{:S(2)}, u32[]{:S(2)}) collective-permute-start(bf16[128,1024]{1,0:T(8,128)(2,1)S(1)} %bitcast.59), channel_id=1, source_target_pairs={{0,64},{64,0},{1,65},{65,1},{2,66},{66,2},{3,67},{67,3},{4,68},{68... | collective-permute-start | bytes 786440 | tf_op jit(solution)/shard_map/ppermute | solution.py:39
  162.6 17.4 %all-to-all-start.4 = ((bf16[32,36,128]{2,1,0:T(8,128)(2,1)}), bf16[32,36,128]{2,1,0:T(8,128)(2,1)S(1)}, u32[]{:S(2)}, u32[]{:S(2)}) async-start(bf16[32,36,128]{2,1,0:T(8,128)(2,1)} %bitcast.24), calls=%async_computation.4 | async-start | bytes 655360 | tf_op jit(solution)/shard_map/all_to_all | solution.py:25
  167.3 10.6 %collective-permute-start.7 = (bf16[2,1,128,256]{3,2,0,1:T(8,128)(2,1)S(1)}, bf16[2,1,128,256]{3,2,0,1:T(8,128)(2,1)S(1)}, u32[]{:S(2)}, u32[]{:S(2)}) collective-permute-start(bf16[2,1,128,256]{3,2,0,1:T(8,128)(2,1)S(1)} %bitcast.68), channel_id=1, source_target_pairs={{0,1},{1,2},{2,3},{3,0},{4,5},{5,6},{6,7},{7,4},{8,9},{9,10},{10,1... | collective-permute-start | bytes 393224 | tf_op jit(solution)/shard_map/ppermute | solution.py:342
  170.5 16.6 %collective-permute-start.8 = (bf16[2,1,128,256]{3,2,0,1:T(8,128)(2,1)S(1)}, bf16[2,1,128,256]{3,2,0,1:T(8,128)(2,1)S(1)}, u32[]{:S(2)}, u32[]{:S(2)}) collective-permute-start(bf16[2,1,128,256]{3,2,0,1:T(8,128)(2,1)S(1)} %bitcast.67), channel_id=1, source_target_pairs={{0,2},{1,3},{2,0},{3,1},{4,6},{5,7},{6,4},{7,5},{8,10},{9,11},{10,... | collective-permute-start | bytes 393224 | tf_op jit(solution)/shard_map/ppermute | solution.py:342
  174.8 12.3 %collective-permute-start.9 = (bf16[2,1,128,256]{3,2,0,1:T(8,128)(2,1)S(1)}, bf16[2,1,128,256]{3,2,0,1:T(8,128)(2,1)S(1)}, u32[]{:S(2)}, u32[]{:S(2)}) collective-permute-start(bf16[2,1,128,256]{3,2,0,1:T(8,128)(2,1)S(1)} %bitcast.66), channel_id=1, source_target_pairs={{0,3},{1,0},{2,1},{3,2},{4,7},{5,4},{6,5},{7,6},{8,11},{9,8},{10,9... | collective-permute-start | bytes 393224 | tf_op jit(solution)/shard_map/ppermute | solution.py:342
  180.8 15.8 %all-to-all-start.5 = ((bf16[16,36,128]{2,1,0:T(8,128)(2,1)}), bf16[16,36,128]{2,1,0:T(8,128)(2,1)S(1)}, u32[]{:S(2)}, u32[]{:S(2)}) async-start(bf16[16,36,128]{2,1,0:T(8,128)(2,1)} %broadcast_in_dim.35), calls=%async_computation.5 | async-start | bytes 327680 | tf_op jit(solution)/shard_map/all_to_all | solution.py:25
  187.1 11.1 %copy-start.1 = (bf16[2,4,128,256]{3,2,1,0:T(8,128)(2,1)}, bf16[2,4,128,256]{3,2,1,0:T(8,128)(2,1)S(1)}, u32[]{:S(2)}) copy-start(bf16[2,4,128,256]{3,2,1,0:T(8,128)(2,1)S(1)} %bitcast_dynamic-update-slice_fusion) | copy-start | bytes 1572868

commit v6 on v5

--- a/solution.py
+++ b/solution.py
@@ -119,7 +119,7 @@
         dequant_kernel,
         grid=(1,),
         in_specs=[
-            pl.BlockSpec(block.shape, lambda i: (0, 0)),
+            pl.BlockSpec(memory_space=pltpu.VMEM),
             pl.BlockSpec(books[0].shape, lambda i: (0, 0)),
             pl.BlockSpec(books[1].shape, lambda i: (0, 0)),
         ]
@@ -156,7 +156,7 @@
 
 
 def project(core, attended, weight):
-    steps, tokens, width = attended.shape
+    _, tokens, _ = attended.shape
     blocks, depth, rows = weight.shape
     out = jax.ShapeDtypeStruct((tokens // 2, blocks * rows), f32)
     out_spec = pl.BlockSpec((tokens // 2, rows), lambda i, core: (0, i))
@@ -166,7 +166,7 @@
             num_scalar_prefetch=1,
             grid=(blocks,),
             in_specs=[
-                pl.BlockSpec((steps, tokens, width), lambda i, core: (0, 0, 0)),
+                pl.BlockSpec(memory_space=pltpu.VMEM),
                 pl.BlockSpec((None, depth, rows), lambda i, core: (i, 0, 0)),
             ],
             out_specs=[out_spec, out_spec],
@@ -177,15 +177,19 @@
     )(core, attended, weight)
 
 
-def bins_kernel(scaling, att_ref, misfit_ref, plan_ref, bins_ref, grad_ref, digit_ref):
+def bins_kernel(scaling, *refs):
+    own_att_ref, their_att_ref, own_misfit_ref, their_misfit_ref = refs[:4]
+    plan_ref, bins_ref, grad_ref, digit_ref = refs[4:]
     groups, rows = digit_ref.shape[1:]
-    steps, _, width = att_ref.shape
+    steps, _, width = own_att_ref.shape
     scale = plan_ref[groups : groups + 1, :] * scaling
-    misfit = misfit_ref[...]
     for z in range(steps):
-        weight_grad = lax.dot_general(
-            att_ref[z], misfit, (((0,), (0,)), ((), ())), preferred_element_type=f32
-        )
+        weight_grad = None
+        for att_ref, misfit_ref in ((own_att_ref, own_misfit_ref), (their_att_ref, their_misfit_ref)):
+            part = lax.dot_general(
+                att_ref[z], misfit_ref[...], (((0,), (0,)), ((), ())), preferred_element_type=f32
+            )
+            weight_grad = part if weight_grad is None else weight_grad + part
         grad_ref[z * width : (z + 1) * width, :] = weight_grad * scale
     packed = plan_ref[:groups, :].astype(jnp.int32)
     for book in range(2):
@@ -237,16 +241,19 @@
         bins_ref[book] += totals[book]
 
 
-def bin_gradients(attended, misfit, plan, groups, scaling):
-    steps, tokens, width = attended.shape
+def bin_gradients(own, theirs, plan, groups, scaling):
+    steps, tokens, width = own[0].shape
     blocks, depth, rows = plan.shape
+    whole = pl.BlockSpec(memory_space=pltpu.VMEM)
     return pl.pallas_call(
         lambda *refs: bins_kernel(scaling, *refs),
-        grid=(blocks,),
+        grid=(blocks // 2,),
         in_specs=[
-            pl.BlockSpec((steps, tokens, width), lambda i: (0, 0, 0)),
+            whole,
+            whole,
+            pl.BlockSpec((tokens, rows), lambda i: (0, 2 * i)),
             pl.BlockSpec((tokens, rows), lambda i: (0, i)),
-            pl.BlockSpec((None, depth, rows), lambda i: (i, 0, 0)),
+            pl.BlockSpec((None, depth, rows), lambda i: (2 * i, 0, 0)),
         ],
         out_specs=pl.BlockSpec((2, HIGH, LOW * GROUP), lambda i: (0, 0, 0)),
         out_shape=jax.ShapeDtypeStruct((2, HIGH, LOW * GROUP), f32),
@@ -255,10 +262,10 @@
             pltpu.VMEM((4, groups, rows), f32),
         ],
         cost_estimate=pl.CostEstimate(
-            flops=blocks * 8_000_000_000, transcendentals=0, bytes_accessed=blocks * 2_000_000
+            flops=blocks * 4_000_000_000, transcendentals=0, bytes_accessed=blocks * 1_000_000
         ),
         name="bins",
-    )(attended, misfit, plan)
+    )(own[0], theirs[0], own[1], theirs[1], plan)
 
 
 def attend(queries, keys, values, query_places, key_places):
@@ -327,6 +334,8 @@
     weight, plan = built
 
     keep, send = project(core[None], attended, weight)
+    pair = [(0, 1), (1, 0), (2, 3), (3, 2)]
+    their_attended = lax.ppermute(attended, "tok_1", pair)
     half_sum = (keep + swap(send, "col_1")).astype(bf16)
     parts = exchange(half_sum.reshape(count_lane, share, -1), "col_0")
     output = jnp.sum(parts.astype(f32), axis=0)
@@ -335,18 +344,27 @@
     other_half = swap(misfit_half, "col_1")
     misfit = jnp.concatenate(in_order(misfit_half, other_half, core), axis=0)
 
-    out_pieces = []
-    for k in range(count_across):
-        piece = misfit[:, k * rows : (k + 1) * rows].reshape(2, 1, tok_rows, rows)
-        route = [(i, (i + k) % count_across) for i in range(count_across)]
-        out_pieces.append(lax.ppermute(piece, "tok_1", route) if k else piece)
+    even = across % 2 == 0
+    blocks = [misfit[:, k * rows : (k + 1) * rows] for k in range(count_across)]
+    pairs_own, pairs_next = jnp.where(even, blocks[1], blocks[3]), jnp.where(even, blocks[3], blocks[1])
+    their_misfit = lax.ppermute(jnp.concatenate([pairs_own, pairs_next], axis=1), "tok_1", pair)
+    from_across = lax.ppermute(blocks[2], "tok_1", [(0, 2), (1, 3), (2, 0), (3, 1)])
+    from_beside = lax.ppermute(pairs_next, "tok_1", [(1, 2), (2, 1), (3, 0), (0, 3)])
+    step = jnp.where(even, 1, count_across - 1)
+    out_pieces = (
+        (blocks[0], across),
+        (their_misfit[:, :rows], (across + step) % count_across),
+        (from_across, (across + 2) % count_across),
+        (from_beside, (across + count_across - step) % count_across),
+    )
 
     scale_part = jnp.sum(misfit_share.astype(f32) * output, axis=0).reshape(count_across, -1, 128)
     extra = scale_part.shape[1]
     scale_part = jnp.concatenate([scale_part, scale_part], axis=0)
     start = (count_across - across) % count_across
     scale_part = in_two(lax.dynamic_slice_in_dim(scale_part, start, count_across, 0), 1)
-    bins = bin_gradients(attended, misfit, plan, groups, 1.0 / tokens)
+    theirs = (their_attended, their_misfit)
+    bins = bin_gradients((attended, misfit), theirs, plan, groups, 1.0 / tokens)
 
     count_row = lax.axis_size("row")
     bins = bins.reshape(-1, 128).astype(bf16)
@@ -367,9 +385,9 @@
     grad_books = jnp.sum(sums[:, : -2 * extra].astype(f32), axis=0).reshape(2, ENTRIES, GROUP)
 
     misfit_out = jnp.zeros((2, count_across, tok_rows, rows), bf16)
-    for k in range(count_across):
-        peer = (across + count_across - k) % count_across
-        misfit_out = lax.dynamic_update_slice_in_dim(misfit_out, out_pieces[k], peer, 1)
+    for piece, peer in out_pieces:
+        piece = piece.reshape(2, 1, tok_rows, rows)
+        misfit_out = lax.dynamic_update_slice_in_dim(misfit_out, piece, peer, 1)
     return misfit_out.reshape(tokens, rows), grad_scales, grad_books
 
 

time: 199 us -> 217 us (1.090)
  waiting for transfers between devices: 37.4 us -> 60.2 us
  Pallas kernels: 58.6 us -> 45.3 us
  blocking collectives: 0 us -> 9.38 us
    ppermute x3 -> x4, waiting for transfers between devices: 0.01 us -> 24.9 us  [the longest x1 19.3 us: device_part(): their_attended = lax.ppermute(attended, 'tok_1', pair)]
    pallas_call x5, Pallas kernels: 53.5 us -> 40.2 us  [the longest x4 22.8 us: dequantize(): pl.pallas_call(dequant_kernel, grid=(1,), in_specs=[pl.BlockSpec(memory_s...]
    all_to_all x0 -> x1, blocking collectives: none -> 9.38 us  [exchange(): return lax.all_to_all(pieces, axis, 0, 0, tiled=True)]
    all_to_all x6 -> x5, starting transfers between devices: 32.5 us -> 29.1 us  [exchange(): return lax.all_to_all(pieces, axis, 0, 0, tiled=True)]
    all_to_all x6 -> x5, waiting for transfers between devices: 35.6 us -> 33.5 us  [exchange(): return lax.all_to_all(pieces, axis, 0, 0, tiled=True)]
    ppermute x3 -> x4, starting transfers between devices: 10.5 us -> 12.1 us  [the longest x1 4.35 us: device_part(): lax.ppermute(pairs_next, 'tok_1', [(1, 2), (2, 1), (3, 0), (0, 3)])]
    unnamed x18 -> x24, local copies, waits for them, and re-layouts: 5.98 us -> 6.71 us
  transfers between devices with their start and end apart: 16 -> 16, of which waited for: 8 -> 8; matrix products, arithmetic and copies ran while one was open for 4% -> 4% of each run, Pallas kernels for 12% -> 11%
where the time goes in v6:
time: 217 us; the launch traced here: 215 us
  starting transfers between devices  78.4 us (36%)
  waiting for transfers between devices  60.2 us (28%)
  Pallas kernels  45.3 us (21%)
  local copies, waits for them, and re-layouts  11.6 us (5%)
  blocking collectives  9.38 us (4%)
  other arithmetic  8.36 us (4%)
    all_to_all x5, waiting for transfers between devices, exchange(): return lax.all_to_all(pieces, axis, 0, 0, tiled=True)  33.5 us
    ppermute x4, starting transfers between devices, swap(): return lax.ppermute(array, axis, [(0, 1), (1, 0)])  29.4 us
    all_to_all x5, starting transfers between devices, exchange(): return lax.all_to_all(pieces, axis, 0, 0, tiled=True)  29.1 us
    pallas_call x4, Pallas kernels, dequantize(): pl.pallas_call(dequant_kernel, grid=(1,), in_specs=[pl.BlockSpec(memory_s...  22.8 us
    ppermute x1, waiting for transfers between devices, device_part(): their_attended = lax.ppermute(attended, 'tok_1', pair)  19.3 us
    pallas_call x1, Pallas kernels, bin_gradients(): pl.pallas_call(lambda *refs: bins_kernel(scaling, *refs), grid=(blocks //...  17.3 us
    all_to_all x1, blocking collectives, exchange(): return lax.all_to_all(pieces, axis, 0, 0, tiled=True)  9.38 us
    ppermute x3, starting transfers between devices, device_part(): received.append(lax.ppermute(sent, 'tok_1', route))  7.8 us
  transfers between devices with their start and end apart: 16, of which 8 were waited for; matrix products, arithmetic and copies ran while one was open for 4% of the time, Pallas kernels for 11%

profile of v6, /device:TPU:1, one launch (start us, length us, event | category | flops | bytes accessed | tf_op | source)
XLA Modules:
  0.0 215.3 jit_solution(17553000249915966923)
XLA Ops:
  2.3 8.3 %collective-permute-start = (bf16[128,384]{1,0:T(8,128)(2,1)S(1)}, bf16[128,384]{1,0:T(8,128)(2,1)S(1)}, u32[]{:S(2)}, u32[]{:S(2)}) collective-permute-start(bf16[128,384]{1,0:T(8,128)(2,1)S(1)} %pad_maximum_fusion.11), channel_id=1, source_target_pairs={{0,4},{4,0},{1,5},{5,1},{2,6},{6,2},{3,7},{7,3},{8,12},{12,8},{9,1... | collective-permute-start | bytes 294920 | tf_op jit(solution)/shard_map/ppermute | solution.py:39
  13.8 4.0 %all-to-all-start = ((bf16[4,256,256]{2,1,0:T(8,128)(2,1)}), bf16[4,256,256]{2,1,0:T(8,128)(2,1)S(1)}, u32[]{:S(2)}, u32[]{:S(2)}) async-start(bf16[4,256,256]{2,1,0:T(8,128)(2,1)} %broadcast_in_dim.27), calls=%async_computation | async-start | bytes 1048576 | tf_op jit(solution)/shard_map/all_to_all | solution.py:25
  18.8 6.0 %all-to-all-done = bf16[4,256,256]{2,1,0:T(8,128)(2,1)S(1)} async-done(((bf16[4,256,256]{2,1,0:T(8,128)(2,1)}), bf16[4,256,256]{2,1,0:T(8,128)(2,1)S(1)}, u32[]{:S(2)}, u32[]{:S(2)}) %all-to-all-start) | async-done | bytes 524320 | tf_op jit(solution)/shard_map/all_to_all | solution.py:25
  26.0 9.0 %collective-permute-start.1 = (bf16[256,128]{0,1:T(8,128)(2,1)S(1)}, bf16[256,128]{0,1:T(8,128)(2,1)S(1)}, u32[]{:S(2)}, u32[]{:S(2)}) collective-permute-start(bf16[256,128]{0,1:T(8,128)(2,1)S(1)} %fusion), channel_id=1, source_target_pairs={{0,4},{4,0},{1,5},{5,1},{2,6},{6,2},{3,7},{7,3},{8,12},{12,8},{9,1... | collective-permute-start | bytes 196616 | tf_op jit(solution)/shard_map/ppermute | solution.py:39
  35.1 5.7 %dequant.4 = (bf16[4,2048,256]{2,1,0:T(8,128)(2,1)}, f32[4,296,256]{2,1,0:T(8,128)}) custom-call(f32[296,256]{1,0:T(8,128)} %get-tuple-element.45.block_ref, bf16[8,256]{1,0:T(8,128)(2,1)} %bitcast.73, bf16[8,256]{1,0:T(8,128)(2,1)} %bitcast.77), custom_call_target="tpu_custom_call" | custom-call | flops 8000000000 | bytes 1500000 | tf_op jit(solution)/shard_map/dequant/pallas_call | solution.py:118
  49.8 8.0 %all-to-all-start.1 = ((bf16[8,256,256]{2,1,0:T(8,128)(2,1)}), bf16[8,256,256]{2,1,0:T(8,128)(2,1)S(1)}, u32[]{:S(2)}, u32[]{:S(2)}) async-start(bf16[8,256,256]{2,1,0:T(8,128)(2,1)} %broadcast_in_dim.30), calls=%async_computation.1 | async-start | bytes 2097152 | tf_op jit(solution)/shard_map/all_to_all | solution.py:25
  58.5 5.7 %dequant.5 = (bf16[4,2048,256]{2,1,0:T(8,128)(2,1)}, f32[4,296,256]{2,1,0:T(8,128)}) custom-call(f32[296,256]{1,0:T(8,128)} %copy-done.9, bf16[8,256]{1,0:T(8,128)(2,1)} %bitcast.74, bf16[8,256]{1,0:T(8,128)(2,1)} %bitcast.78, bf16[4,2048,256]{2,1,0:T(8,128)(2,1)} %get-tuple-element.19.refs_0_, ...), custom_call_target="tpu_custom_call", output_to_operand_aliasing={{0}: (3, {}), {1}: (4, {})} | custom-call | flops 8000000000 | bytes 1500000 | tf_op jit(solution)/shard_map/dequant/pallas_call | solution.py:118
  65.0 5.7 %dequant.6 = (bf16[4,2048,256]{2,1,0:T(8,128)(2,1)}, f32[4,296,256]{2,1,0:T(8,128)}) custom-call(f32[296,256]{1,0:T(8,128)} %copy-done.8, bf16[8,256]{1,0:T(8,128)(2,1)} %bitcast.75, bf16[8,256]{1,0:T(8,128)(2,1)} %bitcast.79, bf16[4,2048,256]{2,1,0:T(8,128)(2,1)} %get-tuple-element.21.refs_0_, ...), custom_call_target="tpu_custom_call", output_to_operand_aliasing={{0}: (3, {}), {1}: (4, {})} | custom-call | flops 8000000000 | bytes 1500000 | tf_op jit(solution)/shard_map/dequant/pallas_call | solution.py:118
  71.4 5.7 %dequant.7 = (bf16[4,2048,256]{2,1,0:T(8,128)(2,1)}, f32[4,296,256]{2,1,0:T(8,128)}) custom-call(f32[296,256]{1,0:T(8,128)} %copy-done.7, bf16[8,256]{1,0:T(8,128)(2,1)} %bitcast.76, bf16[8,256]{1,0:T(8,128)(2,1)} %bitcast.80, bf16[4,2048,256]{2,1,0:T(8,128)(2,1)} %get-tuple-element.23.refs_0_, ...), custom_call_target="tpu_custom_call", output_to_operand_aliasing={{0}: (3, {}), {1}: (4, {})} | custom-call | flops 8000000000 | bytes 1500000 | tf_op jit(solution)/shard_map/dequant/pallas_call | solution.py:118
  77.1 5.8 %all-to-all-done.1.att_ref.refs_0_ = bf16[8,256,256]{2,1,0:T(8,128)(2,1)S(1)} async-done(((bf16[8,256,256]{2,1,0:T(8,128)(2,1)}), bf16[8,256,256]{2,1,0:T(8,128)(2,1)S(1)}, u32[]{:S(2)}, u32[]{:S(2)}) %all-to-all-start.1) | async-done | bytes 1048608 | tf_op jit(solution)/shard_map/all_to_all | solution.py:25
  83.9 5.2 %project.1 = (f32[128,1024]{1,0:T(8,128)}, f32[128,1024]{1,0:T(8,128)}) custom-call(s32[1]{0:T(128)} %bitcast.core_ref, bf16[8,256,256]{2,1,0:T(8,128)(2,1)} %copy-done, bf16[4,2048,256]{2,1,0:T(8,128)(2,1)} %get-tuple-element.25.weight_ref), custom_call_target="tpu_custom_call" | custom-call | tf_op jit(solution)/shard_map/project/pallas_call | solution.py:163
  89.1 6.5 %collective-permute-start.5 = (f32[128,1024]{1,0:T(8,128)}, f32[128,1024]{1,0:T(8,128)S(1)}, u32[]{:S(2)}, u32[]{:S(2)}) collective-permute-start(f32[128,1024]{1,0:T(8,128)} %get-tuple-element.27), channel_id=1, source_target_pairs={{0,64},{64,0},{1,65},{65,1},{2,66},{66,2},{3,67},{67,3},{4,68},{68... | collective-permute-start | bytes 1572872 | tf_op jit(solution)/shard_map/ppermute | solution.py:39
  99.2 6.4 %all-to-all-start.2 = ((bf16[4,32,1024]{2,1,0:T(8,128)(2,1)}), bf16[4,32,1024]{2,1,0:T(8,128)(2,1)S(1)}, u32[]{:S(2)}, u32[]{:S(2)}) async-start(bf16[4,32,1024]{2,1,0:T(8,128)(2,1)} %bitcast.12), calls=%async_computation.2 | async-start | bytes 524288 | tf_op jit(solution)/shard_map/all_to_all | solution.py:25
  106.4 6.5 %all-to-all-done.2 = bf16[4,32,1024]{2,1,0:T(8,128)(2,1)S(1)} async-done(((bf16[4,32,1024]{2,1,0:T(8,128)(2,1)}), bf16[4,32,1024]{2,1,0:T(8,128)(2,1)S(1)}, u32[]{:S(2)}, u32[]{:S(2)}) %all-to-all-start.2) | async-done | bytes 262176 | tf_op jit(solution)/shard_map/all_to_all | solution.py:25
  113.0 9.4 %all_to_all.30 = bf16[4,32,1024]{2,1,0:T(8,128)(2,1)S(1)} all-to-all(bf16[4,32,1024]{2,1,0:T(8,128)(2,1)S(1)} %broadcast_in_dim.32), channel_id=1, replica_groups=mesh['col_0'=4,'col_1'=2,'row'=8,'tok_0'=2,'tok_1'=4] {'col_0'}, dimensions={0} | all-to-all | bytes 524288 | tf_op jit(solution)/shard_map/all_to_all | solution.py:25
  122.4 5.6 %collective-permute-start.6 = (bf16[128,1024]{1,0:T(8,128)(2,1)S(1)}, bf16[128,1024]{1,0:T(8,128)(2,1)S(1)}, u32[]{:S(2)}, u32[]{:S(2)}) collective-permute-start(bf16[128,1024]{1,0:T(8,128)(2,1)S(1)} %bitcast.59), channel_id=1, source_target_pairs={{0,64},{64,0},{1,65},{65,1},{2,66},{66,2},{3,67},{67,3},{4,68},{68... | collective-permute-start | bytes 786440 | tf_op jit(solution)/shard_map/ppermute | solution.py:39
  135.4 19.3 %collective-permute-done.10.refs_1_ = bf16[8,256,256]{2,1,0:T(8,128)(2,1)S(1)} collective-permute-done((bf16[8,256,256]{2,1,0:T(8,128)(2,1)S(1)}, bf16[8,256,256]{2,1,0:T(8,128)(2,1)S(1)}, u32[]{:S(2)}, u32[]{:S(2)}) %collective-permute-start.10) | collective-permute-done | bytes 1048608 | tf_op jit(solution)/shard_map/ppermute | solution.py:338
  154.6 5.6 %collective-permute-done.7.refs_3_ = bf16[256,512]{1,0:T(8,128)(2,1)S(1)} collective-permute-done((bf16[256,512]{1,0:T(8,128)(2,1)S(1)}, bf16[256,512]{1,0:T(8,128)(2,1)S(1)}, u32[]{:S(2)}, u32[]{:S(2)}) %collective-permute-start.7) | collective-permute-done | bytes 262176 | tf_op jit(solution)/shard_map/ppermute | solution.py:350
  161.0 17.3 %bins.1 = f32[2,32,64]{2,1,0:T(8,128)} custom-call(bf16[8,256,256]{2,1,0:T(8,128)(2,1)} %copy-done, bf16[8,256,256]{2,1,0:T(8,128)(2,1)} %copy-done.6, bf16[256,1024]{1,0:T(8,128)(2,1)} %pad_maximum_fusion.refs_2_, bf16[256,512]{1,0:T(8,128)(2,1)} %copy-done.3, f32[4,296,256]{2,1,0:T(8,128)} %get-tuple-element.28.refs_4_), custom_call_target="tpu_custom_call" | custom-call | flops 16000000000 | bytes 4000000 | tf_op jit(solution)/shard_map/bins/pallas_call | solution.py:248
  180.0 4.7 %all-to-all-start.4 = ((bf16[32,36,128]{2,1,0:T(8,128)(2,1)}), bf16[32,36,128]{2,1,0:T(8,128)(2,1)S(1)}, u32[]{:S(2)}, u32[]{:S(2)}) async-start(bf16[32,36,128]{2,1,0:T(8,128)(2,1)} %bitcast.24), calls=%async_computation.4 | async-start | bytes 655360 | tf_op jit(solution)/shard_map/all_to_all | solution.py:25
  184.8 4.3 %collective-permute-start.9 = (bf16[256,256]{1,0:T(8,128)(2,1)S(1)}, bf16[256,256]{1,0:T(8,128)(2,1)S(1)}, u32[]{:S(2)}, u32[]{:S(2)}) collective-permute-start(bf16[256,256]{1,0:T(8,128)(2,1)S(1)} %get-tuple-element.41), channel_id=1, source_target_pairs={{1,2},{2,1},{3,0},{0,3},{5,6},{6,5},{7,4},{4,7},{9,10},{10,9},{11,... | collective-permute-start | bytes 393224 | tf_op jit(solution)/shard_map/ppermute | solution.py:352
  191.7 5.7 %all-to-all-done.4 = bf16[32,36,128]{2,1,0:T(8,128)(2,1)S(1)} async-done(((bf16[32,36,128]{2,1,0:T(8,128)(2,1)}), bf16[32,36,128]{2,1,0:T(8,128)(2,1)S(1)}, u32[]{:S(2)}, u32[]{:S(2)}) %all-to-all-start.4) | async-done | bytes 294944 | tf_op jit(solution)/shard_map/all_to_all | solution.py:25
  198.2 6.0 %all-to-all-start.5 = ((bf16[16,36,128]{2,1,0:T(8,128)(2,1)}), bf16[16,36,128]{2,1,0:T(8,128)(2,1)S(1)}, u32[]{:S(2)}, u32[]{:S(2)}) async-start(bf16[16,36,128]{2,1,0:T(8,128)(2,1)} %broadcast_in_dim.35), calls=%async_computation.5 | async-start | bytes 327680 | tf_op jit(solution)/shard_map/all_to_all | solution.py:25
  204.3 9.5 %all-to-all-done.5 = bf16[16,36,128]{2,1,0:T(8,128)(2,1)S(1)} async-done(((bf16[16,36,128]{2,1,0:T(8,128)(2,1)}), bf16[16,36,128]{2,1,0:T(8,128)(2,1)S(1)}, u32[]{:S(2)}, u32[]{:S(2)}) %all-to-all-start.5) | async-done | bytes 147488 | tf_op jit(solution)/shard_map/all_to_all | solution.py:25
  (98 shorter events, 38.1 us)
Async XLA Ops:
  0.6 11.1 %copy-start.4 = (s32[256,256]{1,0:T(8,128)S(1)}, s32[256,256]{1,0:T(8,128)}, u32[]{:S(2)}) copy-start(s32[256,256]{1,0:T(8,128)} %param.12) | copy-start | bytes 786436
  2.3 10.6 %collective-permute-start = (bf16[128,384]{1,0:T(8,128)(2,1)S(1)}, bf16[128,384]{1,0:T(8,128)(2,1)S(1)}, u32[]{:S(2)}, u32[]{:S(2)}) collective-permute-start(bf16[128,384]{1,0:T(8,128)(2,1)S(1)} %pad_maximum_fusion.11), channel_id=1, source_target_pairs={{0,4},{4,0},{1,5},{5,1},{2,6},{6,2},{3,7},{7,3},{8,12},{12,8},{9,1... | collective-permute-start | bytes 294920 | tf_op jit(solution)/shard_map/ppermute | solution.py:39
  12.9 5.0 %copy-start.5 = (f32[256]{0:T(256)S(1)}, f32[256]{0:T(256)}, u32[]{:S(2)}) copy-start(f32[256]{0:T(256)} %param.16) | copy-start | bytes 3076
  13.8 11.0 %all-to-all-start = ((bf16[4,256,256]{2,1,0:T(8,128)(2,1)}), bf16[4,256,256]{2,1,0:T(8,128)(2,1)S(1)}, u32[]{:S(2)}, u32[]{:S(2)}) async-start(bf16[4,256,256]{2,1,0:T(8,128)(2,1)} %broadcast_in_dim.27), calls=%async_computation | async-start | bytes 1048576 | tf_op jit(solution)/shard_map/all_to_all | solution.py:25
  26.0 22.6 %collective-permute-start.1 = (bf16[256,128]{0,1:T(8,128)(2,1)S(1)}, bf16[256,128]{0,1:T(8,128)(2,1)S(1)}, u32[]{:S(2)}, u32[]{:S(2)}) collective-permute-start(bf16[256,128]{0,1:T(8,128)(2,1)S(1)} %fusion), channel_id=1, source_target_pairs={{0,4},{4,0},{1,5},{5,1},{2,6},{6,2},{3,7},{7,3},{8,12},{12,8},{9,1... | collective-permute-start | bytes 196616 | tf_op jit(solution)/shard_map/ppermute | solution.py:39
  40.8 17.0 %collective-permute-start.4 = (f32[296,256]{1,0:T(8,128)S(1)}, f32[296,256]{1,0:T(8,128)S(1)}, u32[]{:S(2)}, u32[]{:S(2)}) collective-permute-start(f32[296,256]{1,0:T(8,128)S(1)} %get-tuple-element.18), channel_id=1, source_target_pairs={{1,0},{2,1},{3,2},{0,3},{5,4},{6,5},{7,6},{4,7},{9,8},{10,9},{11,1... | collective-permute-start | bytes 909320 | tf_op jit(solution)/shard_map/ppermute | solution.py:332
  43.7 20.6 %collective-permute-start.3 = (f32[296,256]{1,0:T(8,128)S(1)}, f32[296,256]{1,0:T(8,128)S(1)}, u32[]{:S(2)}, u32[]{:S(2)}) collective-permute-start(f32[296,256]{1,0:T(8,128)S(1)} %get-tuple-element.17), channel_id=1, source_target_pairs={{2,0},{3,1},{0,2},{1,3},{6,4},{7,5},{4,6},{5,7},{10,8},{11,9},{8,1... | collective-permute-start | bytes 909320 | tf_op jit(solution)/shard_map/ppermute | solution.py:332
  46.7 24.0 %collective-permute-start.2 = (f32[296,256]{1,0:T(8,128)S(1)}, f32[296,256]{1,0:T(8,128)S(1)}, u32[]{:S(2)}, u32[]{:S(2)}) collective-permute-start(f32[296,256]{1,0:T(8,128)S(1)} %get-tuple-element.16), channel_id=1, source_target_pairs={{3,0},{0,1},{1,2},{2,3},{7,4},{4,5},{5,6},{6,7},{11,8},{8,9},{9,10... | collective-permute-start | bytes 909320 | tf_op jit(solution)/shard_map/ppermute | solution.py:332
  49.8 33.1 %all-to-all-start.1 = ((bf16[8,256,256]{2,1,0:T(8,128)(2,1)}), bf16[8,256,256]{2,1,0:T(8,128)(2,1)S(1)}, u32[]{:S(2)}, u32[]{:S(2)}) async-start(bf16[8,256,256]{2,1,0:T(8,128)(2,1)} %broadcast_in_dim.30), calls=%async_computation.1 | async-start | bytes 2097152 | tf_op jit(solution)/shard_map/all_to_all | solution.py:25
  57.8 0.7 copy-start.9
  82.9 1.0 copy-start
  89.1 8.2 %collective-permute-start.5 = (f32[128,1024]{1,0:T(8,128)}, f32[128,1024]{1,0:T(8,128)S(1)}, u32[]{:S(2)}, u32[]{:S(2)}) collective-permute-start(f32[128,1024]{1,0:T(8,128)} %get-tuple-element.27), channel_id=1, source_target_pairs={{0,64},{64,0},{1,65},{65,1},{2,66},{66,2},{3,67},{67,3},{4,68},{68... | collective-permute-start | bytes 1572872 | tf_op jit(solution)/shard_map/ppermute | solution.py:39
  99.2 28.9 %copy-start.1 = (bf16[8,256,256]{2,1,0:T(8,128)(2,1)S(1)}, bf16[8,256,256]{2,1,0:T(8,128)(2,1)}, u32[]{:S(2)}) copy-start(bf16[8,256,256]{2,1,0:T(8,128)(2,1)} %copy-done) | copy-start | bytes 3145732
  99.2 13.8 %all-to-all-start.2 = ((bf16[4,32,1024]{2,1,0:T(8,128)(2,1)}), bf16[4,32,1024]{2,1,0:T(8,128)(2,1)S(1)}, u32[]{:S(2)}, u32[]{:S(2)}) async-start(bf16[4,32,1024]{2,1,0:T(8,128)(2,1)} %bitcast.12), calls=%async_computation.2 | async-start | bytes 524288 | tf_op jit(solution)/shard_map/all_to_all | solution.py:25
  122.4 10.0 %collective-permute-start.6 = (bf16[128,1024]{1,0:T(8,128)(2,1)S(1)}, bf16[128,1024]{1,0:T(8,128)(2,1)S(1)}, u32[]{:S(2)}, u32[]{:S(2)}) collective-permute-start(bf16[128,1024]{1,0:T(8,128)(2,1)S(1)} %bitcast.59), channel_id=1, source_target_pairs={{0,64},{64,0},{1,65},{65,1},{2,66},{66,2},{3,67},{67,3},{4,68},{68... | collective-permute-start | bytes 786440 | tf_op jit(solution)/shard_map/ppermute | solution.py:39
  128.0 26.6 %collective-permute-start.10 = (bf16[8,256,256]{2,1,0:T(8,128)(2,1)S(1)}, bf16[8,256,256]{2,1,0:T(8,128)(2,1)S(1)}, u32[]{:S(2)}, u32[]{:S(2)}) collective-permute-start(bf16[8,256,256]{2,1,0:T(8,128)(2,1)S(1)} %copy-done.1), channel_id=1, source_target_pairs={{0,1},{1,0},{2,3},{3,2},{4,5},{5,4},{6,7},{7,6},{8,9},{9,8},{10,11... | collective-permute-start | bytes 3145736 | tf_op jit(solution)/shard_map/ppermute | solution.py:338
  132.5 27.7 %collective-permute-start.7 = (bf16[256,512]{1,0:T(8,128)(2,1)S(1)}, bf16[256,512]{1,0:T(8,128)(2,1)S(1)}, u32[]{:S(2)}, u32[]{:S(2)}) collective-permute-start(bf16[256,512]{1,0:T(8,128)(2,1)S(1)} %pad_maximum_fusion.7), channel_id=1, source_target_pairs={{0,1},{1,0},{2,3},{3,2},{4,5},{5,4},{6,7},{7,6},{8,9},{9,8},{10,11... | collective-permute-start | bytes 786440 | tf_op jit(solution)/shard_map/ppermute | solution.py:350
  154.6 5.6 %copy-start.6 = (bf16[8,256,256]{2,1,0:T(8,128)(2,1)}, bf16[8,256,256]{2,1,0:T(8,128)(2,1)S(1)}, u32[]{:S(2)}) copy-start(bf16[8,256,256]{2,1,0:T(8,128)(2,1)S(1)} %collective-permute-done.10.refs_1_) | copy-start | bytes 3145732
  180.0 24.2 %slice-start = ((bf16[256,512]{1,0:T(8,128)(2,1)}), bf16[256,256]{1,0:T(8,128)(2,1)S(1)}, s32[]{:S(2)}) async-start(bf16[256,512]{1,0:T(8,128)(2,1)} %copy-done.3), calls=%async_computation.6 | async-start | bytes 262144 | tf_op jit(solution)/shard_map/slice | solution.py:356
  180.0 17.4 %all-to-all-start.4 = ((bf16[32,36,128]{2,1,0:T(8,128)(2,1)}), bf16[32,36,128]{2,1,0:T(8,128)(2,1)S(1)}, u32[]{:S(2)}, u32[]{:S(2)}) async-start(bf16[32,36,128]{2,1,0:T(8,128)(2,1)} %bitcast.24), calls=%async_computation.4 | async-start | bytes 655360 | tf_op jit(solution)/shard_map/all_to_all | solution.py:25
  184.8 19.5 %collective-permute-start.9 = (bf16[256,256]{1,0:T(8,128)(2,1)S(1)}, bf16[256,256]{1,0:T(8,128)(2,1)S(1)}, u32[]{:S(2)}, u32[]{:S(2)}) collective-permute-start(bf16[256,256]{1,0:T(8,128)(2,1)S(1)} %get-tuple-element.41), channel_id=1, source_target_pairs={{1,2},{2,1},{3,0},{0,3},{5,6},{6,5},{7,4},{4,7},{9,10},{10,9},{11,... | collective-permute-start | bytes 393224 | tf_op jit(solution)/shard_map/ppermute | solution.py:352
  189.1 15.1 %collective-permute-start.8 = (bf16[256,256]{1,0:T(8,128)(2,1)S(1)}, bf16[256,256]{1,0:T(8,128)(2,1)S(1)}, u32[]{:S(2)}, u32[]{:S(2)}) collective-permute-start(bf16[256,256]{1,0:T(8,128)(2,1)S(1)} %get-tuple-element.39), channel_id=1, source_target_pairs={{0,2},{1,3},{2,0},{3,1},{4,6},{5,7},{6,4},{7,5},{8,10},{9,11},{10,... | collective-permute-start | bytes 393224 | tf_op jit(solution)/shard_map/ppermute | solution.py:351
  198.2 15.6 %all-to-all-start.5 = ((bf16[16,36,128]{2,1,0:T(8,128)(2,1)}), bf16[16,36,128]{2,1,0:T(8,128)(2,1)S(1)}, u32[]{:S(2)}, u32[]{:S(2)}) async-start(bf16[16,36,128]{2,1,0:T(8,128)(2,1)} %broadcast_in_dim.35), calls=%async_computation.5 | async-start | bytes 327680 | tf_op jit(solution)/shard_map/all_to_all | solution.py:25
  204.2 11.0 %copy-start.2 = (bf16[2,4,128,256]{3,2,1,0:T(8,128)(2,1)}, bf16[2,4,128,256]{3,2,1,0:T(8,128)(2,1)S(1)}, u32[]{:S(2)}) copy-start(bf16[2,4,128,256]{3,2,1,0:T(8,128)(2,1)S(1)} %constant_dynamic-update-slice_fusion) | copy-start | bytes 1572868
  (3 other events, 2.1 us)

commit v7 on v6

--- a/solution.py
+++ b/solution.py
@@ -143,36 +143,32 @@
 
 def project_kernel(core_ref, att_ref, weight_ref, keep_ref, send_ref, all_ref):
     steps, tokens, width = att_ref.shape
+    blocks, _, rows = weight_ref.shape
     half = tokens // 2
-    total = None
-    for z in range(steps):
-        part = jnp.dot(
-            att_ref[z], weight_ref[z * width : (z + 1) * width, :], preferred_element_type=f32
-        )
-        total = part if total is None else total + part
-    all_ref[...] = total
-    keep_ref[...] = all_ref[pl.ds(pl.multiple_of(core_ref[0] * half, half), half), :]
-    send_ref[...] = all_ref[pl.ds(pl.multiple_of((1 - core_ref[0]) * half, half), half), :]
+    for i in range(blocks):
+        total = None
+        for z in range(steps):
+            tile = weight_ref[i, z * width : (z + 1) * width, :]
+            part = jnp.dot(att_ref[z], tile, preferred_element_type=f32)
+            total = part if total is None else total + part
+        all_ref[...] = total
+        columns = slice(i * rows, (i + 1) * rows)
+        for out_ref, who in ((keep_ref, core_ref[0]), (send_ref, 1 - core_ref[0])):
+            out_ref[:, columns] = all_ref[pl.ds(pl.multiple_of(who * half, half), half), :]
 
 
 def project(core, attended, weight):
     _, tokens, _ = attended.shape
-    blocks, depth, rows = weight.shape
+    blocks, _, rows = weight.shape
     out = jax.ShapeDtypeStruct((tokens // 2, blocks * rows), f32)
-    out_spec = pl.BlockSpec((tokens // 2, rows), lambda i, core: (0, i))
+    whole = pl.BlockSpec(memory_space=pltpu.VMEM)
     return pl.pallas_call(
         project_kernel,
-        grid_spec=pltpu.PrefetchScalarGridSpec(
-            num_scalar_prefetch=1,
-            grid=(blocks,),
-            in_specs=[
-                pl.BlockSpec(memory_space=pltpu.VMEM),
-                pl.BlockSpec((None, depth, rows), lambda i, core: (i, 0, 0)),
-            ],
-            out_specs=[out_spec, out_spec],
-            scratch_shapes=[pltpu.VMEM((tokens, rows), f32)],
-        ),
+        in_specs=[pl.BlockSpec(memory_space=pltpu.SMEM), whole, whole],
+        out_specs=[whole, whole],
         out_shape=[out, out],
+        scratch_shapes=[pltpu.VMEM((tokens, rows), f32)],
+        compiler_params=pltpu.CompilerParams(vmem_limit_bytes=14 << 20),
         name="project",
     )(core, attended, weight)
 
@@ -264,6 +260,7 @@
         cost_estimate=pl.CostEstimate(
             flops=blocks * 4_000_000_000, transcendentals=0, bytes_accessed=blocks * 1_000_000
         ),
+        compiler_params=pltpu.CompilerParams(vmem_limit_bytes=16 << 20),
         name="bins",
     )(own[0], theirs[0], own[1], theirs[1], plan)
 
@@ -341,13 +338,19 @@
     output = jnp.sum(parts.astype(f32), axis=0)
     misfit_share = (output - plan[:, groups + 8 :].transpose(1, 0, 2).reshape(share, -1)).astype(bf16)
     misfit_half = copies(misfit_share, "col_0").reshape(tok_rows, -1)
+    even = across % 2 == 0
+
+    def pairs_blocks(array):
+        second, fourth = array[:, rows : 2 * rows], array[:, 3 * rows :]
+        return jnp.where(even, second, fourth), jnp.where(even, fourth, second)
+
     other_half = swap(misfit_half, "col_1")
+    their_half = lax.ppermute(jnp.concatenate(pairs_blocks(misfit_half), axis=1), "tok_1", pair)
     misfit = jnp.concatenate(in_order(misfit_half, other_half, core), axis=0)
-
-    even = across % 2 == 0
+    their_other = swap(their_half, "col_1")
+    their_misfit = jnp.concatenate(in_order(their_half, their_other, core), axis=0)
     blocks = [misfit[:, k * rows : (k + 1) * rows] for k in range(count_across)]
-    pairs_own, pairs_next = jnp.where(even, blocks[1], blocks[3]), jnp.where(even, blocks[3], blocks[1])
-    their_misfit = lax.ppermute(jnp.concatenate([pairs_own, pairs_next], axis=1), "tok_1", pair)
+    pairs_next = pairs_blocks(misfit)[1]
     from_across = lax.ppermute(blocks[2], "tok_1", [(0, 2), (1, 3), (2, 0), (3, 1)])
     from_beside = lax.ppermute(pairs_next, "tok_1", [(1, 2), (2, 1), (3, 0), (0, 3)])
     step = jnp.where(even, 1, count_across - 1)

time: 217 us -> 201 us (0.926)
  starting transfers between devices: 78.4 us -> 89.1 us
  waiting for transfers between devices: 60.2 us -> 50.6 us
  blocking collectives: 9.38 us -> 0 us
  Pallas kernels: 45.3 us -> 39.1 us
    all_to_all x1 -> x0, blocking collectives: 9.38 us -> none  [exchange(): return lax.all_to_all(pieces, axis, 0, 0, tiled=True)]
    ppermute x1, waiting for transfers between devices: 19.3 us -> 10.2 us  [device_part(): their_attended = lax.ppermute(attended, 'tok_1', pair)]
    all_to_all x5 -> x6, starting transfers between devices: 29.1 us -> 34.6 us  [exchange(): return lax.all_to_all(pieces, axis, 0, 0, tiled=True)]
    ppermute x1, waiting for transfers between devices: 5.61 us -> 0.64 us  [device_part(): lax.ppermute(jnp.concatenate(pairs_blocks(misfit_half), axis=1), 'tok_1',...]
    ppermute x4 -> x5, starting transfers between devices: 29.4 us -> 34 us  [swap(): return lax.ppermute(array, axis, [(0, 1), (1, 0)])]
    all_to_all x5 -> x6, waiting for transfers between devices: 33.5 us -> 37.6 us  [exchange(): return lax.all_to_all(pieces, axis, 0, 0, tiled=True)]
    pallas_call x1, Pallas kernels: 5.16 us -> 1.35 us  [project(): pl.pallas_call(project_kernel, in_specs=[pl.BlockSpec(memory_space=pltpu....]
    pallas_call x1, Pallas kernels: 17.3 us -> 15 us  [bin_gradients(): pl.pallas_call(lambda *refs: bins_kernel(scaling, *refs), grid=(blocks //...]
  transfers between devices with their start and end apart: 16 -> 18, of which waited for: 8 -> 10; matrix products, arithmetic and copies ran while one was open for 4% -> 3% of each run, Pallas kernels for 11% -> 11%
where the time goes in v7:
time: 201 us; the launch traced here: 200 us
  starting transfers between devices  89.1 us (44%)
  waiting for transfers between devices  50.6 us (25%)
  Pallas kernels  39.1 us (19%)
  local copies, waits for them, and re-layouts  12.5 us (6%)
  other arithmetic  6.56 us (3%)
    all_to_all x6, waiting for transfers between devices, exchange(): return lax.all_to_all(pieces, axis, 0, 0, tiled=True)  37.6 us
    all_to_all x6, starting transfers between devices, exchange(): return lax.all_to_all(pieces, axis, 0, 0, tiled=True)  34.6 us
    ppermute x5, starting transfers between devices, swap(): return lax.ppermute(array, axis, [(0, 1), (1, 0)])  34 us
    pallas_call x4, Pallas kernels, dequantize(): pl.pallas_call(dequant_kernel, grid=(1,), in_specs=[pl.BlockSpec(memory_s...  22.8 us
    pallas_call x1, Pallas kernels, bin_gradients(): pl.pallas_call(lambda *refs: bins_kernel(scaling, *refs), grid=(blocks //...  15 us
    ppermute x1, waiting for transfers between devices, device_part(): their_attended = lax.ppermute(attended, 'tok_1', pair)  10.2 us
    ppermute x3, starting transfers between devices, device_part(): received.append(lax.ppermute(sent, 'tok_1', route))  7.8 us
    unnamed x36, local copies, waits for them, and re-layouts  7.02 us
  transfers between devices with their start and end apart: 18, of which 10 were waited for; matrix products, arithmetic and copies ran while one was open for 3% of the time, Pallas kernels for 11%

profile of v7, /device:TPU:1, one launch (start us, length us, event | category | flops | bytes accessed | tf_op | source)
XLA Modules:
  0.0 200.1 jit_solution(9725425103046572616)
XLA Ops:
  2.3 8.3 %collective-permute-start = (bf16[128,384]{1,0:T(8,128)(2,1)S(1)}, bf16[128,384]{1,0:T(8,128)(2,1)S(1)}, u32[]{:S(2)}, u32[]{:S(2)}) collective-permute-start(bf16[128,384]{1,0:T(8,128)(2,1)S(1)} %pad_maximum_fusion.12), channel_id=1, source_target_pairs={{0,4},{4,0},{1,5},{5,1},{2,6},{6,2},{3,7},{7,3},{8,12},{12,8},{9,1... | collective-permute-start | bytes 294920 | tf_op jit(solution)/shard_map/ppermute | solution.py:39
  13.8 4.0 %all-to-all-start = ((bf16[4,256,256]{2,1,0:T(8,128)(2,1)}), bf16[4,256,256]{2,1,0:T(8,128)(2,1)S(1)}, u32[]{:S(2)}, u32[]{:S(2)}) async-start(bf16[4,256,256]{2,1,0:T(8,128)(2,1)} %broadcast_in_dim.27), calls=%async_computation | async-start | bytes 1048576 | tf_op jit(solution)/shard_map/all_to_all | solution.py:25
  18.8 6.0 %all-to-all-done = bf16[4,256,256]{2,1,0:T(8,128)(2,1)S(1)} async-done(((bf16[4,256,256]{2,1,0:T(8,128)(2,1)}), bf16[4,256,256]{2,1,0:T(8,128)(2,1)S(1)}, u32[]{:S(2)}, u32[]{:S(2)}) %all-to-all-start) | async-done | bytes 524320 | tf_op jit(solution)/shard_map/all_to_all | solution.py:25
  26.0 9.0 %collective-permute-start.1 = (bf16[256,128]{0,1:T(8,128)(2,1)S(1)}, bf16[256,128]{0,1:T(8,128)(2,1)S(1)}, u32[]{:S(2)}, u32[]{:S(2)}) collective-permute-start(bf16[256,128]{0,1:T(8,128)(2,1)S(1)} %fusion), channel_id=1, source_target_pairs={{0,4},{4,0},{1,5},{5,1},{2,6},{6,2},{3,7},{7,3},{8,12},{12,8},{9,1... | collective-permute-start | bytes 196616 | tf_op jit(solution)/shard_map/ppermute | solution.py:39
  35.1 5.7 %dequant.4 = (bf16[4,2048,256]{2,1,0:T(8,128)(2,1)}, f32[4,296,256]{2,1,0:T(8,128)}) custom-call(f32[296,256]{1,0:T(8,128)} %get-tuple-element.44.block_ref, bf16[8,256]{1,0:T(8,128)(2,1)} %bitcast.74, bf16[8,256]{1,0:T(8,128)(2,1)} %bitcast.78), custom_call_target="tpu_custom_call" | custom-call | flops 8000000000 | bytes 1500000 | tf_op jit(solution)/shard_map/dequant/pallas_call | solution.py:118
  49.8 8.0 %all-to-all-start.1 = ((bf16[8,256,256]{2,1,0:T(8,128)(2,1)}), bf16[8,256,256]{2,1,0:T(8,128)(2,1)S(1)}, u32[]{:S(2)}, u32[]{:S(2)}) async-start(bf16[8,256,256]{2,1,0:T(8,128)(2,1)} %broadcast_in_dim.30), calls=%async_computation.1 | async-start | bytes 2097152 | tf_op jit(solution)/shard_map/all_to_all | solution.py:25
  58.5 5.7 %dequant.5 = (bf16[4,2048,256]{2,1,0:T(8,128)(2,1)}, f32[4,296,256]{2,1,0:T(8,128)}) custom-call(f32[296,256]{1,0:T(8,128)} %copy-done.15, bf16[8,256]{1,0:T(8,128)(2,1)} %bitcast.75, bf16[8,256]{1,0:T(8,128)(2,1)} %bitcast.79, bf16[4,2048,256]{2,1,0:T(8,128)(2,1)} %get-tuple-element.19.refs_0_, ...), custom_call_target="tpu_custom_call", output_to_operand_aliasing={{0}: (3, {}), {1}: (4, {})} | custom-call | flops 8000000000 | bytes 1500000 | tf_op jit(solution)/shard_map/dequant/pallas_call | solution.py:118
  64.9 5.7 %dequant.6 = (bf16[4,2048,256]{2,1,0:T(8,128)(2,1)}, f32[4,296,256]{2,1,0:T(8,128)}) custom-call(f32[296,256]{1,0:T(8,128)} %copy-done.14, bf16[8,256]{1,0:T(8,128)(2,1)} %bitcast.76, bf16[8,256]{1,0:T(8,128)(2,1)} %bitcast.80, bf16[4,2048,256]{2,1,0:T(8,128)(2,1)} %get-tuple-element.21.refs_0_, ...), custom_call_target="tpu_custom_call", output_to_operand_aliasing={{0}: (3, {}), {1}: (4, {})} | custom-call | flops 8000000000 | bytes 1500000 | tf_op jit(solution)/shard_map/dequant/pallas_call | solution.py:118
  71.3 5.7 %dequant.7 = (bf16[4,2048,256]{2,1,0:T(8,128)(2,1)}, f32[4,296,256]{2,1,0:T(8,128)}) custom-call(f32[296,256]{1,0:T(8,128)} %copy-done.13, bf16[8,256]{1,0:T(8,128)(2,1)} %bitcast.77, bf16[8,256]{1,0:T(8,128)(2,1)} %bitcast.81, bf16[4,2048,256]{2,1,0:T(8,128)(2,1)} %get-tuple-element.23.refs_0_, ...), custom_call_target="tpu_custom_call", output_to_operand_aliasing={{0}: (3, {}), {1}: (4, {})} | custom-call | flops 8000000000 | bytes 1500000 | tf_op jit(solution)/shard_map/dequant/pallas_call | solution.py:118
  77.0 5.9 %all-to-all-done.1.att_ref.refs_0_ = bf16[8,256,256]{2,1,0:T(8,128)(2,1)S(1)} async-done(((bf16[8,256,256]{2,1,0:T(8,128)(2,1)}), bf16[8,256,256]{2,1,0:T(8,128)(2,1)S(1)}, u32[]{:S(2)}, u32[]{:S(2)}) %all-to-all-start.1) | async-done | bytes 1048608 | tf_op jit(solution)/shard_map/all_to_all | solution.py:25
  86.4 6.6 %collective-permute-start.5 = (f32[128,1024]{1,0:T(8,128)S(1)}, f32[128,1024]{1,0:T(8,128)S(1)}, u32[]{:S(2)}, u32[]{:S(2)}) collective-permute-start(f32[128,1024]{1,0:T(8,128)S(1)} %get-tuple-element.27), channel_id=1, source_target_pairs={{0,64},{64,0},{1,65},{65,1},{2,66},{66,2},{3,67},{67,3},{4,68},{68... | collective-permute-start | bytes 1572872 | tf_op jit(solution)/shard_map/ppermute | solution.py:39
  95.4 6.2 %all-to-all-start.2 = ((bf16[4,32,1024]{2,1,0:T(8,128)(2,1)}), bf16[4,32,1024]{2,1,0:T(8,128)(2,1)S(1)}, u32[]{:S(2)}, u32[]{:S(2)}) async-start(bf16[4,32,1024]{2,1,0:T(8,128)(2,1)} %bitcast.12), calls=%async_computation.2 | async-start | bytes 524288 | tf_op jit(solution)/shard_map/all_to_all | solution.py:25
  101.6 7.4 %all-to-all-done.2 = bf16[4,32,1024]{2,1,0:T(8,128)(2,1)S(1)} async-done(((bf16[4,32,1024]{2,1,0:T(8,128)(2,1)}), bf16[4,32,1024]{2,1,0:T(8,128)(2,1)S(1)}, u32[]{:S(2)}, u32[]{:S(2)}) %all-to-all-start.2) | async-done | bytes 262176 | tf_op jit(solution)/shard_map/all_to_all | solution.py:25
  109.8 3.4 %all-to-all-start.3 = ((bf16[4,32,1024]{2,1,0:T(8,128)(2,1)}), bf16[4,32,1024]{2,1,0:T(8,128)(2,1)S(1)}, u32[]{:S(2)}, u32[]{:S(2)}) async-start(bf16[4,32,1024]{2,1,0:T(8,128)(2,1)} %broadcast_in_dim.32), calls=%async_computation.3 | async-start | bytes 524288 | tf_op jit(solution)/shard_map/all_to_all | solution.py:25
  113.3 5.6 %all-to-all-done.3 = bf16[4,32,1024]{2,1,0:T(8,128)(2,1)S(1)} async-done(((bf16[4,32,1024]{2,1,0:T(8,128)(2,1)}), bf16[4,32,1024]{2,1,0:T(8,128)(2,1)S(1)}, u32[]{:S(2)}, u32[]{:S(2)}) %all-to-all-start.3) | async-done | bytes 262176 | tf_op jit(solution)/shard_map/all_to_all | solution.py:25
  119.7 3.4 %collective-permute-start.7 = (bf16[128,512]{1,0:T(8,128)(2,1)}, bf16[128,512]{1,0:T(8,128)(2,1)}, u32[]{:S(2)}, u32[]{:S(2)}) collective-permute-start(bf16[128,512]{1,0:T(8,128)(2,1)} %pad_maximum_fusion.10), channel_id=1, source_target_pairs={{0,1},{1,0},{2,3},{3,2},{4,5},{5,4},{6,7},{7,6},{8,9},{9,8},{10,11... | collective-permute-start | bytes 393224 | tf_op jit(solution)/shard_map/ppermute | solution.py:348
  125.7 8.1 %collective-permute-start.8 = (bf16[128,512]{1,0:T(8,128)(2,1)}, bf16[128,512]{1,0:T(8,128)(2,1)S(1)}, u32[]{:S(2)}, u32[]{:S(2)}) collective-permute-start(bf16[128,512]{1,0:T(8,128)(2,1)} %collective-permute-done.7), channel_id=1, source_target_pairs={{0,64},{64,0},{1,65},{65,1},{2,66},{66,2},{3,67},{67,3},{4,68},{68... | collective-permute-start | bytes 393224 | tf_op jit(solution)/shard_map/ppermute | solution.py:39
  138.4 10.2 %collective-permute-done.11.refs_1_ = bf16[8,256,256]{2,1,0:T(8,128)(2,1)S(1)} collective-permute-done((bf16[8,256,256]{2,1,0:T(8,128)(2,1)S(1)}, bf16[8,256,256]{2,1,0:T(8,128)(2,1)S(1)}, u32[]{:S(2)}, u32[]{:S(2)}) %collective-permute-start.11) | collective-permute-done | bytes 1048608 | tf_op jit(solution)/shard_map/ppermute | solution.py:335
  148.5 15.0 %bins.1 = f32[2,32,64]{2,1,0:T(8,128)S(1)} custom-call(bf16[8,256,256]{2,1,0:T(8,128)(2,1)S(1)} %all-to-all-done.1.att_ref.refs_0_, bf16[8,256,256]{2,1,0:T(8,128)(2,1)S(1)} %collective-permute-done.11.refs_1_, bf16[256,1024]{1,0:T(8,128)(2,1)S(1)} %pad_maximum_fusion.refs_2_, bf16[256,512]{1,0:T(8,128)(2,1)S(1)} %pad_maximum_fusion.7.refs_3_, ...), custom_call_target="tpu_custom_call" | custom-call | flops 16000000000 | bytes 4000000 | tf_op jit(solution)/shard_map/bins/pallas_call | solution.py:244
  164.4 4.1 %all-to-all-start.4 = ((bf16[32,36,128]{2,1,0:T(8,128)(2,1)}), bf16[32,36,128]{2,1,0:T(8,128)(2,1)S(1)}, u32[]{:S(2)}, u32[]{:S(2)}) async-start(bf16[32,36,128]{2,1,0:T(8,128)(2,1)} %bitcast.24), calls=%async_computation.4 | async-start | bytes 655360 | tf_op jit(solution)/shard_map/all_to_all | solution.py:25
  168.6 4.6 %collective-permute-start.9 = (bf16[256,256]{1,0:T(8,128)(2,1)S(1)}, bf16[256,256]{1,0:T(8,128)(2,1)S(1)}, u32[]{:S(2)}, u32[]{:S(2)}) collective-permute-start(bf16[256,256]{1,0:T(8,128)(2,1)S(1)} %get-tuple-element.40), channel_id=1, source_target_pairs={{0,2},{1,3},{2,0},{3,1},{4,6},{5,7},{6,4},{7,5},{8,10},{9,11},{10,... | collective-permute-start | bytes 393224 | tf_op jit(solution)/shard_map/ppermute | solution.py:354
  176.2 3.2 %all-to-all-done.4 = bf16[32,36,128]{2,1,0:T(8,128)(2,1)S(1)} async-done(((bf16[32,36,128]{2,1,0:T(8,128)(2,1)}), bf16[32,36,128]{2,1,0:T(8,128)(2,1)S(1)}, u32[]{:S(2)}, u32[]{:S(2)}) %all-to-all-start.4) | async-done | bytes 294944 | tf_op jit(solution)/shard_map/all_to_all | solution.py:25
  180.1 8.9 %all-to-all-start.5 = ((bf16[16,36,128]{2,1,0:T(8,128)(2,1)}), bf16[16,36,128]{2,1,0:T(8,128)(2,1)S(1)}, u32[]{:S(2)}, u32[]{:S(2)}) async-start(bf16[16,36,128]{2,1,0:T(8,128)(2,1)} %broadcast_in_dim.35), calls=%async_computation.5 | async-start | bytes 327680 | tf_op jit(solution)/shard_map/all_to_all | solution.py:25
  189.1 9.5 %all-to-all-done.5 = bf16[16,36,128]{2,1,0:T(8,128)(2,1)S(1)} async-done(((bf16[16,36,128]{2,1,0:T(8,128)(2,1)}), bf16[16,36,128]{2,1,0:T(8,128)(2,1)S(1)}, u32[]{:S(2)}, u32[]{:S(2)}) %all-to-all-start.5) | async-done | bytes 147488 | tf_op jit(solution)/shard_map/all_to_all | solution.py:25
  (115 shorter events, 38.6 us)
Async XLA Ops:
  0.6 11.1 %copy-start.11 = (s32[256,256]{1,0:T(8,128)S(1)}, s32[256,256]{1,0:T(8,128)}, u32[]{:S(2)}) copy-start(s32[256,256]{1,0:T(8,128)} %param.12) | copy-start | bytes 786436
  2.3 10.6 %collective-permute-start = (bf16[128,384]{1,0:T(8,128)(2,1)S(1)}, bf16[128,384]{1,0:T(8,128)(2,1)S(1)}, u32[]{:S(2)}, u32[]{:S(2)}) collective-permute-start(bf16[128,384]{1,0:T(8,128)(2,1)S(1)} %pad_maximum_fusion.12), channel_id=1, source_target_pairs={{0,4},{4,0},{1,5},{5,1},{2,6},{6,2},{3,7},{7,3},{8,12},{12,8},{9,1... | collective-permute-start | bytes 294920 | tf_op jit(solution)/shard_map/ppermute | solution.py:39
  13.8 11.0 %all-to-all-start = ((bf16[4,256,256]{2,1,0:T(8,128)(2,1)}), bf16[4,256,256]{2,1,0:T(8,128)(2,1)S(1)}, u32[]{:S(2)}, u32[]{:S(2)}) async-start(bf16[4,256,256]{2,1,0:T(8,128)(2,1)} %broadcast_in_dim.27), calls=%async_computation | async-start | bytes 1048576 | tf_op jit(solution)/shard_map/all_to_all | solution.py:25
  26.0 22.5 %collective-permute-start.1 = (bf16[256,128]{0,1:T(8,128)(2,1)S(1)}, bf16[256,128]{0,1:T(8,128)(2,1)S(1)}, u32[]{:S(2)}, u32[]{:S(2)}) collective-permute-start(bf16[256,128]{0,1:T(8,128)(2,1)S(1)} %fusion), channel_id=1, source_target_pairs={{0,4},{4,0},{1,5},{5,1},{2,6},{6,2},{3,7},{7,3},{8,12},{12,8},{9,1... | collective-permute-start | bytes 196616 | tf_op jit(solution)/shard_map/ppermute | solution.py:39
  40.7 17.0 %collective-permute-start.4 = (f32[296,256]{1,0:T(8,128)S(1)}, f32[296,256]{1,0:T(8,128)S(1)}, u32[]{:S(2)}, u32[]{:S(2)}) collective-permute-start(f32[296,256]{1,0:T(8,128)S(1)} %get-tuple-element.18), channel_id=1, source_target_pairs={{1,0},{2,1},{3,2},{0,3},{5,4},{6,5},{7,6},{4,7},{9,8},{10,9},{11,1... | collective-permute-start | bytes 909320 | tf_op jit(solution)/shard_map/ppermute | solution.py:329
  43.6 20.6 %collective-permute-start.3 = (f32[296,256]{1,0:T(8,128)S(1)}, f32[296,256]{1,0:T(8,128)S(1)}, u32[]{:S(2)}, u32[]{:S(2)}) collective-permute-start(f32[296,256]{1,0:T(8,128)S(1)} %get-tuple-element.17), channel_id=1, source_target_pairs={{2,0},{3,1},{0,2},{1,3},{6,4},{7,5},{4,6},{5,7},{10,8},{11,9},{8,1... | collective-permute-start | bytes 909320 | tf_op jit(solution)/shard_map/ppermute | solution.py:329
  46.6 24.0 %collective-permute-start.2 = (f32[296,256]{1,0:T(8,128)S(1)}, f32[296,256]{1,0:T(8,128)S(1)}, u32[]{:S(2)}, u32[]{:S(2)}) collective-permute-start(f32[296,256]{1,0:T(8,128)S(1)} %get-tuple-element.16), channel_id=1, source_target_pairs={{3,0},{0,1},{1,2},{2,3},{7,4},{4,5},{5,6},{6,7},{11,8},{8,9},{9,10... | collective-permute-start | bytes 909320 | tf_op jit(solution)/shard_map/ppermute | solution.py:329
  49.8 33.1 %all-to-all-start.1 = ((bf16[8,256,256]{2,1,0:T(8,128)(2,1)}), bf16[8,256,256]{2,1,0:T(8,128)(2,1)S(1)}, u32[]{:S(2)}, u32[]{:S(2)}) async-start(bf16[8,256,256]{2,1,0:T(8,128)(2,1)} %broadcast_in_dim.30), calls=%async_computation.1 | async-start | bytes 2097152 | tf_op jit(solution)/shard_map/all_to_all | solution.py:25
  86.4 15.2 %copy-start.1 = (f32[4,296,256]{2,1,0:T(8,128)S(1)}, f32[4,296,256]{2,1,0:T(8,128)}, u32[]{:S(2)}) copy-start(f32[4,296,256]{2,1,0:T(8,128)} %get-tuple-element.28.refs_4_) | copy-start | bytes 3637252
  86.4 8.2 %collective-permute-start.5 = (f32[128,1024]{1,0:T(8,128)S(1)}, f32[128,1024]{1,0:T(8,128)S(1)}, u32[]{:S(2)}, u32[]{:S(2)}) collective-permute-start(f32[128,1024]{1,0:T(8,128)S(1)} %get-tuple-element.27), channel_id=1, source_target_pairs={{0,64},{64,0},{1,65},{65,1},{2,66},{66,2},{3,67},{67,3},{4,68},{68... | collective-permute-start | bytes 1572872 | tf_op jit(solution)/shard_map/ppermute | solution.py:39
  95.4 13.7 %all-to-all-start.2 = ((bf16[4,32,1024]{2,1,0:T(8,128)(2,1)}), bf16[4,32,1024]{2,1,0:T(8,128)(2,1)S(1)}, u32[]{:S(2)}, u32[]{:S(2)}) async-start(bf16[4,32,1024]{2,1,0:T(8,128)(2,1)} %bitcast.12), calls=%async_computation.2 | async-start | bytes 524288 | tf_op jit(solution)/shard_map/all_to_all | solution.py:25
  109.8 9.1 %all-to-all-start.3 = ((bf16[4,32,1024]{2,1,0:T(8,128)(2,1)}), bf16[4,32,1024]{2,1,0:T(8,128)(2,1)S(1)}, u32[]{:S(2)}, u32[]{:S(2)}) async-start(bf16[4,32,1024]{2,1,0:T(8,128)(2,1)} %broadcast_in_dim.32), calls=%async_computation.3 | async-start | bytes 524288 | tf_op jit(solution)/shard_map/all_to_all | solution.py:25
  119.7 6.0 %collective-permute-start.7 = (bf16[128,512]{1,0:T(8,128)(2,1)}, bf16[128,512]{1,0:T(8,128)(2,1)}, u32[]{:S(2)}, u32[]{:S(2)}) collective-permute-start(bf16[128,512]{1,0:T(8,128)(2,1)} %pad_maximum_fusion.10), channel_id=1, source_target_pairs={{0,1},{1,0},{2,3},{3,2},{4,5},{5,4},{6,7},{7,6},{8,9},{9,8},{10,11... | collective-permute-start | bytes 393224 | tf_op jit(solution)/shard_map/ppermute | solution.py:348
  123.1 25.5 %collective-permute-start.11 = (bf16[8,256,256]{2,1,0:T(8,128)(2,1)S(1)}, bf16[8,256,256]{2,1,0:T(8,128)(2,1)S(1)}, u32[]{:S(2)}, u32[]{:S(2)}) collective-permute-start(bf16[8,256,256]{2,1,0:T(8,128)(2,1)S(1)} %all-to-all-done.1.att_ref.refs_0_), channel_id=1, source_target_pairs={{0,1},{1,0},{2,3},{3,2},{4,5},{5,4},{6,7},{7,6},{8,9},{9,8},{10,11... | collective-permute-start | bytes 3145736 | tf_op jit(solution)/shard_map/ppermute | solution.py:335
  125.1 12.5 %copy-start.7 = (bf16[4,32,1024]{2,1,0:T(8,128)(2,1)S(1)}, bf16[4,32,1024]{2,1,0:T(8,128)(2,1)}, u32[]{:S(2)}) copy-start(bf16[4,32,1024]{2,1,0:T(8,128)(2,1)} %copy-done.6) | copy-start | bytes 786436
  125.7 10.1 %collective-permute-start.8 = (bf16[128,512]{1,0:T(8,128)(2,1)}, bf16[128,512]{1,0:T(8,128)(2,1)S(1)}, u32[]{:S(2)}, u32[]{:S(2)}) collective-permute-start(bf16[128,512]{1,0:T(8,128)(2,1)} %collective-permute-done.7), channel_id=1, source_target_pairs={{0,64},{64,0},{1,65},{65,1},{2,66},{66,2},{3,67},{67,3},{4,68},{68... | collective-permute-start | bytes 393224 | tf_op jit(solution)/shard_map/ppermute | solution.py:39
  133.9 3.6 %collective-permute-start.6 = (bf16[128,1024]{1,0:T(8,128)(2,1)}, bf16[128,1024]{1,0:T(8,128)(2,1)S(1)}, u32[]{:S(2)}, u32[]{:S(2)}) collective-permute-start(bf16[128,1024]{1,0:T(8,128)(2,1)} %bitcast.58), channel_id=1, source_target_pairs={{0,64},{64,0},{1,65},{65,1},{2,66},{66,2},{3,67},{67,3},{4,68},{68... | collective-permute-start | bytes 786440 | tf_op jit(solution)/shard_map/ppermute | solution.py:39
  163.5 5.1 %copy-start.3 = (bf16[128,1024]{1,0:T(8,128)(2,1)S(1)}, bf16[128,1024]{1,0:T(8,128)(2,1)}, u32[]{:S(2)}) copy-start(bf16[128,1024]{1,0:T(8,128)(2,1)} %copy-done.2) | copy-start | bytes 786436
  163.7 12.4 %copy-start.9 = (bf16[128,512]{1,0:T(8,128)(2,1)S(1)}, bf16[128,512]{1,0:T(8,128)(2,1)}, u32[]{:S(2)}) copy-start(bf16[128,512]{1,0:T(8,128)(2,1)} %copy-done.8) | copy-start | bytes 393220
  164.4 14.9 %all-to-all-start.4 = ((bf16[32,36,128]{2,1,0:T(8,128)(2,1)}), bf16[32,36,128]{2,1,0:T(8,128)(2,1)S(1)}, u32[]{:S(2)}, u32[]{:S(2)}) async-start(bf16[32,36,128]{2,1,0:T(8,128)(2,1)} %bitcast.24), calls=%async_computation.4 | async-start | bytes 655360 | tf_op jit(solution)/shard_map/all_to_all | solution.py:25
  168.6 20.4 %collective-permute-start.9 = (bf16[256,256]{1,0:T(8,128)(2,1)S(1)}, bf16[256,256]{1,0:T(8,128)(2,1)S(1)}, u32[]{:S(2)}, u32[]{:S(2)}) collective-permute-start(bf16[256,256]{1,0:T(8,128)(2,1)S(1)} %get-tuple-element.40), channel_id=1, source_target_pairs={{0,2},{1,3},{2,0},{3,1},{4,6},{5,7},{6,4},{7,5},{8,10},{9,11},{10,... | collective-permute-start | bytes 393224 | tf_op jit(solution)/shard_map/ppermute | solution.py:354
  173.3 15.8 %collective-permute-start.10 = (bf16[256,256]{1,0:T(8,128)(2,1)S(1)}, bf16[256,256]{1,0:T(8,128)(2,1)S(1)}, u32[]{:S(2)}, u32[]{:S(2)}) collective-permute-start(bf16[256,256]{1,0:T(8,128)(2,1)S(1)} %get-tuple-element.39), channel_id=1, source_target_pairs={{1,2},{2,1},{3,0},{0,3},{5,6},{6,5},{7,4},{4,7},{9,10},{10,9},{11,... | collective-permute-start | bytes 393224 | tf_op jit(solution)/shard_map/ppermute | solution.py:355
  180.1 18.5 %all-to-all-start.5 = ((bf16[16,36,128]{2,1,0:T(8,128)(2,1)}), bf16[16,36,128]{2,1,0:T(8,128)(2,1)S(1)}, u32[]{:S(2)}, u32[]{:S(2)}) async-start(bf16[16,36,128]{2,1,0:T(8,128)(2,1)} %broadcast_in_dim.35), calls=%async_computation.5 | async-start | bytes 327680 | tf_op jit(solution)/shard_map/all_to_all | solution.py:25
  189.1 11.0 %copy-start.10 = (bf16[2,4,128,256]{3,2,1,0:T(8,128)(2,1)}, bf16[2,4,128,256]{3,2,1,0:T(8,128)(2,1)S(1)}, u32[]{:S(2)}) copy-start(bf16[2,4,128,256]{3,2,1,0:T(8,128)(2,1)S(1)} %constant_dynamic-update-slice_fusion) | copy-start | bytes 1572868
  (10 other events, 20.8 us)

commit v8 on v7

--- a/solution.py
+++ b/solution.py
@@ -338,19 +338,13 @@
     output = jnp.sum(parts.astype(f32), axis=0)
     misfit_share = (output - plan[:, groups + 8 :].transpose(1, 0, 2).reshape(share, -1)).astype(bf16)
     misfit_half = copies(misfit_share, "col_0").reshape(tok_rows, -1)
+    other_half = swap(misfit_half, "col_1")
+    misfit = jnp.concatenate(in_order(misfit_half, other_half, core), axis=0)
+
     even = across % 2 == 0
-
-    def pairs_blocks(array):
-        second, fourth = array[:, rows : 2 * rows], array[:, 3 * rows :]
-        return jnp.where(even, second, fourth), jnp.where(even, fourth, second)
-
-    other_half = swap(misfit_half, "col_1")
-    their_half = lax.ppermute(jnp.concatenate(pairs_blocks(misfit_half), axis=1), "tok_1", pair)
-    misfit = jnp.concatenate(in_order(misfit_half, other_half, core), axis=0)
-    their_other = swap(their_half, "col_1")
-    their_misfit = jnp.concatenate(in_order(their_half, their_other, core), axis=0)
     blocks = [misfit[:, k * rows : (k + 1) * rows] for k in range(count_across)]
-    pairs_next = pairs_blocks(misfit)[1]
+    pairs_own, pairs_next = jnp.where(even, blocks[1], blocks[3]), jnp.where(even, blocks[3], blocks[1])
+    their_misfit = lax.ppermute(jnp.concatenate([pairs_own, pairs_next], axis=1), "tok_1", pair)
     from_across = lax.ppermute(blocks[2], "tok_1", [(0, 2), (1, 3), (2, 0), (3, 1)])
     from_beside = lax.ppermute(pairs_next, "tok_1", [(1, 2), (2, 1), (3, 0), (0, 3)])
     step = jnp.where(even, 1, count_across - 1)

time: 201 us -> 210 us (1.045)
  waiting for transfers between devices: 50.6 us -> 62.5 us
  starting transfers between devices: 89.1 us -> 78.3 us
  blocking collectives: 0 us -> 9.38 us
    ppermute x1, waiting for transfers between devices: 10.2 us -> 21.1 us  [device_part(): their_attended = lax.ppermute(attended, 'tok_1', pair)]
    all_to_all x0 -> x1, blocking collectives: none -> 9.38 us  [exchange(): return lax.all_to_all(pieces, axis, 0, 0, tiled=True)]
    all_to_all x6 -> x5, starting transfers between devices: 34.6 us -> 28.8 us  [exchange(): return lax.all_to_all(pieces, axis, 0, 0, tiled=True)]
    ppermute x1, waiting for transfers between devices: 0.64 us -> 5.51 us  [device_part(): lax.ppermute(jnp.concatenate([pairs_own, pairs_next], axis=1), 'tok_1', p...]
    ppermute x5 -> x4, starting transfers between devices: 34 us -> 29.5 us  [swap(): return lax.ppermute(array, axis, [(0, 1), (1, 0)])]
    all_to_all x6 -> x5, waiting for transfers between devices: 37.6 us -> 34.4 us  [exchange(): return lax.all_to_all(pieces, axis, 0, 0, tiled=True)]
    ppermute x1, starting transfers between devices: 4.64 us -> 2.48 us  [device_part(): lax.ppermute(blocks[2], 'tok_1', [(0, 2), (1, 3), (2, 0), (3, 1)])]
    unnamed x36 -> x20, local copies, waits for them, and re-layouts: 7.02 us -> 6.28 us
  transfers between devices with their start and end apart: 18 -> 16, of which waited for: 10 -> 8; matrix products, arithmetic and copies ran while one was open for 3% -> 3% of each run, Pallas kernels for 11% -> 11%
where the time goes in v8:
time: 210 us; the launch traced here: 209 us
  starting transfers between devices  78.3 us (37%)
  waiting for transfers between devices  62.5 us (30%)
  Pallas kernels  40.3 us (19%)
  local copies, waits for them, and re-layouts  11.1 us (5%)
  blocking collectives  9.38 us (4%)
  other arithmetic  4.86 us (2%)
    all_to_all x5, waiting for transfers between devices, exchange(): return lax.all_to_all(pieces, axis, 0, 0, tiled=True)  34.4 us
    ppermute x4, starting transfers between devices, swap(): return lax.ppermute(array, axis, [(0, 1), (1, 0)])  29.5 us
    all_to_all x5, starting transfers between devices, exchange(): return lax.all_to_all(pieces, axis, 0, 0, tiled=True)  28.8 us
    pallas_call x4, Pallas kernels, dequantize(): pl.pallas_call(dequant_kernel, grid=(1,), in_specs=[pl.BlockSpec(memory_s...  22.8 us
    ppermute x1, waiting for transfers between devices, device_part(): their_attended = lax.ppermute(attended, 'tok_1', pair)  21.1 us
    pallas_call x1, Pallas kernels, bin_gradients(): pl.pallas_call(lambda *refs: bins_kernel(scaling, *refs), grid=(blocks //...  16.1 us
    all_to_all x1, blocking collectives, exchange(): return lax.all_to_all(pieces, axis, 0, 0, tiled=True)  9.38 us
    ppermute x3, starting transfers between devices, device_part(): received.append(lax.ppermute(sent, 'tok_1', route))  7.8 us
  transfers between devices with their start and end apart: 16, of which 8 were waited for; matrix products, arithmetic and copies ran while one was open for 3% of the time, Pallas kernels for 11%

profile of v8, /device:TPU:1, one launch (start us, length us, event | category | flops | bytes accessed | tf_op | source)
XLA Modules:
  0.0 208.6 jit_solution(10139462314249664771)
XLA Ops:
  2.3 8.3 %collective-permute-start = (bf16[128,384]{1,0:T(8,128)(2,1)S(1)}, bf16[128,384]{1,0:T(8,128)(2,1)S(1)}, u32[]{:S(2)}, u32[]{:S(2)}) collective-permute-start(bf16[128,384]{1,0:T(8,128)(2,1)S(1)} %pad_maximum_fusion.11), channel_id=1, source_target_pairs={{0,4},{4,0},{1,5},{5,1},{2,6},{6,2},{3,7},{7,3},{8,12},{12,8},{9,1... | collective-permute-start | bytes 294920 | tf_op jit(solution)/shard_map/ppermute | solution.py:39
  13.8 4.0 %all-to-all-start = ((bf16[4,256,256]{2,1,0:T(8,128)(2,1)}), bf16[4,256,256]{2,1,0:T(8,128)(2,1)S(1)}, u32[]{:S(2)}, u32[]{:S(2)}) async-start(bf16[4,256,256]{2,1,0:T(8,128)(2,1)} %broadcast_in_dim.27), calls=%async_computation | async-start | bytes 1048576 | tf_op jit(solution)/shard_map/all_to_all | solution.py:25
  18.8 6.0 %all-to-all-done = bf16[4,256,256]{2,1,0:T(8,128)(2,1)S(1)} async-done(((bf16[4,256,256]{2,1,0:T(8,128)(2,1)}), bf16[4,256,256]{2,1,0:T(8,128)(2,1)S(1)}, u32[]{:S(2)}, u32[]{:S(2)}) %all-to-all-start) | async-done | bytes 524320 | tf_op jit(solution)/shard_map/all_to_all | solution.py:25
  26.0 9.0 %collective-permute-start.1 = (bf16[256,128]{0,1:T(8,128)(2,1)S(1)}, bf16[256,128]{0,1:T(8,128)(2,1)S(1)}, u32[]{:S(2)}, u32[]{:S(2)}) collective-permute-start(bf16[256,128]{0,1:T(8,128)(2,1)S(1)} %fusion), channel_id=1, source_target_pairs={{0,4},{4,0},{1,5},{5,1},{2,6},{6,2},{3,7},{7,3},{8,12},{12,8},{9,1... | collective-permute-start | bytes 196616 | tf_op jit(solution)/shard_map/ppermute | solution.py:39
  35.1 5.7 %dequant.4 = (bf16[4,2048,256]{2,1,0:T(8,128)(2,1)}, f32[4,296,256]{2,1,0:T(8,128)}) custom-call(f32[296,256]{1,0:T(8,128)} %get-tuple-element.45.block_ref, bf16[8,256]{1,0:T(8,128)(2,1)} %bitcast.73, bf16[8,256]{1,0:T(8,128)(2,1)} %bitcast.77), custom_call_target="tpu_custom_call" | custom-call | flops 8000000000 | bytes 1500000 | tf_op jit(solution)/shard_map/dequant/pallas_call | solution.py:118
  49.8 8.0 %all-to-all-start.1 = ((bf16[8,256,256]{2,1,0:T(8,128)(2,1)}), bf16[8,256,256]{2,1,0:T(8,128)(2,1)S(1)}, u32[]{:S(2)}, u32[]{:S(2)}) async-start(bf16[8,256,256]{2,1,0:T(8,128)(2,1)} %broadcast_in_dim.30), calls=%async_computation.1 | async-start | bytes 2097152 | tf_op jit(solution)/shard_map/all_to_all | solution.py:25
  58.5 5.7 %dequant.5 = (bf16[4,2048,256]{2,1,0:T(8,128)(2,1)}, f32[4,296,256]{2,1,0:T(8,128)}) custom-call(f32[296,256]{1,0:T(8,128)} %copy-done.7, bf16[8,256]{1,0:T(8,128)(2,1)} %bitcast.74, bf16[8,256]{1,0:T(8,128)(2,1)} %bitcast.78, bf16[4,2048,256]{2,1,0:T(8,128)(2,1)} %get-tuple-element.19.refs_0_, ...), custom_call_target="tpu_custom_call", output_to_operand_aliasing={{0}: (3, {}), {1}: (4, {})} | custom-call | flops 8000000000 | bytes 1500000 | tf_op jit(solution)/shard_map/dequant/pallas_call | solution.py:118
  64.9 5.7 %dequant.6 = (bf16[4,2048,256]{2,1,0:T(8,128)(2,1)}, f32[4,296,256]{2,1,0:T(8,128)}) custom-call(f32[296,256]{1,0:T(8,128)} %copy-done.6, bf16[8,256]{1,0:T(8,128)(2,1)} %bitcast.75, bf16[8,256]{1,0:T(8,128)(2,1)} %bitcast.79, bf16[4,2048,256]{2,1,0:T(8,128)(2,1)} %get-tuple-element.21.refs_0_, ...), custom_call_target="tpu_custom_call", output_to_operand_aliasing={{0}: (3, {}), {1}: (4, {})} | custom-call | flops 8000000000 | bytes 1500000 | tf_op jit(solution)/shard_map/dequant/pallas_call | solution.py:118
  71.3 5.7 %dequant.7 = (bf16[4,2048,256]{2,1,0:T(8,128)(2,1)}, f32[4,296,256]{2,1,0:T(8,128)}) custom-call(f32[296,256]{1,0:T(8,128)} %copy-done.5, bf16[8,256]{1,0:T(8,128)(2,1)} %bitcast.76, bf16[8,256]{1,0:T(8,128)(2,1)} %bitcast.80, bf16[4,2048,256]{2,1,0:T(8,128)(2,1)} %get-tuple-element.23.refs_0_, ...), custom_call_target="tpu_custom_call", output_to_operand_aliasing={{0}: (3, {}), {1}: (4, {})} | custom-call | flops 8000000000 | bytes 1500000 | tf_op jit(solution)/shard_map/dequant/pallas_call | solution.py:118
  77.0 5.9 %all-to-all-done.1.att_ref.refs_0_ = bf16[8,256,256]{2,1,0:T(8,128)(2,1)S(1)} async-done(((bf16[8,256,256]{2,1,0:T(8,128)(2,1)}), bf16[8,256,256]{2,1,0:T(8,128)(2,1)S(1)}, u32[]{:S(2)}, u32[]{:S(2)}) %all-to-all-start.1) | async-done | bytes 1048608 | tf_op jit(solution)/shard_map/all_to_all | solution.py:25
  86.5 6.6 %collective-permute-start.5 = (f32[128,1024]{1,0:T(8,128)S(1)}, f32[128,1024]{1,0:T(8,128)S(1)}, u32[]{:S(2)}, u32[]{:S(2)}) collective-permute-start(f32[128,1024]{1,0:T(8,128)S(1)} %get-tuple-element.27), channel_id=1, source_target_pairs={{0,64},{64,0},{1,65},{65,1},{2,66},{66,2},{3,67},{67,3},{4,68},{68... | collective-permute-start | bytes 1572872 | tf_op jit(solution)/shard_map/ppermute | solution.py:39
  95.4 6.2 %all-to-all-start.2 = ((bf16[4,32,1024]{2,1,0:T(8,128)(2,1)}), bf16[4,32,1024]{2,1,0:T(8,128)(2,1)S(1)}, u32[]{:S(2)}, u32[]{:S(2)}) async-start(bf16[4,32,1024]{2,1,0:T(8,128)(2,1)} %bitcast.12), calls=%async_computation.2 | async-start | bytes 524288 | tf_op jit(solution)/shard_map/all_to_all | solution.py:25
  101.6 7.4 %all-to-all-done.2 = bf16[4,32,1024]{2,1,0:T(8,128)(2,1)S(1)} async-done(((bf16[4,32,1024]{2,1,0:T(8,128)(2,1)}), bf16[4,32,1024]{2,1,0:T(8,128)(2,1)S(1)}, u32[]{:S(2)}, u32[]{:S(2)}) %all-to-all-start.2) | async-done | bytes 262176 | tf_op jit(solution)/shard_map/all_to_all | solution.py:25
  109.1 9.4 %all_to_all.30 = bf16[4,32,1024]{2,1,0:T(8,128)(2,1)S(1)} all-to-all(bf16[4,32,1024]{2,1,0:T(8,128)(2,1)S(1)} %broadcast_in_dim.32), channel_id=1, replica_groups=mesh['col_0'=4,'col_1'=2,'row'=8,'tok_0'=2,'tok_1'=4] {'col_0'}, dimensions={0} | all-to-all | bytes 524288 | tf_op jit(solution)/shard_map/all_to_all | solution.py:25
  118.5 5.6 %collective-permute-start.6 = (bf16[128,1024]{1,0:T(8,128)(2,1)S(1)}, bf16[128,1024]{1,0:T(8,128)(2,1)S(1)}, u32[]{:S(2)}, u32[]{:S(2)}) collective-permute-start(bf16[128,1024]{1,0:T(8,128)(2,1)S(1)} %bitcast.59), channel_id=1, source_target_pairs={{0,64},{64,0},{1,65},{65,1},{2,66},{66,2},{3,67},{67,3},{4,68},{68... | collective-permute-start | bytes 786440 | tf_op jit(solution)/shard_map/ppermute | solution.py:39
  124.1 3.4 %collective-permute-start.10 = (bf16[8,256,256]{2,1,0:T(8,128)(2,1)S(1)}, bf16[8,256,256]{2,1,0:T(8,128)(2,1)}, u32[]{:S(2)}, u32[]{:S(2)}) collective-permute-start(bf16[8,256,256]{2,1,0:T(8,128)(2,1)S(1)} %all-to-all-done.1.att_ref.refs_0_), channel_id=1, source_target_pairs={{0,1},{1,0},{2,3},{3,2},{4,5},{5,4},{6,7},{7,6},{8,9},{9,8},{10,11... | collective-permute-start | bytes 3145736 | tf_op jit(solution)/shard_map/ppermute | solution.py:335
  129.7 21.1 %collective-permute-done.10.refs_1_ = bf16[8,256,256]{2,1,0:T(8,128)(2,1)} collective-permute-done((bf16[8,256,256]{2,1,0:T(8,128)(2,1)S(1)}, bf16[8,256,256]{2,1,0:T(8,128)(2,1)}, u32[]{:S(2)}, u32[]{:S(2)}) %collective-permute-start.10) | collective-permute-done | bytes 1048608 | tf_op jit(solution)/shard_map/ppermute | solution.py:335
  150.8 5.5 %collective-permute-done.7.refs_3_ = bf16[256,512]{1,0:T(8,128)(2,1)S(1)} collective-permute-done((bf16[256,512]{1,0:T(8,128)(2,1)S(1)}, bf16[256,512]{1,0:T(8,128)(2,1)S(1)}, u32[]{:S(2)}, u32[]{:S(2)}) %collective-permute-start.7) | collective-permute-done | bytes 262176 | tf_op jit(solution)/shard_map/ppermute | solution.py:347
  156.3 16.1 %bins.1 = f32[2,32,64]{2,1,0:T(8,128)S(1)} custom-call(bf16[8,256,256]{2,1,0:T(8,128)(2,1)S(1)} %all-to-all-done.1.att_ref.refs_0_, bf16[8,256,256]{2,1,0:T(8,128)(2,1)} %collective-permute-done.10.refs_1_, bf16[256,1024]{1,0:T(8,128)(2,1)S(1)} %pad_maximum_fusion.refs_2_, bf16[256,512]{1,0:T(8,128)(2,1)S(1)} %collective-permute-done.7.refs_3_, ...), custom_call_target="tpu_custom_call" | custom-call | flops 16000000000 | bytes 4000000 | tf_op jit(solution)/shard_map/bins/pallas_call | solution.py:244
  173.4 4.6 %all-to-all-start.4 = ((bf16[32,36,128]{2,1,0:T(8,128)(2,1)}), bf16[32,36,128]{2,1,0:T(8,128)(2,1)S(1)}, u32[]{:S(2)}, u32[]{:S(2)}) async-start(bf16[32,36,128]{2,1,0:T(8,128)(2,1)} %bitcast.24), calls=%async_computation.4 | async-start | bytes 655360 | tf_op jit(solution)/shard_map/all_to_all | solution.py:25
  178.1 4.3 %collective-permute-start.9 = (bf16[256,256]{1,0:T(8,128)(2,1)S(1)}, bf16[256,256]{1,0:T(8,128)(2,1)S(1)}, u32[]{:S(2)}, u32[]{:S(2)}) collective-permute-start(bf16[256,256]{1,0:T(8,128)(2,1)S(1)} %get-tuple-element.41), channel_id=1, source_target_pairs={{1,2},{2,1},{3,0},{0,3},{5,6},{6,5},{7,4},{4,7},{9,10},{10,9},{11,... | collective-permute-start | bytes 393224 | tf_op jit(solution)/shard_map/ppermute | solution.py:349
  185.0 5.7 %all-to-all-done.4 = bf16[32,36,128]{2,1,0:T(8,128)(2,1)S(1)} async-done(((bf16[32,36,128]{2,1,0:T(8,128)(2,1)}), bf16[32,36,128]{2,1,0:T(8,128)(2,1)S(1)}, u32[]{:S(2)}, u32[]{:S(2)}) %all-to-all-start.4) | async-done | bytes 294944 | tf_op jit(solution)/shard_map/all_to_all | solution.py:25
  191.5 6.0 %all-to-all-start.5 = ((bf16[16,36,128]{2,1,0:T(8,128)(2,1)}), bf16[16,36,128]{2,1,0:T(8,128)(2,1)S(1)}, u32[]{:S(2)}, u32[]{:S(2)}) async-start(bf16[16,36,128]{2,1,0:T(8,128)(2,1)} %broadcast_in_dim.35), calls=%async_computation.5 | async-start | bytes 327680 | tf_op jit(solution)/shard_map/all_to_all | solution.py:25
  197.5 9.5 %all-to-all-done.5 = bf16[16,36,128]{2,1,0:T(8,128)(2,1)S(1)} async-done(((bf16[16,36,128]{2,1,0:T(8,128)(2,1)}), bf16[16,36,128]{2,1,0:T(8,128)(2,1)S(1)}, u32[]{:S(2)}, u32[]{:S(2)}) %all-to-all-start.5) | async-done | bytes 147488 | tf_op jit(solution)/shard_map/all_to_all | solution.py:25
  (93 shorter events, 31.9 us)
Async XLA Ops:
  0.6 11.1 %copy-start.3 = (s32[256,256]{1,0:T(8,128)S(1)}, s32[256,256]{1,0:T(8,128)}, u32[]{:S(2)}) copy-start(s32[256,256]{1,0:T(8,128)} %param.12) | copy-start | bytes 786436
  2.3 10.6 %collective-permute-start = (bf16[128,384]{1,0:T(8,128)(2,1)S(1)}, bf16[128,384]{1,0:T(8,128)(2,1)S(1)}, u32[]{:S(2)}, u32[]{:S(2)}) collective-permute-start(bf16[128,384]{1,0:T(8,128)(2,1)S(1)} %pad_maximum_fusion.11), channel_id=1, source_target_pairs={{0,4},{4,0},{1,5},{5,1},{2,6},{6,2},{3,7},{7,3},{8,12},{12,8},{9,1... | collective-permute-start | bytes 294920 | tf_op jit(solution)/shard_map/ppermute | solution.py:39
  12.9 5.0 %copy-start.4 = (f32[256]{0:T(256)S(1)}, f32[256]{0:T(256)}, u32[]{:S(2)}) copy-start(f32[256]{0:T(256)} %param.16) | copy-start | bytes 3076
  13.8 11.0 %all-to-all-start = ((bf16[4,256,256]{2,1,0:T(8,128)(2,1)}), bf16[4,256,256]{2,1,0:T(8,128)(2,1)S(1)}, u32[]{:S(2)}, u32[]{:S(2)}) async-start(bf16[4,256,256]{2,1,0:T(8,128)(2,1)} %broadcast_in_dim.27), calls=%async_computation | async-start | bytes 1048576 | tf_op jit(solution)/shard_map/all_to_all | solution.py:25
  26.0 22.6 %collective-permute-start.1 = (bf16[256,128]{0,1:T(8,128)(2,1)S(1)}, bf16[256,128]{0,1:T(8,128)(2,1)S(1)}, u32[]{:S(2)}, u32[]{:S(2)}) collective-permute-start(bf16[256,128]{0,1:T(8,128)(2,1)S(1)} %fusion), channel_id=1, source_target_pairs={{0,4},{4,0},{1,5},{5,1},{2,6},{6,2},{3,7},{7,3},{8,12},{12,8},{9,1... | collective-permute-start | bytes 196616 | tf_op jit(solution)/shard_map/ppermute | solution.py:39
  40.7 17.0 %collective-permute-start.4 = (f32[296,256]{1,0:T(8,128)S(1)}, f32[296,256]{1,0:T(8,128)S(1)}, u32[]{:S(2)}, u32[]{:S(2)}) collective-permute-start(f32[296,256]{1,0:T(8,128)S(1)} %get-tuple-element.18), channel_id=1, source_target_pairs={{1,0},{2,1},{3,2},{0,3},{5,4},{6,5},{7,6},{4,7},{9,8},{10,9},{11,1... | collective-permute-start | bytes 909320 | tf_op jit(solution)/shard_map/ppermute | solution.py:329
  43.6 20.6 %collective-permute-start.3 = (f32[296,256]{1,0:T(8,128)S(1)}, f32[296,256]{1,0:T(8,128)S(1)}, u32[]{:S(2)}, u32[]{:S(2)}) collective-permute-start(f32[296,256]{1,0:T(8,128)S(1)} %get-tuple-element.17), channel_id=1, source_target_pairs={{2,0},{3,1},{0,2},{1,3},{6,4},{7,5},{4,6},{5,7},{10,8},{11,9},{8,1... | collective-permute-start | bytes 909320 | tf_op jit(solution)/shard_map/ppermute | solution.py:329
  46.6 24.0 %collective-permute-start.2 = (f32[296,256]{1,0:T(8,128)S(1)}, f32[296,256]{1,0:T(8,128)S(1)}, u32[]{:S(2)}, u32[]{:S(2)}) collective-permute-start(f32[296,256]{1,0:T(8,128)S(1)} %get-tuple-element.16), channel_id=1, source_target_pairs={{3,0},{0,1},{1,2},{2,3},{7,4},{4,5},{5,6},{6,7},{11,8},{8,9},{9,10... | collective-permute-start | bytes 909320 | tf_op jit(solution)/shard_map/ppermute | solution.py:329
  49.8 33.1 %all-to-all-start.1 = ((bf16[8,256,256]{2,1,0:T(8,128)(2,1)}), bf16[8,256,256]{2,1,0:T(8,128)(2,1)S(1)}, u32[]{:S(2)}, u32[]{:S(2)}) async-start(bf16[8,256,256]{2,1,0:T(8,128)(2,1)} %broadcast_in_dim.30), calls=%async_computation.1 | async-start | bytes 2097152 | tf_op jit(solution)/shard_map/all_to_all | solution.py:25
  57.8 0.7 copy-start.7
  64.2 0.7 copy-start.6
  70.6 0.7 copy-start.5
  82.9 2.2 %copy-start = (bf16[4,2048,256]{2,1,0:T(8,128)(2,1)S(1)}, bf16[4,2048,256]{2,1,0:T(8,128)(2,1)}, u32[]{:S(2)}) copy-start(bf16[4,2048,256]{2,1,0:T(8,128)(2,1)} %get-tuple-element.25.weight_ref) | copy-start | bytes 12582916
  86.4 15.2 %copy-start.1 = (f32[4,296,256]{2,1,0:T(8,128)S(1)}, f32[4,296,256]{2,1,0:T(8,128)}, u32[]{:S(2)}) copy-start(f32[4,296,256]{2,1,0:T(8,128)} %get-tuple-element.28.refs_4_) | copy-start | bytes 3637252
  86.5 8.2 %collective-permute-start.5 = (f32[128,1024]{1,0:T(8,128)S(1)}, f32[128,1024]{1,0:T(8,128)S(1)}, u32[]{:S(2)}, u32[]{:S(2)}) collective-permute-start(f32[128,1024]{1,0:T(8,128)S(1)} %get-tuple-element.27), channel_id=1, source_target_pairs={{0,64},{64,0},{1,65},{65,1},{2,66},{66,2},{3,67},{67,3},{4,68},{68... | collective-permute-start | bytes 1572872 | tf_op jit(solution)/shard_map/ppermute | solution.py:39
  95.4 13.7 %all-to-all-start.2 = ((bf16[4,32,1024]{2,1,0:T(8,128)(2,1)}), bf16[4,32,1024]{2,1,0:T(8,128)(2,1)S(1)}, u32[]{:S(2)}, u32[]{:S(2)}) async-start(bf16[4,32,1024]{2,1,0:T(8,128)(2,1)} %bitcast.12), calls=%async_computation.2 | async-start | bytes 524288 | tf_op jit(solution)/shard_map/all_to_all | solution.py:25
  118.5 9.1 %collective-permute-start.6 = (bf16[128,1024]{1,0:T(8,128)(2,1)S(1)}, bf16[128,1024]{1,0:T(8,128)(2,1)S(1)}, u32[]{:S(2)}, u32[]{:S(2)}) collective-permute-start(bf16[128,1024]{1,0:T(8,128)(2,1)S(1)} %bitcast.59), channel_id=1, source_target_pairs={{0,64},{64,0},{1,65},{65,1},{2,66},{66,2},{3,67},{67,3},{4,68},{68... | collective-permute-start | bytes 786440 | tf_op jit(solution)/shard_map/ppermute | solution.py:39
  124.1 26.7 %collective-permute-start.10 = (bf16[8,256,256]{2,1,0:T(8,128)(2,1)S(1)}, bf16[8,256,256]{2,1,0:T(8,128)(2,1)}, u32[]{:S(2)}, u32[]{:S(2)}) collective-permute-start(bf16[8,256,256]{2,1,0:T(8,128)(2,1)S(1)} %all-to-all-done.1.att_ref.refs_0_), channel_id=1, source_target_pairs={{0,1},{1,0},{2,3},{3,2},{4,5},{5,4},{6,7},{7,6},{8,9},{9,8},{10,11... | collective-permute-start | bytes 3145736 | tf_op jit(solution)/shard_map/ppermute | solution.py:335
  127.7 28.6 %collective-permute-start.7 = (bf16[256,512]{1,0:T(8,128)(2,1)S(1)}, bf16[256,512]{1,0:T(8,128)(2,1)S(1)}, u32[]{:S(2)}, u32[]{:S(2)}) collective-permute-start(bf16[256,512]{1,0:T(8,128)(2,1)S(1)} %pad_maximum_fusion.7), channel_id=1, source_target_pairs={{0,1},{1,0},{2,3},{3,2},{4,5},{5,4},{6,7},{7,6},{8,9},{9,8},{10,11... | collective-permute-start | bytes 786440 | tf_op jit(solution)/shard_map/ppermute | solution.py:347
  173.4 17.3 %all-to-all-start.4 = ((bf16[32,36,128]{2,1,0:T(8,128)(2,1)}), bf16[32,36,128]{2,1,0:T(8,128)(2,1)S(1)}, u32[]{:S(2)}, u32[]{:S(2)}) async-start(bf16[32,36,128]{2,1,0:T(8,128)(2,1)} %bitcast.24), calls=%async_computation.4 | async-start | bytes 655360 | tf_op jit(solution)/shard_map/all_to_all | solution.py:25
  178.1 19.4 %collective-permute-start.9 = (bf16[256,256]{1,0:T(8,128)(2,1)S(1)}, bf16[256,256]{1,0:T(8,128)(2,1)S(1)}, u32[]{:S(2)}, u32[]{:S(2)}) collective-permute-start(bf16[256,256]{1,0:T(8,128)(2,1)S(1)} %get-tuple-element.41), channel_id=1, source_target_pairs={{1,2},{2,1},{3,0},{0,3},{5,6},{6,5},{7,4},{4,7},{9,10},{10,9},{11,... | collective-permute-start | bytes 393224 | tf_op jit(solution)/shard_map/ppermute | solution.py:349
  182.4 15.0 %collective-permute-start.8 = (bf16[256,256]{1,0:T(8,128)(2,1)S(1)}, bf16[256,256]{1,0:T(8,128)(2,1)S(1)}, u32[]{:S(2)}, u32[]{:S(2)}) collective-permute-start(bf16[256,256]{1,0:T(8,128)(2,1)S(1)} %get-tuple-element.39), channel_id=1, source_target_pairs={{0,2},{1,3},{2,0},{3,1},{4,6},{5,7},{6,4},{7,5},{8,10},{9,11},{10,... | collective-permute-start | bytes 393224 | tf_op jit(solution)/shard_map/ppermute | solution.py:348
  191.5 15.6 %all-to-all-start.5 = ((bf16[16,36,128]{2,1,0:T(8,128)(2,1)}), bf16[16,36,128]{2,1,0:T(8,128)(2,1)S(1)}, u32[]{:S(2)}, u32[]{:S(2)}) async-start(bf16[16,36,128]{2,1,0:T(8,128)(2,1)} %broadcast_in_dim.35), calls=%async_computation.5 | async-start | bytes 327680 | tf_op jit(solution)/shard_map/all_to_all | solution.py:25
  197.5 11.0 %copy-start.2 = (bf16[2,4,128,256]{3,2,1,0:T(8,128)(2,1)}, bf16[2,4,128,256]{3,2,1,0:T(8,128)(2,1)S(1)}, u32[]{:S(2)}) copy-start(bf16[2,4,128,256]{3,2,1,0:T(8,128)(2,1)S(1)} %constant_dynamic-update-slice_fusion) | copy-start | bytes 1572868
